TPU v7x, 256 devices: a whole 4x4x8 slice. The times are simulated.
256 devices in a mesh: dp: 8 (over x, core), seq: 32 (over z, y).
Axes of the slice: x: 4, y: 4, z: 8, core: 2. Of those that a mesh axis runs over, the one named last changes fastest.
Arguments:
- queries: bfloat16 [8, 8192, 2048], P('dp', 'seq'), may hold values from -40 to 40
- keys: bfloat16 [8, 8192, 2048], P('dp', 'seq'), may hold values from -40 to 40
- values: bfloat16 [8, 8192, 2048], P('dp', 'seq'), may hold values from -6 to 6
- key_gain: float32 [2048], replicated, may hold values from 0.25 to 1.75
- random_blocks: int32 [16, 128, 3], P(None, 'seq'), may hold values from 2 to 127, as said below
- out_grad: bfloat16 [8, 8192, 2048], P('dp', 'seq'), may hold values from -6 to 6
Outputs:
- attended: bfloat16 [8, 8192, 2048], P('dp', 'seq')
- query_grad: bfloat16 [8, 8192, 2048], P('dp', 'seq')
- key_grad: bfloat16 [8, 8192, 2048], P('dp', 'seq')
- value_grad: bfloat16 [8, 8192, 2048], P('dp', 'seq')
- gain_grad: float32 [2048], replicated
Inputs may be any that keep to these rules, and one draw needn't show every extreme that they name: `random_blocks`: for the 4 query blocks of one device, all heads and entries together, at most 9 entries name blocks held by any one device (blocks d * 4 to d * 4 + 3), and exactly 9 name the blocks of some device.
All inputs are finite; a program needn't handle non-finite values.
Results may differ from a plain program's by a relative error of at most 0.03.
The roundings to bfloat16 on the way count: a program that leaves them out, or rounds other values in their place, can miss the bound.
Values may be sent and summed in bfloat16 or wider, within the bound.
No kernel may reach another device: no remote copies, remote signals or barrier semaphores. Data moves between devices by JAX's collectives and lax.ppermute only.
A program may use at most 128 MiB of HBM per device.

v0:
```python
import math

import jax
import jax.numpy as jnp
from jax import lax
from jax.sharding import PartitionSpec as P

HEADS = 16
HD = 128
BLOCK = 64
NG = 2
NR = 3
NK = 8


NEGATIVE = -1e30


def broadcast(block, axis, owner):
    block = jnp.where(lax.axis_index(axis) == owner, block, jnp.zeros_like(block))
    return lax.psum(block, axis)


def padded_2(cells, sides, width):
    for axis, dim in sides:
        count = lax.axis_size(axis)
        ends = count - 1
        head = lax.slice_in_dim(cells, 0, width, axis=dim)
        tail = lax.slice_in_dim(cells, cells.shape[dim] - width, cells.shape[dim], axis=dim)
        cells = jnp.concatenate(
            [
                lax.ppermute(tail, axis, [(i, (i + 1) % count) for i in range(ends)]),
                cells,
                lax.ppermute(head, axis, [((i + 1) % count, i) for i in range(ends)]),
            ],
            axis=dim,
        )
    return cells


def passed_along(array, axis, by):
    length = lax.axis_size(axis)
    pairs = [(i, i + by) for i in range(length) if 0 <= i + by < length]
    return lax.ppermute(array, axis, pairs)


def to_heads(rows_in):
    return rows_in.reshape(rows_in.shape[0] // BLOCK, BLOCK, HEADS, HD).transpose(2, 0, 1, 3)


def from_heads(blocks_in):
    return blocks_in.transpose(1, 2, 0, 3).reshape(1, blocks_in.shape[1] * BLOCK, HEADS * HD)


def build_list(edge_part, window_part, random_in):
    head_count = random_in.shape[0]
    block_count = random_in.shape[1]
    global_list = jnp.broadcast_to(
        edge_part[:, None], (head_count, block_count) + edge_part.shape[1:]
    )
    window_list = jnp.stack(
        [window_part[:, offset : offset + block_count] for offset in range(3)], axis=2
    )
    joined = jnp.concatenate([global_list, window_list, random_in], axis=2)
    return joined.reshape(head_count, block_count, NK * BLOCK, HD)


def spread_terms(coef, rows_in):
    head_count = rows_in.shape[0]
    block_count = rows_in.shape[1]
    coef_blocks = coef.reshape(head_count, block_count, BLOCK, NK, BLOCK)
    global_term = jnp.einsum(
        "hpbgc,hpbd->hgcd", coef_blocks[:, :, :, :NG], rows_in, preferred_element_type=jnp.float32
    )
    padded = jnp.zeros((head_count, block_count + 2, BLOCK, HD), jnp.float32)
    for offset in range(3):
        term = jnp.einsum(
            "hpbc,hpbd->hpcd",
            coef_blocks[:, :, :, NG + offset],
            rows_in,
            preferred_element_type=jnp.float32,
        )
        padded = padded + jnp.pad(term, ((0, 0), (offset, 2 - offset), (0, 0), (0, 0)))
    random_term = jnp.einsum(
        "hpbrc,hpbd->hprcd",
        coef_blocks[:, :, :, NG + 3 :],
        rows_in,
        preferred_element_type=jnp.float32,
    )
    return (global_term, padded, random_term)


def sparse_group(
    query_blk,
    edge_key,
    edge_value,
    window_key,
    window_value,
    random_key,
    random_value,
    grad_blk,
    valid_keys,
    keep_rows,
):
    score_scale = HD ** (-0.5)
    key_list = build_list(edge_key, window_key, random_key)
    value_list = build_list(edge_value, window_value, random_value)
    key_mask = jnp.repeat(valid_keys, BLOCK, axis=1)[None, :, None, :]
    scores = (
        jnp.einsum("hpbd,hpnd->hpbn", query_blk, key_list, preferred_element_type=jnp.float32)
        * score_scale
    )
    scores = jnp.where(key_mask, scores, NEGATIVE)
    row_top = jnp.max(scores, axis=3, keepdims=True)
    expo_vals = jnp.where(key_mask, jnp.exp(scores - row_top), 0.0)
    row_total = jnp.sum(expo_vals, axis=3, keepdims=True)
    numerator = jnp.einsum(
        "hpbn,hpnd->hpbd",
        expo_vals.astype(jnp.bfloat16),
        value_list,
        preferred_element_type=jnp.float32,
    )
    attended = (numerator / row_total).astype(jnp.bfloat16)
    row_delta = jnp.sum(grad_blk.astype(jnp.float32) * attended.astype(jnp.float32), axis=3)
    weights = expo_vals / row_total * keep_rows[None, :, None, None]
    dprobs = jnp.einsum("hpbd,hpnd->hpbn", grad_blk, value_list, preferred_element_type=jnp.float32)
    dscores = (weights * (dprobs - row_delta[:, :, :, None]) * score_scale).astype(jnp.bfloat16)
    dquery = jnp.einsum("hpbn,hpnd->hpbd", dscores, key_list, preferred_element_type=jnp.float32)
    key_global, key_padded, key_random = spread_terms(dscores, query_blk)
    value_global, value_padded, value_random = spread_terms(weights.astype(jnp.bfloat16), grad_blk)
    global_part = jnp.stack([key_global, value_global], axis=1)
    padded = jnp.stack([key_padded, value_padded], axis=1)
    random_part = jnp.stack([key_random, value_random], axis=1)
    return (attended, dquery, global_part, padded, random_part)


def shards(queries, keys, values, key_gain, random_blocks, out_grad):
    score_scale = HD ** (-0.5)
    tok_count = queries.shape[1]
    per_dev = tok_count // BLOCK
    owners = lax.axis_size("seq")
    seq_place = lax.axis_index("seq")
    total_blocks = owners * per_dev
    first_block = seq_place * per_dev
    key_eff = (keys[0].astype(jnp.float32) * key_gain).astype(jnp.bfloat16)
    edge_count = NG * BLOCK
    edge_rows = broadcast(
        jnp.stack(
            [
                queries[0, :edge_count],
                key_eff[:edge_count],
                values[0, :edge_count],
                out_grad[0, :edge_count],
            ]
        ),
        "seq",
        0,
    )
    window_rows = padded_2(jnp.stack([key_eff, values[0]]), (("seq", 1),), BLOCK)
    query_h = to_heads(queries[0])
    key_h = to_heads(key_eff)
    value_h = to_heads(values[0])
    grad_h = to_heads(out_grad[0])
    edge_heads = [to_heads(edge_rows[slot_pick]) for slot_pick in range(4)]
    window_key = to_heads(window_rows[0])
    window_value = to_heads(window_rows[1])
    request_count = HEADS * per_dev * NR
    capacity = (request_count + owners - 1) // owners + 3
    target = random_blocks.reshape(request_count)
    owner_dev = target // per_dev
    table_index = (
        jnp.arange(request_count, dtype=jnp.int32) // (per_dev * NR) * per_dev + target % per_dev
    )
    onehot = (owner_dev[:, None] == jnp.arange(owners, dtype=jnp.int32)[None, :]).astype(jnp.int32)
    before = jnp.cumsum(onehot, axis=0) - onehot
    slot_rank = jnp.sum(before * onehot, axis=1)
    position = owner_dev * capacity + slot_rank
    outgoing = (
        jnp.full((owners * capacity,), -1, jnp.int32)
        .at[position]
        .set(table_index)
        .reshape(owners, capacity)
    )
    kv_table = jnp.concatenate([key_h, value_h], axis=3).reshape(HEADS * per_dev, BLOCK, 2 * HD)
    index_part = lax.all_to_all(outgoing, "seq", split_axis=0, concat_axis=0, tiled=True)
    picked = kv_table[jnp.clip(index_part, 0, HEADS * per_dev - 1)]
    fetch_result = (
        lax.all_to_all(picked, "seq", split_axis=0, concat_axis=0, tiled=True),
        index_part,
    )
    arrived, served = fetch_result
    fetched = arrived.reshape(owners * capacity, BLOCK, 2 * HD)[position].reshape(
        HEADS, per_dev, NR, BLOCK, 2 * HD
    )
    fetched_key = fetched[..., :HD]
    fetched_value = fetched[..., HD:]
    block_index = first_block + jnp.arange(per_dev, dtype=jnp.int32)
    window_index = block_index[:, None] + jnp.arange(-1, 2, dtype=jnp.int32)[None, :]
    valid_keys = jnp.concatenate(
        [
            jnp.ones((per_dev, NG), bool),
            (window_index >= NG) & (window_index < total_blocks),
            jnp.ones((per_dev, NR), bool),
        ],
        axis=1,
    )
    keep_rows = (block_index >= NG).astype(jnp.float32)
    group_size = math.gcd(HEADS, 4)

    def by_group(array_in):
        return array_in.reshape((HEADS // group_size, group_size) + array_in.shape[1:])

    def merge_groups(array_in):
        return array_in.reshape((HEADS,) + array_in.shape[2:])

    def run_group(bundle):
        return sparse_group(
            bundle[0],
            bundle[1],
            bundle[2],
            bundle[3],
            bundle[4],
            bundle[5],
            bundle[6],
            bundle[7],
            valid_keys,
            keep_rows,
        )

    grouped = lax.map(
        run_group,
        (
            by_group(query_h),
            by_group(edge_heads[1]),
            by_group(edge_heads[2]),
            by_group(window_key),
            by_group(window_value),
            by_group(fetched_key),
            by_group(fetched_value),
            by_group(grad_h),
        ),
    )
    attended_h, dquery_h, global_part, padded, random_part = [
        merge_groups(piece_out) for piece_out in grouped
    ]
    edge_query = edge_heads[0].reshape(HEADS, edge_count, HD)
    edge_grad = edge_heads[3].reshape(HEADS, edge_count, HD)
    flat_key = key_h.reshape(HEADS, tok_count, HD)
    flat_value = value_h.reshape(HEADS, tok_count, HD)
    edge_scores = (
        jnp.einsum("hqd,htd->hqt", edge_query, flat_key, preferred_element_type=jnp.float32)
        * score_scale
    )
    edge_top = lax.pmax(jnp.max(edge_scores, axis=2), "seq")
    edge_expo = jnp.exp(edge_scores - edge_top[:, :, None])
    edge_total, edge_numer = lax.psum(
        (
            jnp.sum(edge_expo, axis=2),
            jnp.einsum(
                "hqt,htd->hqd",
                edge_expo.astype(jnp.bfloat16),
                flat_value,
                preferred_element_type=jnp.float32,
            ),
        ),
        "seq",
    )
    edge_out = (edge_numer / edge_total[:, :, None]).astype(jnp.bfloat16)
    edge_delta = jnp.sum(edge_grad.astype(jnp.float32) * edge_out.astype(jnp.float32), axis=2)
    edge_weights = edge_expo / edge_total[:, :, None]
    edge_dprobs = jnp.einsum(
        "hqd,htd->hqt", edge_grad, flat_value, preferred_element_type=jnp.float32
    )
    edge_dscores = (edge_weights * (edge_dprobs - edge_delta[:, :, None]) * score_scale).astype(
        jnp.bfloat16
    )
    edge_dquery = jnp.einsum(
        "hqt,htd->hqd", edge_dscores, flat_key, preferred_element_type=jnp.float32
    )
    local_dkey = jnp.einsum(
        "hqt,hqd->htd", edge_dscores, edge_query, preferred_element_type=jnp.float32
    )
    local_dvalue = jnp.einsum(
        "hqt,hqd->htd",
        edge_weights.astype(jnp.bfloat16),
        edge_grad,
        preferred_element_type=jnp.float32,
    )
    random_rounded = (
        random_part.transpose(0, 2, 3, 4, 1, 5)
        .reshape(request_count, BLOCK, 2 * HD)
        .astype(jnp.bfloat16)
    )
    sendback = (
        jnp.zeros((owners * capacity, BLOCK, 2 * HD), jnp.bfloat16)
        .at[position]
        .set(random_rounded)
        .reshape(owners, capacity, BLOCK, 2 * HD)
    )
    returned = lax.all_to_all(sendback, "seq", split_axis=0, concat_axis=0, tiled=True)
    owner_table = (
        served.reshape(1, owners * capacity)
        == jnp.arange(HEADS * per_dev, dtype=jnp.int32)[:, None]
    ).astype(jnp.bfloat16)
    summed = jnp.dot(
        owner_table,
        returned.reshape(owners * capacity, BLOCK * 2 * HD),
        preferred_element_type=jnp.float32,
    )
    summed = summed.reshape(HEADS, per_dev, BLOCK, 2, HD).transpose(0, 3, 1, 2, 4)
    from_right = passed_along(padded[:, :, 0].astype(jnp.bfloat16), "seq", -1).astype(jnp.float32)
    from_left = passed_along(padded[:, :, per_dev + 1].astype(jnp.bfloat16), "seq", 1).astype(
        jnp.float32
    )
    edge_dquery_sum, global_sum = lax.psum((edge_dquery, global_part), "seq")
    accum = padded[:, :, 1 : per_dev + 1]
    accum = accum + jnp.stack([local_dkey, local_dvalue], axis=1).reshape(
        HEADS, 2, per_dev, BLOCK, HD
    )
    accum = accum + summed
    accum = accum.at[:, :, per_dev - 1].add(from_right)
    accum = accum.at[:, :, 0].add(from_left)
    is_first = (seq_place == 0).astype(jnp.float32)
    accum = accum.at[:, :, :NG].add(global_sum * is_first)
    is_edge = (block_index < NG)[None, :, None, None]
    tail_zeros = jnp.zeros((HEADS, per_dev - NG, BLOCK, HD), jnp.float32)
    edge_dq_blocks = jnp.concatenate(
        [edge_dquery_sum.reshape(HEADS, NG, BLOCK, HD), tail_zeros], axis=1
    )
    edge_out_blocks = jnp.concatenate(
        [edge_out.reshape(HEADS, NG, BLOCK, HD), tail_zeros.astype(jnp.bfloat16)], axis=1
    )
    dquery_all = jnp.where(is_edge, edge_dq_blocks, dquery_h).astype(jnp.bfloat16)
    attended_all = jnp.where(is_edge, edge_out_blocks, attended_h)
    key_eff_grad = accum[:, 0]
    gain_heads = key_gain.reshape(HEADS, HD)
    key_grad_h = (key_eff_grad * gain_heads[:, None, None, :]).astype(jnp.bfloat16)
    value_grad_h = accum[:, 1].astype(jnp.bfloat16)
    gain_term = jnp.sum(key_eff_grad * to_heads(keys[0]).astype(jnp.float32), axis=(1, 2)).reshape(
        HEADS * HD
    )
    gain_grad = lax.psum(gain_term, ("dp", "seq"))
    return (
        from_heads(attended_all),
        from_heads(dquery_all),
        from_heads(key_grad_h),
        from_heads(value_grad_h),
        gain_grad,
    )


def solution(mesh):
    placed = (
        P("dp", "seq", None),
        P("dp", "seq", None),
        P("dp", "seq", None),
        P(),
        P(None, "seq", None),
        P("dp", "seq", None),
    )
    return jax.shard_map(
        shards,
        mesh=mesh,
        in_specs=placed,
        out_specs=(
            P("dp", "seq", None),
            P("dp", "seq", None),
            P("dp", "seq", None),
            P("dp", "seq", None),
            P(),
        ),
        check_vma=False,
    )
```

profile of v0, /device:TPU:1, one launch (start us, length us, event | category | flops | bytes accessed | tf_op | source)
XLA Modules:
  0.0 1441.8 jit_solution(389370633972243564)
XLA Ops:
  11.2 12.0 all-to-all-start
  23.2 2.8 convert_bitcast_fusion
  33.7 10.3 gather_fusion
  43.9 7.5 all-to-all-start.1
  58.0 3.9 collective-permute-start
  68.2 25.1 %collective-permute-done = bf16[2,64,2048]{2,1,0:T(8,128)(2,1)} collective-permute-done((bf16[2,64,2048]{2,1,0:T(8,128)(2,1)}, bf16[2,64,2048]{2,1,0:T(8,128)(2,1)}, u32[]{:S(2)}, u32[]{:S(2)}) %collective-permute-start) | collective-permute-done | bytes 524320 | tf_op jit(solution)/shard_map/ppermute | solution.py:32
  93.3 21.3 %collective-permute-done.1 = bf16[2,64,2048]{2,1,0:T(8,128)(2,1)} collective-permute-done((bf16[2,64,2048]{2,1,0:T(8,128)(2,1)}, bf16[2,64,2048]{2,1,0:T(8,128)(2,1)}, u32[]{:S(2)}, u32[]{:S(2)}) %collective-permute-start.1) | collective-permute-done | bytes 524320 | tf_op jit(solution)/shard_map/ppermute | solution.py:34
  119.2 206.0 %all-reduce.14.cloned.1.call-done = bf16[4,128,2048]{2,1,0:T(8,128)(2,1)} async-done(((bf16[4,128,2048]{2,1,0:T(8,128)(2,1)}), bf16[4,128,2048]{2,1,0:T(8,128)(2,1)}) %all-reduce.14.cloned.1.call-update) | async-done | bytes 2097168 | tf_op jit(solution)/shard_map/psum | solution.py:21
  325.1 2.7 slice_bitcast_fusion.14
  329.1 11.8 gather_fusion.1
  340.9 8.0 fusion.134
  348.9 287.8 %while.24 = (s32[]{:T(128)}, bf16[4,4,4,64,128]{4,3,2,1,0:T(8,128)(2,1)}, bf16[4,4,4,64,128]{4,3,2,1,0:T(8,128)(2,1)}, f32[4,4,2,2,64,128]{5,1,0,2,4,3:T(4,128)}...) while((s32[]{:T(128)}, ...), condition=%wide.region_14.15_spmd.clone, body=%wide.region_10.14_spmd.clone.sunk | while | flops 952370176 | bytes 142396560 | solution.py:230
  356.1 3.5 fusion.232
  365.5 3.1 fusion.233
  368.6 5.1 bitcast_dynamic-update-slice_fusion.6
  374.9 3.2 multiply_convert_fusion.4
  380.2 2.3 slice.441
  385.4 2.9 fusion.240
  399.4 2.8 fusion.236
  427.9 3.5 fusion.232
  437.3 3.1 fusion.233
  440.4 5.1 bitcast_dynamic-update-slice_fusion.6
  446.7 3.2 multiply_convert_fusion.4
  452.0 2.3 slice.441
  457.2 2.9 fusion.240
  471.1 2.8 fusion.236
  484.4 2.3 copy_dynamic-update-slice_fusion.7
  499.7 3.5 fusion.232
  509.1 3.1 fusion.233
  512.2 5.1 bitcast_dynamic-update-slice_fusion.6
  518.5 3.2 multiply_convert_fusion.4
  523.8 2.3 slice.441
  529.0 2.9 fusion.240
  543.0 2.8 fusion.236
  556.3 2.3 copy_dynamic-update-slice_fusion.7
  571.5 3.5 fusion.232
  581.0 3.1 fusion.233
  584.1 5.1 bitcast_dynamic-update-slice_fusion.6
  590.4 3.2 multiply_convert_fusion.4
  595.6 2.3 slice.441
  600.8 2.9 fusion.240
  614.7 2.8 fusion.236
  628.0 2.3 copy_dynamic-update-slice_fusion.7
  636.7 12.7 copy.168
  649.5 10.8 reshape.529
  660.3 4.9 broadcast_in_dim.167
  665.2 29.2 %scatter_fusion = bf16[288,64,256]{2,1,0:T(8,128)(2,1)} fusion(bf16[288,64,256]{2,1,0:T(8,128)(2,1)} %broadcast_in_dim.167, s32[192]{0:T(256)S(1)} %bitcast.511, bf16[192,64,256]{2,1,0:T(8,128)(2,1)} %reshape.529), kind=kCustom, calls=%fused_computation.3 | custom fusion | bytes 18875136 | tf_op jit(solution)/shard_map/scatter | solution.py:297
  694.4 5.8 all-to-all-start.2
  704.2 248.3 %pmax.7 = f32[16,128]{1,0:T(8,128)S(1)} all-reduce(f32[16,128]{1,0:T(8,128)S(1)} %get-tuple-element.352), channel_id=1, replica_groups=mesh['dp'=8,'seq'=32] {'seq'}, use_global_device_ids=true, to_apply=%region_2.3 | all-reduce | flops 2048 | bytes 16384 | tf_op jit(solution)/shard_map/pmax | solution.py:254
  952.5 3.5 fusion.97
  959.9 58.9 %psum.44 = f32[16,128]{1,0:T(8,128)S(1)} all-reduce(f32[16,128]{1,0:T(8,128)S(1)} %fusion.95), channel_id=1, replica_groups=mesh['dp'=8,'seq'=32] {'seq'}, use_global_device_ids=true, to_apply=%region_5.6 | all-reduce | flops 2048 | bytes 16384 | tf_op jit(solution)/shard_map/psum | solution.py:256
  1018.8 2.9 fusion.104
  1021.7 2.5 copy.166
  1027.5 4.8 collective-permute-start.3
  1032.3 100.2 %all-reduce.16.cloned.1.call-done = (f32[16,128,128]{2,1,0:T(8,128)}, f32[16,2,2,64,128]{4,0,1,3,2:T(8,128)}) async-done(((f32[16,128,128]{2,1,0:T(8,128)}, f32[16,2,2,64,128]{4,0,1,3,2:T(8,128)}), (f32[16,128,128]{2,1,0:T(8,128)}, f32[16,2,2,64,128]{4,0,1,3,2:T(8,128)})) %all-reduce.16.cloned.1.call-update) | async-done | bytes 3145744 | tf_op jit(solution)/shard_map/psum | solution.py:256
  1132.5 2.7 multiply_reduce_fusion.2
  1135.2 2.5 multiply_convert_fusion.2
  1138.2 2.6 copy.165
  1142.2 123.4 %all-reduce.17 = bf16[16,2,64,128]{3,2,1,0:T(8,128)(2,1)S(1)} all-reduce(f32[16,2,64,128]{3,2,1,0:T(8,128)} %bitcast.485), channel_id=1, replica_groups=mesh['dp'=8,'seq'=32] {'seq'}, use_global_device_ids=true, to_apply=%region_16.17 | all-reduce | flops 262144 | bytes 1572864 | tf_op jit(solution)/shard_map/psum | solution.py:315
  1265.6 2.9 fusion.93
  1273.8 18.5 %copy.212 = bf16[36,8,64,256]{3,1,2,0:T(8,128)(2,1)} copy(bf16[36,8,64,256]{3,2,1,0:T(8,128)(2,1)} %bitcast.182) | data formatting | bytes 18874368
  1292.3 16.1 %dot_general.116 = bf16[64,2,128,288]{2,1,0,3:T(2,128)(2,1)} reshape(bf16[16384,288]{0,1:T(8,128)(2,1)} %bitcast.460) | data formatting | bytes 18874368 | tf_op jit(solution)/shard_map/dot_general | solution.py:305
  1308.4 12.3 fusion.85
  1328.6 106.2 %psum.47 = f32[2048]{0:T(1024)} all-reduce(f32[2048]{0:T(1024)S(1)} %bitcast.508), channel_id=1, replica_groups=mesh['dp'=8,'seq'=32] {'dp','seq'}, use_global_device_ids=true, to_apply=%region_20.21 | all-reduce | flops 2048 | bytes 16384 | tf_op jit(solution)/shard_map/psum | solution.py:342
  (437 shorter events, 243.4 us)
Async XLA Ops:
  9.3 58.8 %copy-start.31 = (s32[192,1]{0,1:T(1,128)}, s32[192,1]{0,1:T(1,128)S(1)}, u32[]{:S(2)}) copy-start(s32[192,1]{0,1:T(1,128)S(1)} %compare_select_fusion.1) | copy-start | bytes 2308
  11.2 20.6 %all-to-all-start = ((s32[32,1,9]{2,1,0:T(1,128)}), s32[32,1,9]{2,1,0:T(1,128)S(1)}, u32[]{:S(2)}, u32[]{:S(2)}) async-start(s32[32,1,9]{2,1,0:T(1,128)} %bitcast.20), calls=%async_computation | async-start | bytes 32768 | tf_op jit(solution)/shard_map/all_to_all | solution.py:185
  26.5 2.3 copy-start.6
  27.3 1.4 copy-start.28
  43.9 285.2 %all-to-all-start.1 = ((bf16[32,9,64,256]{3,2,1,0:T(8,128)(2,1)}), bf16[32,9,64,256]{3,2,1,0:T(8,128)(2,1)}, u32[]{:S(2)}, u32[]{:S(2)}) async-start(bf16[32,9,64,256]{3,2,1,0:T(8,128)(2,1)} %bitcast.459), calls=%async_computation.1 | async-start | bytes 18874368 | tf_op jit(solution)/shard_map/all_to_all | solution.py:188
  51.4 1.8 copy-start.16
  51.4 273.7 %all-reduce.14.cloned.1.call-start = ((), (), s32[]{:S(2)}) async-start(), calls=%async_computation.3 | async-start | bytes 4194304 | tf_op jit(solution)/shard_map/psum | solution.py:21
  52.3 1.5 copy-start.24
  58.0 35.3 %collective-permute-start = (bf16[2,64,2048]{2,1,0:T(8,128)(2,1)}, bf16[2,64,2048]{2,1,0:T(8,128)(2,1)}, u32[]{:S(2)}, u32[]{:S(2)}) collective-permute-start(bf16[2,64,2048]{2,1,0:T(8,128)(2,1)} %get-tuple-element.342), channel_id=1, source_target_pairs={{0,1},{1,2},{2,3},{3,4},{4,5},{5,6},{6,7},{7,8},{8,9},{9,10},{10,1... | collective-permute-start | bytes 1572872 | tf_op jit(solution)/shard_map/ppermute | solution.py:32
  61.8 52.8 %collective-permute-start.1 = (bf16[2,64,2048]{2,1,0:T(8,128)(2,1)}, bf16[2,64,2048]{2,1,0:T(8,128)(2,1)}, u32[]{:S(2)}, u32[]{:S(2)}) collective-permute-start(bf16[2,64,2048]{2,1,0:T(8,128)(2,1)} %get-tuple-element.343), channel_id=1, source_target_pairs={{1,0},{2,1},{3,2},{4,3},{5,4},{6,5},{7,6},{8,7},{9,8},{10,9},{11,1... | collective-permute-start | bytes 1572872 | tf_op jit(solution)/shard_map/ppermute | solution.py:34
  63.7 2.8 copy-start.22
  355.9 3.7 copy-start.1
  362.6 2.9 copy-start.2
  380.2 3.8 copy-start.5
  382.5 2.9 copy-start
  409.9 2.6 copy-start.4
  414.9 1.7 slice-start
  416.6 2.7 copy-start.3
  416.6 2.7 copy-start.26
  419.3 1.5 copy-start.13
  419.3 1.6 copy-start.21
  427.7 3.7 copy-start.1
  434.4 2.9 copy-start.2
  452.0 3.8 copy-start.5
  454.3 2.9 copy-start
  481.7 2.6 copy-start.4
  486.7 1.7 slice-start
  488.4 2.7 copy-start.3
  488.4 2.6 copy-start.26
  491.0 1.5 copy-start.13
  491.1 1.6 copy-start.21
  499.5 3.7 copy-start.1
  506.2 2.9 copy-start.2
  523.8 3.8 copy-start.5
  526.1 3.0 copy-start
  553.6 2.6 copy-start.4
  558.6 1.7 slice-start
  560.3 2.7 copy-start.3
  560.3 2.7 copy-start.26
  562.9 1.5 copy-start.13
  562.9 1.6 copy-start.21
  571.4 3.7 copy-start.1
  578.1 2.9 copy-start.2
  595.6 3.8 copy-start.5
  597.9 2.8 copy-start
  625.3 2.6 copy-start.4
  630.3 1.7 slice-start
  632.0 2.7 copy-start.3
  632.1 2.7 copy-start.26
  634.7 1.5 copy-start.13
  634.7 1.6 copy-start.21
  660.3 4.9 copy-start.32
  694.4 5.9 copy-start.7
  694.4 5.9 copy-start.29
  694.4 579.4 %all-to-all-start.2 = ((bf16[32,9,64,256]{3,2,1,0:T(8,128)(2,1)}), bf16[32,9,64,256]{3,2,1,0:T(8,128)(2,1)}, u32[]{:S(2)}, u32[]{:S(2)}) async-start(bf16[32,9,64,256]{3,2,1,0:T(8,128)(2,1)} %bitcast.457), calls=%async_computation.2 | async-start | bytes 18874368 | tf_op jit(solution)/shard_map/all_to_all | solution.py:300
  700.2 432.3 %all-reduce.16.cloned.1.call-start = ((), (), s32[]{:S(2)}) async-start(), calls=%async_computation.4 | async-start | bytes 6291456 | tf_op jit(solution)/shard_map/psum | solution.py:256
  956.9 2.2 copy-start.8
  1018.8 5.5 slice-start.1
  1018.8 5.5 slice-start.2
  1026.2 294.6 %collective-permute-start.2 = (bf16[16,2,64,128]{3,0,1,2:T(8,128)(2,1)}, bf16[16,2,64,128]{3,0,1,2:T(8,128)(2,1)}, u32[]{:S(2)}, u32[]{:S(2)}) collective-permute-start(bf16[16,2,64,128]{3,0,1,2:T(8,128)(2,1)} %get-tuple-element.335), channel_id=1, source_target_pairs={{1,0},{2,1},{3,2},{4,3},{5,4},{6,5},{7,6},{8,7},{9,8},{10,9},{11,1... | collective-permute-start | bytes 1572872 | tf_op jit(solution)/shard_map/ppermute | solution.py:44
  1027.5 294.8 %collective-permute-start.3 = (bf16[16,2,64,128]{3,0,1,2:T(8,128)(2,1)}, bf16[16,2,64,128]{3,0,1,2:T(8,128)(2,1)}, u32[]{:S(2)}, u32[]{:S(2)}) collective-permute-start(bf16[16,2,64,128]{3,0,1,2:T(8,128)(2,1)} %get-tuple-element.334), channel_id=1, source_target_pairs={{0,1},{1,2},{2,3},{3,4},{4,5},{5,6},{6,7},{7,8},{8,9},{9,10},{10,1... | collective-permute-start | bytes 1572872 | tf_op jit(solution)/shard_map/ppermute | solution.py:44
  1132.5 2.7 copy-start.9
  1135.2 2.5 copy-start.15
  1320.7 2.8 copy-start.23
  (25 other events, 29.7 us)
Sparse Core Ops, SparseCore 0:
  55.8 269.2 all-reduce.13
  956.2 176.2 all-reduce.15
where the time goes:
time: 1450 us; the launch traced here: 1440 us
  blocking collectives  537 us (37%)
  waiting for transfers between devices  354 us (24%)
  local copies, waits for them, and re-layouts  289 us (20%)
  matrix products  154 us (11%)
  other arithmetic  53.4 us (4%)
  starting transfers between devices  37.1 us (3%)
  between operations  14.9 us (1%)
    pmax x1, blocking collectives, shards(): edge_top = lax.pmax(jnp.max(edge_scores, axis=2), 'seq')  248 us
    psum x1, waiting for transfers between devices, broadcast(): return lax.psum(block, axis)  206 us
    psum x1, blocking collectives, shards(): edge_dquery_sum, global_sum = lax.psum((edge_dquery, global_part), 'seq')  123 us
    psum x1, blocking collectives, shards(): gain_grad = lax.psum(gain_term, ('dp', 'seq'))  106 us
    psum x1, waiting for transfers between devices, shards(): lax.psum((jnp.sum(edge_expo, axis=2), jnp.einsum('hqt,htd->hqd', edge_exp...  100 us
    psum x1, blocking collectives, shards(): lax.psum((jnp.sum(edge_expo, axis=2), jnp.einsum('hqt,htd->hqd', edge_exp...  58.9 us
    while x160, local copies, waits for them, and re-layouts  46.8 us
    dot_general x24, matrix products, spread_terms(): jnp.einsum('hpbc,hpbd->hpcd', coef_blocks[:, :, :, NG + offset], rows_in,...  41.4 us
  transfers between devices with their start and end apart: 9, of which 5 were waited for; matrix products, arithmetic and copies ran while one was open for 7% of the time, Pallas kernels for 0%

commit v1 on v0

v1 whole, which is shorter than its diff:
```python
import functools
import math

import jax
import jax.numpy as jnp
from jax import lax
from jax.experimental import pallas as pl
from jax.experimental.pallas import tpu as pltpu
from jax.sharding import PartitionSpec as P

HD = 128
BLOCK = 64
NR = 3
NEGATIVE = -1e30
SCALE = HD**-0.5
EXP_SCALE = SCALE * math.log2(math.e)


def nt(a, b):
    return lax.dot_general(a, b, (((1,), (1,)), ((), ())), preferred_element_type=jnp.float32)


def nn(a, b):
    return lax.dot_general(a, b, (((1,), (0,)), ((), ())), preferred_element_type=jnp.float32)


def tn(a, b):
    return lax.dot_general(a, b, (((0,), (0,)), ((), ())), preferred_element_type=jnp.float32)


def pack_kernel(group, a_ref, b_ref, out_ref):
    for h in range(group):
        for slot, ref in enumerate((a_ref, b_ref)):
            for block in range(4):
                out_ref[block % 2, h, slot, block // 2] = ref[
                    block * BLOCK : (block + 1) * BLOCK, h * HD : (h + 1) * HD
                ]


def pack(a, b, heads):
    group = min(heads, 4)
    spec = pl.BlockSpec((4 * BLOCK, group * HD), lambda i: (0, i))
    return pl.pallas_call(
        functools.partial(pack_kernel, group),
        grid=(heads // group,),
        in_specs=[spec, spec],
        out_specs=pl.BlockSpec((2, group, 2, 2, BLOCK, HD), lambda i: (0, i, 0, 0, 0, 0)),
        out_shape=jax.ShapeDtypeStruct((2, heads, 2, 2, BLOCK, HD), a.dtype),
        name="pack",
    )(a, b)


def unpack_kernel(group, in_ref, a_ref, b_ref):
    for h in range(group):
        for slot, ref in enumerate((a_ref, b_ref)):
            for block in range(4):
                ref[block * BLOCK : (block + 1) * BLOCK, h * HD : (h + 1) * HD] = in_ref[
                    block % 2, h, slot, block // 2
                ]


def unpack(x, heads):
    group = min(heads, 4)
    spec = pl.BlockSpec((4 * BLOCK, group * HD), lambda i: (0, i))
    shape = jax.ShapeDtypeStruct((4 * BLOCK, heads * HD), x.dtype)
    return pl.pallas_call(
        functools.partial(unpack_kernel, group),
        grid=(heads // group,),
        in_specs=[pl.BlockSpec((2, group, 2, 2, BLOCK, HD), lambda i: (0, i, 0, 0, 0, 0))],
        out_specs=[spec, spec],
        out_shape=[shape, shape],
        name="unpack",
    )(x)


def attention_kernel(
    places,
    unroll,
    core_ref,
    table_ref,
    gain_ref,
    qg_ref,
    kv_own,
    kv_other,
    ad_ref,
    own_out,
    other_out,
    k_scr,
    v_scr,
    acc_k,
    acc_v,
    score_scr,
    in_sem,
    out_sem,
):
    core = core_ref[0]
    total_blocks = 4 * places
    chunk = 4
    copies = [
        pltpu.make_async_copy(kv_own.at[:, 0], k_scr.at[core], in_sem.at[0]),
        pltpu.make_async_copy(kv_other.at[:, 0], k_scr.at[1 - core], in_sem.at[1]),
        pltpu.make_async_copy(kv_own.at[:, 1], v_scr.at[core], in_sem.at[2]),
        pltpu.make_async_copy(kv_other.at[:, 1], v_scr.at[1 - core], in_sem.at[3]),
    ]
    for copy in copies:
        copy.start()
    for copy in copies:
        copy.wait()

    gain = gain_ref[...]
    for parity in range(2):

        def scale_keys(t, carry):
            rows = k_scr[parity, pl.ds(t * chunk, chunk)].astype(jnp.float32)
            k_scr[parity, pl.ds(t * chunk, chunk)] = (rows * gain).astype(jnp.bfloat16)
            return carry

        lax.fori_loop(0, places // chunk, scale_keys, 0)

    steps = places // chunk
    width = chunk * 2 * BLOCK
    query = qg_ref[0, 0, 0]
    grad = qg_ref[0, 1, 0]

    def lanes(x, op):
        out = x[:, :HD]
        for t in range(1, width // HD):
            out = op(out, x[:, t * HD : (t + 1) * HD])
        return out

    def rows_of(ref, t):
        return ref[t // steps, pl.ds((t % steps) * chunk, chunk)].reshape(width, HD)

    def dense_scores(t, top):
        scores = nt(query, rows_of(k_scr, t))
        score_scr[t] = scores
        return jnp.maximum(top, lanes(scores, jnp.maximum))

    top = lax.fori_loop(
        0, 2 * steps, dense_scores, jnp.full((BLOCK, HD), NEGATIVE, jnp.float32)
    )
    top = jnp.max(top, axis=1, keepdims=True)

    def dense_expo(t, carry):
        total, numer = carry
        expo = jnp.exp2((score_scr[t] - top) * EXP_SCALE)
        score_scr[t] = expo
        numer = numer + nn(expo.astype(jnp.bfloat16), rows_of(v_scr, t))
        return total + lanes(expo, jnp.add), numer

    zero = jnp.zeros((BLOCK, HD), jnp.float32)
    total, numer = lax.fori_loop(0, 2 * steps, dense_expo, (zero, zero))
    inverse = 1.0 / jnp.sum(total, axis=1, keepdims=True)
    attended = (numer * inverse).astype(jnp.bfloat16)
    ad_ref[0, 0, 0] = attended
    delta = jnp.sum(grad.astype(jnp.float32) * attended.astype(jnp.float32), axis=1, keepdims=True)

    def dense_back(t, dquery):
        key_rows = rows_of(k_scr, t)
        weights = score_scr[t] * inverse
        dprobs = nt(grad, rows_of(v_scr, t))
        dscores = (weights * (dprobs - delta) * SCALE).astype(jnp.bfloat16)
        where = (t // steps, pl.ds((t % steps) * chunk, chunk))
        acc_k[where] = tn(dscores, query).reshape(chunk, 2, BLOCK, HD)
        acc_v[where] = tn(weights.astype(jnp.bfloat16), grad).reshape(chunk, 2, BLOCK, HD)
        return dquery + nn(dscores, key_rows)

    dquery = lax.fori_loop(0, 2 * steps, dense_back, zero)
    ad_ref[0, 1, 0] = dquery.astype(jnp.bfloat16)

    column = lax.broadcasted_iota(jnp.int32, (1, 8 * BLOCK), 1) // BLOCK

    def locate(block):
        half = block // 2
        return (block % 2, half // 2, half % 2)

    def sparse_block(n):
        block = 2 * n + core
        at_query = (n // 2, n % 2)
        listing = [
            (0, 0, 0),
            (1, 0, 0),
            locate(jnp.maximum(block - 1, 0)),
            locate(block),
            locate(jnp.minimum(block + 1, total_blocks - 1)),
        ] + [locate(table_ref[n * NR + r]) for r in range(NR)]
        query = qg_ref[at_query[0], 0, at_query[1]]
        grad = qg_ref[at_query[0], 1, at_query[1]]
        key_list = jnp.concatenate([k_scr[where] for where in listing], axis=0)
        value_list = jnp.concatenate([v_scr[where] for where in listing], axis=0)
        masked = ((column == 2) & (block == 2)) | ((column == 4) & (block == total_blocks - 1))
        scores = nt(query, key_list) + jnp.where(masked, NEGATIVE, 0.0)
        top = jnp.max(scores, axis=1, keepdims=True)
        expo = jnp.exp2((scores - top) * EXP_SCALE)
        inverse = 1.0 / jnp.sum(expo, axis=1, keepdims=True)
        numer = nn(expo.astype(jnp.bfloat16), value_list)
        attended = (numer * inverse).astype(jnp.bfloat16)
        delta = jnp.sum(
            grad.astype(jnp.float32) * attended.astype(jnp.float32), axis=1, keepdims=True
        )
        dprobs = nt(grad, value_list)
        weights = expo * inverse
        dscores = (weights * (dprobs - delta) * SCALE).astype(jnp.bfloat16)
        dquery = nn(dscores, key_list)
        dkey = tn(dscores, query)
        dvalue = tn(weights.astype(jnp.bfloat16), grad)
        ad_ref[at_query[0], 0, at_query[1]] = attended
        ad_ref[at_query[0], 1, at_query[1]] = dquery.astype(jnp.bfloat16)
        return listing, dkey, dvalue

    def sparse_step(t, carry):
        done = [sparse_block(1 + t * unroll + u) for u in range(unroll)]
        for listing, dkey, dvalue in done:
            for slot, where in enumerate(listing):
                acc_k[where] += dkey[slot * BLOCK : (slot + 1) * BLOCK]
                acc_v[where] += dvalue[slot * BLOCK : (slot + 1) * BLOCK]
        return carry

    lax.fori_loop(0, (2 * places - 1) // unroll, sparse_step, 0)

    def round_other(t, carry):
        where = pl.ds(t * chunk, chunk)
        other_out[where, 0] = acc_k[1 - core, where].astype(jnp.bfloat16)
        other_out[where, 1] = acc_v[1 - core, where].astype(jnp.bfloat16)
        return carry

    copies = [
        pltpu.make_async_copy(acc_k.at[core], own_out.at[:, 0], out_sem.at[0]),
        pltpu.make_async_copy(acc_v.at[core], own_out.at[:, 1], out_sem.at[1]),
    ]
    for copy in copies:
        copy.start()
    lax.fori_loop(0, places // chunk, round_other, 0)
    for copy in copies:
        copy.wait()


def attention(core, table, gain, qg, kv_own, kv_other, places):
    unroll = 3 if (2 * places - 1) % 3 == 0 else 1
    shape = (places, 2, 2, BLOCK, HD)
    half = (2, places, 2, BLOCK, HD)
    smem = pl.BlockSpec(memory_space=pltpu.SMEM)
    vmem = pl.BlockSpec(memory_space=pltpu.VMEM)
    hbm = pl.BlockSpec(memory_space=pl.ANY)
    return pl.pallas_call(
        functools.partial(attention_kernel, places, unroll),
        in_specs=[smem, smem, vmem, vmem, hbm, hbm],
        out_specs=[vmem, hbm, vmem],
        out_shape=[
            jax.ShapeDtypeStruct(shape, jnp.bfloat16),
            jax.ShapeDtypeStruct(shape, jnp.float32),
            jax.ShapeDtypeStruct(shape, jnp.bfloat16),
        ],
        scratch_shapes=[
            pltpu.VMEM(half, jnp.bfloat16),
            pltpu.VMEM(half, jnp.bfloat16),
            pltpu.VMEM(half, jnp.float32),
            pltpu.VMEM(half, jnp.float32),
            pltpu.VMEM((places // 2, BLOCK, 8 * BLOCK), jnp.float32),
            pltpu.SemaphoreType.DMA((4,)),
            pltpu.SemaphoreType.DMA((2,)),
        ],
        compiler_params=pltpu.CompilerParams(vmem_limit_bytes=48 * 1024 * 1024),
        name="attention",
    )(core, table, gain, qg, kv_own, kv_other)


def finish_kernel(own_ref, other_ref, kv_ref, gain_ref, out_ref, gain_out):
    gain = gain_ref[...]
    dkey = own_ref[:, 0] + other_ref[:, 0].astype(jnp.float32)
    out_ref[:, 0] = (dkey * gain).astype(jnp.bfloat16)
    out_ref[:, 1] = (own_ref[:, 1] + other_ref[:, 1].astype(jnp.float32)).astype(jnp.bfloat16)
    term = jnp.sum(dkey * kv_ref[:, 0].astype(jnp.float32), axis=(0, 1, 2)).reshape(1, HD)

    @pl.when(pl.program_id(0) == 0)
    def _():
        gain_out[...] = term

    @pl.when(pl.program_id(0) > 0)
    def _():
        gain_out[...] += term


def finish(own, other, kv, gain, places):
    group = 4
    block = (group, 2, 2, BLOCK, HD)
    spec = pl.BlockSpec(block, lambda i: (i, 0, 0, 0, 0))
    row = pl.BlockSpec((1, HD), lambda i: (0, 0))
    return pl.pallas_call(
        finish_kernel,
        grid=(places // group,),
        in_specs=[spec, spec, spec, row],
        out_specs=[spec, row],
        out_shape=[
            jax.ShapeDtypeStruct(own.shape, jnp.bfloat16),
            jax.ShapeDtypeStruct((1, HD), jnp.float32),
        ],
        name="finish",
    )(own, other, kv, gain)


def shards(queries, keys, values, key_gain, random_blocks, out_grad):
    heads = queries.shape[2] // HD
    places = lax.axis_size("seq")
    dp = lax.axis_size("dp")
    core = lax.axis_index("dp") % 2
    head = lax.axis_index("seq") % heads
    pairs = [[i, i + 1] for i in range(0, dp, 2)]
    swap = [(i, i ^ 1) for i in range(dp)]

    def between_cores(x):
        return lax.all_to_all(
            x, "dp", split_axis=0, concat_axis=0, axis_index_groups=pairs, tiled=True
        )

    def over_seq(x):
        return lax.all_to_all(x, "seq", split_axis=0, concat_axis=0, tiled=True)

    shape = (places, 2, 2, BLOCK, HD)
    by_parity = (2, heads, 2, 2, BLOCK, HD)

    named = lax.dynamic_index_in_dim(
        random_blocks.reshape(heads, 2, 2, NR), core, axis=2, keepdims=False
    ).reshape(1, heads, 2 * NR)
    table = over_seq(jnp.broadcast_to(named, (2, heads, 2 * NR)).reshape(places, 2 * NR))
    gain = lax.dynamic_slice_in_dim(key_gain, head * HD, HD).reshape(1, HD)

    kv = over_seq(between_cores(pack(keys[0], values[0], heads)).reshape(shape))
    qg = over_seq(between_cores(pack(queries[0], out_grad[0], heads)).reshape(shape))
    kv_other = lax.ppermute(kv, "dp", swap)

    ad, own, other = attention(
        core.reshape(1), table.reshape(2 * places * NR), gain, qg, kv, kv_other, places
    )
    ad = between_cores(over_seq(ad).reshape(by_parity))
    attended, query_grad = unpack(ad, heads)

    dkv, gain_term = finish(own, lax.ppermute(other, "dp", swap), kv, gain, places)
    gain_terms = over_seq(jnp.broadcast_to(gain_term, (places, HD)))
    gain_sum = jnp.sum(gain_terms.reshape(2, heads * HD), axis=0)
    gain_all = lax.all_to_all(
        jnp.broadcast_to(gain_sum, (dp, heads * HD)), "dp", split_axis=0, concat_axis=0, tiled=True
    )
    gain_grad = jnp.sum(gain_all, axis=0)

    dkv = between_cores(over_seq(dkv).reshape(by_parity))
    key_grad, value_grad = unpack(dkv, heads)
    return (attended[None], query_grad[None], key_grad[None], value_grad[None], gain_grad)


def solution(mesh):
    rows = P("dp", "seq", None)
    return jax.shard_map(
        shards,
        mesh=mesh,
        in_specs=(rows, rows, rows, P(), P(None, "seq", None), rows),
        out_specs=(rows, rows, rows, rows, P()),
        check_vma=False,
    )
```

time: 1450 us -> 379 us (0.26)
  blocking collectives: 537 us -> 172 us
  local copies, waits for them, and re-layouts: 289 us -> 3.4 us
  waiting for transfers between devices: 354 us -> 90 us
  matrix products: 154 us -> 0 us
  Pallas kernels: 0 us -> 82.9 us
  other arithmetic: 53.4 us -> 2.05 us
    psum x2 -> x0, waiting for transfers between devices: 306 us -> none  [the longest x1 206 us: broadcast(): return lax.psum(block, axis)]
    psum x3 -> x0, blocking collectives: 288 us -> none  [the longest x1 123 us: shards(): edge_dquery_sum, global_sum = lax.psum((edge_dquery, global_part), 'seq')]
    pmax x1 -> x0, blocking collectives: 248 us -> none  [shards(): edge_top = lax.pmax(jnp.max(edge_scores, axis=2), 'seq')]
    all_to_all x0 -> x8, blocking collectives: none -> 172 us  [the longest x4 136 us: over_seq(): return lax.all_to_all(x, 'seq', split_axis=0, concat_axis=0, tiled=True)]
    dot_general x63 -> x0, matrix products: 140 us -> none  [the longest x24 41.4 us: spread_terms(): jnp.einsum('hpbc,hpbd->hpcd', coef_blocks[:, :, :, NG + offset], rows_in,...]
    all_to_all x3, waiting for transfers between devices: 1.84 us -> 86.3 us  [the longest x2 86.3 us: over_seq(): return lax.all_to_all(x, 'seq', split_axis=0, concat_axis=0, tiled=True)]
    pallas_call x0 -> x6, Pallas kernels: none -> 82.9 us  [the longest x1 60.3 us: attention(): pl.pallas_call(functools.partial(attention_kernel, places, unroll), in_sp...]
    while x160 -> x0, local copies, waits for them, and re-layouts: 46.8 us -> none
  transfers between devices with their start and end apart: 9 -> 5, of which waited for: 5 -> 3; matrix products, arithmetic and copies ran while one was open for 7% -> 1% of each run, Pallas kernels for 0% -> 2%
where the time goes in v1:
time: 379 us; the launch traced here: 378 us
  blocking collectives  172 us (45%)
  waiting for transfers between devices  90 us (24%)
  Pallas kernels  82.9 us (22%)
  starting transfers between devices  26.1 us (7%)
    all_to_all x4, blocking collectives, over_seq(): return lax.all_to_all(x, 'seq', split_axis=0, concat_axis=0, tiled=True)  136 us
    all_to_all x2, waiting for transfers between devices, over_seq(): return lax.all_to_all(x, 'seq', split_axis=0, concat_axis=0, tiled=True)  86.3 us
    pallas_call x1, Pallas kernels, attention(): pl.pallas_call(functools.partial(attention_kernel, places, unroll), in_sp...  60.3 us
    all_to_all x3, blocking collectives, between_cores(): lax.all_to_all(x, 'dp', split_axis=0, concat_axis=0, axis_index_groups=pa...  26 us
    all_to_all x2, starting transfers between devices, over_seq(): return lax.all_to_all(x, 'seq', split_axis=0, concat_axis=0, tiled=True)  11.6 us
    all_to_all x1, blocking collectives, shards(): lax.all_to_all(jnp.broadcast_to(gain_sum, (dp, heads * HD)), 'dp', split_...  10.8 us
    pallas_call x2, Pallas kernels, pack(): pl.pallas_call(functools.partial(pack_kernel, group), grid=(heads // grou...  7.77 us
    pallas_call x2, Pallas kernels, unpack(): pl.pallas_call(functools.partial(unpack_kernel, group), grid=(heads // gr...  7.76 us
  transfers between devices with their start and end apart: 5, of which 3 were waited for; matrix products, arithmetic and copies ran while one was open for 1% of the time, Pallas kernels for 2%

profile of v1, /device:TPU:1, one launch (start us, length us, event | category | flops | bytes accessed | tf_op | source)
XLA Modules:
  0.0 377.6 jit_solution(12201784709282684285)
XLA Ops:
  0.6 0.0 copy-start
  0.6 3.9 %pack.3 = bf16[2,16,2,2,64,128]{5,4,3,2,1,0:T(8,128)(2,1)} custom-call(bf16[256,2048]{1,0:T(8,128)(2,1)} %bitcast.24, bf16[256,2048]{1,0:T(8,128)(2,1)} %bitcast.25), custom_call_target="tpu_custom_call" | custom-call | tf_op jit(solution)/shard_map/pack/pallas_call | solution.py:43
  4.5 0.0 copy-start.5
  4.5 7.1 %all-to-all-start.3 = ((bf16[2,16,2,2,64,128]{5,4,3,2,1,0:T(8,128)(2,1)}), bf16[2,16,2,2,64,128]{5,4,3,2,1,0:T(8,128)(2,1)S(1)}, u32[]{:S(2)}, u32[]{:S(2)}) async-start(bf16[2,16,2,2,64,128]{5,4,3,2,1,0:T(8,128)(2,1)} %pack.3), calls=%async_computation.3 | async-start | bytes 4194304 | tf_op jit(solution)/shard_map/all_to_all | solution.py:312
  11.6 0.0 copy-done.5
  11.7 0.1 copy.20
  11.8 3.9 %pack.2 = bf16[2,16,2,2,64,128]{5,4,3,2,1,0:T(8,128)(2,1)} custom-call(bf16[256,2048]{1,0:T(8,128)(2,1)} %bitcast.26, bf16[256,2048]{1,0:T(8,128)(2,1)} %bitcast.27), custom_call_target="tpu_custom_call" | custom-call | tf_op jit(solution)/shard_map/pack/pallas_call | solution.py:43
  15.7 0.0 all-to-all-done.3
  15.7 0.0 copy-start.3
  15.7 8.2 %all_to_all.61 = bf16[2,16,2,2,64,128]{5,4,3,2,1,0:T(8,128)(2,1)} all-to-all(bf16[2,16,2,2,64,128]{5,4,3,2,1,0:T(8,128)(2,1)} %pack.2), channel_id=1, replica_groups={{0,32},{64,96},{128,160},{192,224},{1,33},{65,97},{129,161},{193,225},{..., dimensions={0} | all-to-all | bytes 4194304 | tf_op jit(solution)/shard_map/all_to_all | solution.py:312
  23.9 0.0 copy-done.3
  23.9 17.8 %all_to_all.62 = s32[32,1,6]{2,1,0:T(1,128)S(1)} all-to-all(s32[32,1,6]{2,1,0:T(1,128)S(1)} %bitcast.28), channel_id=1, replica_groups=mesh['dp'=8,'seq'=32] {'seq'}, dimensions={0} | all-to-all | bytes 1536 | tf_op jit(solution)/shard_map/all_to_all | solution.py:317
  41.8 52.1 %all_to_all.63.kv_own.kv_ref = bf16[32,2,2,64,128]{4,3,2,1,0:T(8,128)(2,1)S(1)} all-to-all(bf16[32,2,2,64,128]{4,3,2,1,0:T(8,128)(2,1)} %bitcast.21), channel_id=1, replica_groups=mesh['dp'=8,'seq'=32] {'seq'}, dimensions={0} | all-to-all | bytes 4194304 | tf_op jit(solution)/shard_map/all_to_all | solution.py:317
  93.9 0.0 copy-start.2
  93.9 6.7 %all-to-all-start.2 = ((bf16[32,2,2,64,128]{4,3,2,1,0:T(8,128)(2,1)}), bf16[32,2,2,64,128]{4,3,2,1,0:T(8,128)(2,1)}, u32[]{:S(2)}, u32[]{:S(2)}) async-start(bf16[32,2,2,64,128]{4,3,2,1,0:T(8,128)(2,1)} %bitcast.20), calls=%async_computation.2 | async-start | bytes 4194304 | tf_op jit(solution)/shard_map/all_to_all | solution.py:317
  100.6 0.0 copy-done.2
  100.6 2.5 collective-permute-start
  103.0 0.0 copy-done
  103.0 0.1 dynamic-slice_bitcast_fusion.gain_ref
  103.1 0.0 copy-start.1
  103.1 0.5 broadcast.15
  103.6 0.7 reduce.7
  104.3 0.1 reshape.58.table_ref
  104.4 42.4 %all-to-all-done.2.qg_ref = bf16[32,2,2,64,128]{4,3,2,1,0:T(8,128)(2,1)} async-done(((bf16[32,2,2,64,128]{4,3,2,1,0:T(8,128)(2,1)}), bf16[32,2,2,64,128]{4,3,2,1,0:T(8,128)(2,1)}, u32[]{:S(2)}, u32[]{:S(2)}) %all-to-all-start.2) | async-done | bytes 2097184 | tf_op jit(solution)/shard_map/all_to_all | solution.py:317
  146.8 0.0 collective-permute-done.kv_other
  146.8 60.3 %attention.1 = (bf16[32,2,2,64,128]{4,3,2,1,0:T(8,128)(2,1)S(1)}, f32[32,2,2,64,128]{4,3,2,1,0:T(8,128)}, bf16[32,2,2,64,128]{4,3,2,1,0:T(8,128)(2,1)S(1)}) custom-call(s32[1]{0:T(128)} %bitcast.core_ref, s32[192]{0:T(256)S(1)} %reshape.58.table_ref, f32[1,128]{1,0:T(1,128)S(1)} %dynamic-slice_bitcast_fusion.gain_ref, ...), custom_call_target="tpu_custom_call" | custom-call | tf_op jit(solution)/shard_map/attention/pallas_call | solution.py:245
  207.1 0.0 copy-done.1
  207.1 4.9 %collective-permute-start.1 = (bf16[32,2,2,64,128]{4,3,2,1,0:T(8,128)(2,1)S(1)}, bf16[32,2,2,64,128]{4,3,2,1,0:T(8,128)(2,1)S(1)}, u32[]{:S(2)}, u32[]{:S(2)}) collective-permute-start(bf16[32,2,2,64,128]{4,3,2,1,0:T(8,128)(2,1)S(1)} %get-tuple-element.18), channel_id=1, source_target_pairs={{0,32},{32,0},{64,96},{96,64},{128,160},{160,128},{192,224},{224,1... | collective-permute-start | bytes 6291464 | tf_op jit(solution)/shard_map/ppermute | solution.py:338
  212.0 3.8 %collective-permute-done.1.other_ref = bf16[32,2,2,64,128]{4,3,2,1,0:T(8,128)(2,1)S(1)} collective-permute-done((bf16[32,2,2,64,128]{4,3,2,1,0:T(8,128)(2,1)S(1)}, bf16[32,2,2,64,128]{4,3,2,1,0:T(8,128)(2,1)S(1)}, u32[]{:S(2)}, u32[]{:S(2)}) %collective-permute-start.1) | collective-permute-done | bytes 2097184 | tf_op jit(solution)/shard_map/ppermute | solution.py:338
  215.8 0.0 copy-start.4
  215.8 1.4 copy-done.4
  217.2 7.1 %finish.1 = (bf16[32,2,2,64,128]{4,3,2,1,0:T(8,128)(2,1)}, f32[1,128]{1,0:T(1,128)}) custom-call(f32[32,2,2,64,128]{4,3,2,1,0:T(8,128)} %get-tuple-element.17.own_ref, bf16[32,2,2,64,128]{4,3,2,1,0:T(8,128)(2,1)} %copy-done.4, bf16[32,2,2,64,128]{4,3,2,1,0:T(8,128)(2,1)} %copy-done.2, f32[1,128]{1,0:T(1,128)} %copy-done.1), custom_call_target="tpu_custom_call" | custom-call | tf_op jit(solution)/shard_map/finish/pallas_call | solution.py:289
  224.2 0.7 broadcast_in_dim.33
  224.9 14.0 %all_to_all.64 = f32[32,1,128]{2,1,0:T(1,128)S(1)} all-to-all(f32[32,1,128]{2,1,0:T(1,128)S(1)} %broadcast_in_dim.33), channel_id=1, replica_groups=mesh['dp'=8,'seq'=32] {'seq'}, dimensions={0} | all-to-all | bytes 32768 | tf_op jit(solution)/shard_map/all_to_all | solution.py:317
  238.9 0.5 broadcast.16
  239.4 0.7 reduce.8
  240.2 10.8 %all_to_all.65 = f32[8,1,2048]{2,1,0:T(1,128)S(1)} all-to-all(f32[8,1,2048]{2,1,0:T(1,128)S(1)} %broadcast_in_dim.34), channel_id=1, replica_groups=mesh['dp'=8,'seq'=32] {'dp'}, dimensions={0} | all-to-all | bytes 131072 | tf_op jit(solution)/shard_map/all_to_all | solution.py:341
  251.0 51.6 %all_to_all.66 = bf16[32,2,2,64,128]{4,3,2,1,0:T(8,128)(2,1)S(1)} all-to-all(bf16[32,2,2,64,128]{4,3,2,1,0:T(8,128)(2,1)S(1)} %get-tuple-element.14), channel_id=1, replica_groups=mesh['dp'=8,'seq'=32] {'seq'}, dimensions={0} | all-to-all | bytes 4194304 | tf_op jit(solution)/shard_map/all_to_all | solution.py:317
  302.6 9.1 %all_to_all.67.in_ref = bf16[2,16,2,2,64,128]{5,4,3,2,1,0:T(8,128)(2,1)} all-to-all(bf16[2,16,2,2,64,128]{5,4,3,2,1,0:T(8,128)(2,1)S(1)} %bitcast.23), channel_id=1, replica_groups={{0,32},{64,96},{128,160},{192,224},{1,33},{65,97},{129,161},{193,225},{..., dimensions={0} | all-to-all | bytes 4194304 | tf_op jit(solution)/shard_map/all_to_all | solution.py:312
  311.7 5.0 %all-to-all-start.7 = ((bf16[32,2,2,64,128]{4,3,2,1,0:T(8,128)(2,1)}), bf16[32,2,2,64,128]{4,3,2,1,0:T(8,128)(2,1)S(1)}, u32[]{:S(2)}, u32[]{:S(2)}) async-start(bf16[32,2,2,64,128]{4,3,2,1,0:T(8,128)(2,1)} %get-tuple-element.19), calls=%async_computation.7 | async-start | bytes 4194304 | tf_op jit(solution)/shard_map/all_to_all | solution.py:317
  316.7 0.7 reduce_sum.19
  317.3 3.9 %unpack.2 = (bf16[256,2048]{1,0:T(8,128)(2,1)}, bf16[256,2048]{1,0:T(8,128)(2,1)}) custom-call(bf16[2,16,2,2,64,128]{5,4,3,2,1,0:T(8,128)(2,1)} %all_to_all.67.in_ref), custom_call_target="tpu_custom_call" | custom-call | tf_op jit(solution)/shard_map/unpack/pallas_call | solution.py:66
  321.2 43.8 %all-to-all-done.7 = bf16[32,2,2,64,128]{4,3,2,1,0:T(8,128)(2,1)S(1)} async-done(((bf16[32,2,2,64,128]{4,3,2,1,0:T(8,128)(2,1)}), bf16[32,2,2,64,128]{4,3,2,1,0:T(8,128)(2,1)S(1)}, u32[]{:S(2)}, u32[]{:S(2)}) %all-to-all-start.7) | async-done | bytes 2097184 | tf_op jit(solution)/shard_map/all_to_all | solution.py:317
  365.0 8.6 %all_to_all.68.in_ref = bf16[2,16,2,2,64,128]{5,4,3,2,1,0:T(8,128)(2,1)} all-to-all(bf16[2,16,2,2,64,128]{5,4,3,2,1,0:T(8,128)(2,1)S(1)} %bitcast.22), channel_id=1, replica_groups={{0,32},{64,96},{128,160},{192,224},{1,33},{65,97},{129,161},{193,225},{..., dimensions={0} | all-to-all | bytes 4194304 | tf_op jit(solution)/shard_map/all_to_all | solution.py:312
  373.7 3.9 %unpack.3 = (bf16[256,2048]{1,0:T(8,128)(2,1)}, bf16[256,2048]{1,0:T(8,128)(2,1)}) custom-call(bf16[2,16,2,2,64,128]{5,4,3,2,1,0:T(8,128)(2,1)} %all_to_all.68.in_ref), custom_call_target="tpu_custom_call" | custom-call | tf_op jit(solution)/shard_map/unpack/pallas_call | solution.py:66
  (7 shorter events, 0.1 us)
Async XLA Ops:
  0.6 102.4 %copy-start = (f32[2048]{0:T(1024)S(1)}, f32[2048]{0:T(1024)}, u32[]{:S(2)}) copy-start(f32[2048]{0:T(1024)} %param.9) | copy-start | bytes 24580
  4.5 7.1 %copy-start.5 = (s32[16,4,3]{0,1,2:T(4,128)S(1)}, s32[16,4,3]{0,1,2:T(4,128)}, u32[]{:S(2)}) copy-start(s32[16,4,3]{0,1,2:T(4,128)} %param.10) | copy-start | bytes 2308
  4.5 11.1 %all-to-all-start.3 = ((bf16[2,16,2,2,64,128]{5,4,3,2,1,0:T(8,128)(2,1)}), bf16[2,16,2,2,64,128]{5,4,3,2,1,0:T(8,128)(2,1)S(1)}, u32[]{:S(2)}, u32[]{:S(2)}) async-start(bf16[2,16,2,2,64,128]{5,4,3,2,1,0:T(8,128)(2,1)} %pack.3), calls=%async_computation.3 | async-start | bytes 4194304 | tf_op jit(solution)/shard_map/all_to_all | solution.py:312
  15.7 8.2 %copy-start.3 = (bf16[2,16,2,2,64,128]{5,4,3,2,1,0:T(8,128)(2,1)}, bf16[2,16,2,2,64,128]{5,4,3,2,1,0:T(8,128)(2,1)S(1)}, u32[]{:S(2)}) copy-start(bf16[2,16,2,2,64,128]{5,4,3,2,1,0:T(8,128)(2,1)S(1)} %all-to-all-done.3) | copy-start | bytes 6291460
  93.9 6.7 %copy-start.2 = (bf16[32,2,2,64,128]{4,3,2,1,0:T(8,128)(2,1)}, bf16[32,2,2,64,128]{4,3,2,1,0:T(8,128)(2,1)S(1)}, u32[]{:S(2)}) copy-start(bf16[32,2,2,64,128]{4,3,2,1,0:T(8,128)(2,1)S(1)} %all_to_all.63.kv_own.kv_ref) | copy-start | bytes 6291460
  93.9 52.9 %all-to-all-start.2 = ((bf16[32,2,2,64,128]{4,3,2,1,0:T(8,128)(2,1)}), bf16[32,2,2,64,128]{4,3,2,1,0:T(8,128)(2,1)}, u32[]{:S(2)}, u32[]{:S(2)}) async-start(bf16[32,2,2,64,128]{4,3,2,1,0:T(8,128)(2,1)} %bitcast.20), calls=%async_computation.2 | async-start | bytes 4194304 | tf_op jit(solution)/shard_map/all_to_all | solution.py:317
  100.6 46.3 %collective-permute-start = (bf16[32,2,2,64,128]{4,3,2,1,0:T(8,128)(2,1)S(1)}, bf16[32,2,2,64,128]{4,3,2,1,0:T(8,128)(2,1)}, u32[]{:S(2)}, u32[]{:S(2)}) collective-permute-start(bf16[32,2,2,64,128]{4,3,2,1,0:T(8,128)(2,1)S(1)} %all_to_all.63.kv_own.kv_ref), channel_id=1, source_target_pairs={{0,32},{32,0},{64,96},{96,64},{128,160},{160,128},{192,224},{224,1... | collective-permute-start | bytes 6291464 | tf_op jit(solution)/shard_map/ppermute | solution.py:330
  103.1 104.0 %copy-start.1 = (f32[1,128]{1,0:T(1,128)}, f32[1,128]{1,0:T(1,128)S(1)}, u32[]{:S(2)}) copy-start(f32[1,128]{1,0:T(1,128)S(1)} %dynamic-slice_bitcast_fusion.gain_ref) | copy-start | bytes 1540
  207.1 8.7 %collective-permute-start.1 = (bf16[32,2,2,64,128]{4,3,2,1,0:T(8,128)(2,1)S(1)}, bf16[32,2,2,64,128]{4,3,2,1,0:T(8,128)(2,1)S(1)}, u32[]{:S(2)}, u32[]{:S(2)}) collective-permute-start(bf16[32,2,2,64,128]{4,3,2,1,0:T(8,128)(2,1)S(1)} %get-tuple-element.18), channel_id=1, source_target_pairs={{0,32},{32,0},{64,96},{96,64},{128,160},{160,128},{192,224},{224,1... | collective-permute-start | bytes 6291464 | tf_op jit(solution)/shard_map/ppermute | solution.py:338
  215.8 1.4 copy-start.4
  311.7 53.4 %all-to-all-start.7 = ((bf16[32,2,2,64,128]{4,3,2,1,0:T(8,128)(2,1)}), bf16[32,2,2,64,128]{4,3,2,1,0:T(8,128)(2,1)S(1)}, u32[]{:S(2)}, u32[]{:S(2)}) async-start(bf16[32,2,2,64,128]{4,3,2,1,0:T(8,128)(2,1)} %get-tuple-element.19), calls=%async_computation.7 | async-start | bytes 4194304 | tf_op jit(solution)/shard_map/all_to_all | solution.py:317

commit v2 on v1

v2 whole, which is shorter than its diff:
```python
import functools
import math

import jax
import jax.numpy as jnp
from jax import lax
from jax.experimental import pallas as pl
from jax.experimental.pallas import tpu as pltpu
from jax.sharding import PartitionSpec as P

HD = 128
BLOCK = 64
NR = 3
NK = 8
PAIR = 2 * BLOCK
CHUNK = 4
WIDTH = CHUNK * PAIR
SPARE = 16
NEGATIVE = -1e30
SCALE = HD**-0.5
EXP_SCALE = SCALE * math.log2(math.e)
VMEM_LIMIT = 56 * 1024 * 1024


def nt(a, b):
    return lax.dot_general(a, b, (((1,), (1,)), ((), ())), preferred_element_type=jnp.float32)


def nn(a, b):
    return lax.dot_general(a, b, (((1,), (0,)), ((), ())), preferred_element_type=jnp.float32)


def tn(a, b):
    return lax.dot_general(a, b, (((0,), (0,)), ((), ())), preferred_element_type=jnp.float32)


def pack_kernel(group, count, with_spare, core_ref, *refs):
    core = core_ref[0]
    keep_ref, send_ref = refs[-2:]
    for out_ref, parity in ((keep_ref, core), (send_ref, 1 - core)):
        for h in range(group):
            columns = slice(h * HD, (h + 1) * HD)
            for slot in range(count):
                for turn in range(2):
                    row = slot * PAIR + turn * BLOCK
                    at = pl.multiple_of((2 * turn + parity) * BLOCK, BLOCK)
                    out_ref[h, row : row + BLOCK] = refs[slot][pl.ds(at, BLOCK), columns]
            if with_spare:
                out_ref[h, count * PAIR :] = jnp.broadcast_to(
                    refs[count][parity, h], (SPARE, HD)
                )


def pack(core, arrays, spare, heads):
    group = min(heads, 4)
    count = len(arrays)
    rows = count * PAIR + (SPARE if spare is not None else 0)
    specs = [pl.BlockSpec((4 * BLOCK, group * HD), lambda i, c: (0, i))] * count
    args = list(arrays)
    if spare is not None:
        specs.append(pl.BlockSpec((2, group, 1, HD), lambda i, c: (0, i, 0, 0)))
        args.append(spare)
    return pl.pallas_call(
        functools.partial(pack_kernel, group, count, spare is not None),
        grid_spec=pltpu.PrefetchScalarGridSpec(
            num_scalar_prefetch=1,
            grid=(heads // group,),
            in_specs=specs,
            out_specs=[
                pl.BlockSpec((pl.Squeezed(), group, rows, HD), lambda i, c: (c[0], i, 0, 0)),
                pl.BlockSpec((group, rows, HD), lambda i, c: (i, 0, 0)),
            ],
        ),
        out_shape=[
            jax.ShapeDtypeStruct((2, heads, rows, HD), jnp.bfloat16),
            jax.ShapeDtypeStruct((heads, rows, HD), jnp.bfloat16),
        ],
        name="pack",
    )(core, *args)


def unpack_kernel(group, core_ref, keep_ref, came_ref, *out_refs):
    core = core_ref[0]
    for in_ref, parity in ((keep_ref, core), (came_ref, 1 - core)):
        for h in range(group):
            for slot, ref in enumerate(out_refs):
                for turn in range(2):
                    row = slot * PAIR + turn * BLOCK
                    at = pl.multiple_of((2 * turn + parity) * BLOCK, BLOCK)
                    ref[pl.ds(at, BLOCK), h * HD : (h + 1) * HD] = in_ref[h, row : row + BLOCK]


def unpack(core, keep, came, count):
    heads, rows = keep.shape[1:3]
    group = min(heads, 4)
    return pl.pallas_call(
        functools.partial(unpack_kernel, group),
        grid_spec=pltpu.PrefetchScalarGridSpec(
            num_scalar_prefetch=1,
            grid=(heads // group,),
            in_specs=[
                pl.BlockSpec((pl.Squeezed(), group, rows, HD), lambda i, c: (c[0], i, 0, 0)),
                pl.BlockSpec((group, rows, HD), lambda i, c: (i, 0, 0)),
            ],
            out_specs=[pl.BlockSpec((4 * BLOCK, group * HD), lambda i, c: (0, i))] * count,
        ),
        out_shape=[jax.ShapeDtypeStruct((4 * BLOCK, heads * HD), keep.dtype)] * count,
        name="unpack",
    )(core, keep, came)


def locate(block):
    half = block // 2
    return (block % 2, half // 2, pl.ds(pl.multiple_of((half % 2) * BLOCK, BLOCK), BLOCK))


def key_places(table_ref, n, block, total_blocks):
    return [
        (0, 0, pl.ds(0, BLOCK)),
        (1, 0, pl.ds(0, BLOCK)),
        locate(jnp.maximum(block - 1, 0)),
        locate(block),
        locate(jnp.minimum(block + 1, total_blocks - 1)),
    ] + [locate(table_ref[n * NR + r]) for r in range(NR)]


def chunk_rows(ref, t, steps):
    return ref[t // steps, pl.ds((t % steps) * CHUNK, CHUNK)].reshape(WIDTH, HD)


def forward_kernel(
    places,
    unroll,
    core_ref,
    table_ref,
    gain_ref,
    own_ref,
    other_ref,
    att_ref,
    weight_ref,
    dense_ref,
    key_out,
    k_scr,
    v_scr,
    q_scr,
    score_scr,
    in_sem,
    out_sem,
):
    core = core_ref[0]
    total_blocks = 4 * places
    steps = places // CHUNK

    def rows(ref, slot):
        return ref.at[:, slot * PAIR : (slot + 1) * PAIR]

    copies = [
        pltpu.make_async_copy(rows(own_ref, 0), k_scr.at[core], in_sem.at[0]),
        pltpu.make_async_copy(rows(other_ref, 0), k_scr.at[1 - core], in_sem.at[1]),
        pltpu.make_async_copy(rows(own_ref, 2), q_scr, in_sem.at[2]),
        pltpu.make_async_copy(rows(own_ref, 1), v_scr.at[core], in_sem.at[3]),
        pltpu.make_async_copy(rows(other_ref, 1), v_scr.at[1 - core], in_sem.at[4]),
    ]
    for copy in copies:
        copy.start()
    for copy in copies[:3]:
        copy.wait()

    gain = gain_ref[...]
    query = q_scr[0, :BLOCK]

    def lanes(x, op):
        out = x[:, :HD]
        for t in range(1, WIDTH // HD):
            out = op(out, x[:, t * HD : (t + 1) * HD])
        return out

    def dense_scores(t, top):
        where = (t // steps, pl.ds((t % steps) * CHUNK, CHUNK))
        keys = (k_scr[where].astype(jnp.float32) * gain).astype(jnp.bfloat16)
        k_scr[where] = keys
        scores = nt(query, keys.reshape(WIDTH, HD))
        score_scr[t] = scores
        return jnp.maximum(top, lanes(scores, jnp.maximum))

    top = lax.fori_loop(
        0, 2 * steps, dense_scores, jnp.full((BLOCK, HD), NEGATIVE, jnp.float32)
    )
    top = jnp.max(top, axis=1, keepdims=True)
    key_copy = pltpu.make_async_copy(k_scr, key_out, out_sem)
    key_copy.start()
    for copy in copies[3:]:
        copy.wait()

    def dense_expo(t, carry):
        total, numer = carry
        expo = jnp.exp2((score_scr[t] - top) * EXP_SCALE)
        score_scr[t] = expo
        numer = numer + nn(expo.astype(jnp.bfloat16), chunk_rows(v_scr, t, steps))
        return total + lanes(expo, jnp.add), numer

    zero = jnp.zeros((BLOCK, HD), jnp.float32)
    total, numer = lax.fori_loop(0, 2 * steps, dense_expo, (zero, zero))
    inverse = 1.0 / jnp.sum(total, axis=1, keepdims=True)
    att_ref[0, :BLOCK] = (numer * inverse).astype(jnp.bfloat16)

    def dense_weights(t, carry):
        dense_ref[t] = (score_scr[t] * inverse).astype(jnp.bfloat16)
        return carry

    lax.fori_loop(0, 2 * steps, dense_weights, 0)

    column = lax.broadcasted_iota(jnp.int32, (1, NK * BLOCK), 1) // BLOCK

    def sparse_block(n):
        block = 2 * n + core
        listing = key_places(table_ref, n, block, total_blocks)
        key_list = jnp.concatenate([k_scr[where] for where in listing], axis=0)
        value_list = jnp.concatenate([v_scr[where] for where in listing], axis=0)
        mine = (n // 2, pl.ds(pl.multiple_of((n % 2) * BLOCK, BLOCK), BLOCK))
        masked = ((column == 2) & (block == 2)) | ((column == 4) & (block == total_blocks - 1))
        scores = nt(q_scr[mine], key_list) + jnp.where(masked, NEGATIVE, 0.0)
        top = jnp.max(scores, axis=1, keepdims=True)
        expo = jnp.exp2((scores - top) * EXP_SCALE)
        inverse = 1.0 / jnp.sum(expo, axis=1, keepdims=True)
        numer = nn(expo.astype(jnp.bfloat16), value_list)
        return mine, (numer * inverse).astype(jnp.bfloat16), (expo * inverse).astype(jnp.bfloat16)

    def sparse_step(t, carry):
        first = 1 + t * unroll
        done = [sparse_block(first + u) for u in range(unroll)]
        for u, (mine, attended, weights) in enumerate(done):
            att_ref[mine] = attended
            weight_ref[first + u] = weights
        return carry

    lax.fori_loop(0, (2 * places - 1) // unroll, sparse_step, 0)
    key_copy.wait()


def forward(core, table, gain, own, other, places):
    unroll = 3 if (2 * places - 1) % 3 == 0 else 1
    both = (2, places, PAIR, HD)
    smem = pl.BlockSpec(memory_space=pltpu.SMEM)
    vmem = pl.BlockSpec(memory_space=pltpu.VMEM)
    hbm = pl.BlockSpec(memory_space=pl.ANY)
    blocks = 2 * places
    return pl.pallas_call(
        functools.partial(forward_kernel, places, unroll),
        in_specs=[smem, smem, vmem, hbm, hbm],
        out_specs=[vmem, vmem, vmem, hbm],
        out_shape=[
            jax.ShapeDtypeStruct((places, PAIR, HD), jnp.bfloat16),
            jax.ShapeDtypeStruct((blocks, BLOCK, NK * BLOCK), jnp.bfloat16),
            jax.ShapeDtypeStruct((places // 2, BLOCK, WIDTH), jnp.bfloat16),
            jax.ShapeDtypeStruct(both, jnp.bfloat16),
        ],
        scratch_shapes=[
            pltpu.VMEM(both, jnp.bfloat16),
            pltpu.VMEM(both, jnp.bfloat16),
            pltpu.VMEM((places, PAIR, HD), jnp.bfloat16),
            pltpu.VMEM((places // 2, BLOCK, WIDTH), jnp.float32),
            pltpu.SemaphoreType.DMA((5,)),
            pltpu.SemaphoreType.DMA,
        ],
        compiler_params=pltpu.CompilerParams(vmem_limit_bytes=VMEM_LIMIT),
        cost_estimate=pl.CostEstimate(
            flops=4 * blocks * BLOCK * HD * 3 * NK * BLOCK,
            bytes_accessed=60 << 20,
            transcendentals=blocks * BLOCK * NK * BLOCK,
        ),
        name="forward",
    )(core, table, gain, own, other)


def backward_kernel(
    places,
    unroll,
    core_ref,
    table_ref,
    own_ref,
    other_ref,
    key_ref,
    grad_ref,
    att_ref,
    weight_ref,
    dense_ref,
    dq_ref,
    own_out,
    other_out,
    gain_out,
    k_scr,
    v_scr,
    q_scr,
    g_scr,
    a_scr,
    weight_scr,
    dense_scr,
    acc_k,
    acc_v,
    raw_scr,
    in_sem,
    out_sem,
):
    core = core_ref[0]
    total_blocks = 4 * places
    steps = places // CHUNK

    def rows(ref, slot):
        return ref.at[:, slot * PAIR : (slot + 1) * PAIR]

    copies = [
        pltpu.make_async_copy(src, dst, in_sem.at[at])
        for at, (src, dst) in enumerate(
            [
                (grad_ref, g_scr),
                (att_ref, a_scr),
                (dense_ref, dense_scr),
                (rows(own_ref, 1), v_scr.at[core]),
                (rows(other_ref, 1), v_scr.at[1 - core]),
                (key_ref, k_scr),
                (rows(own_ref, 2), q_scr),
                (weight_ref, weight_scr),
                (rows(own_ref, 0), raw_scr.at[core]),
                (rows(other_ref, 0), raw_scr.at[1 - core]),
            ]
        )
    ]
    for copy in copies:
        copy.start()
    for copy in copies[:7]:
        copy.wait()

    def row_delta(grad, attended):
        return jnp.sum(
            grad.astype(jnp.float32) * attended.astype(jnp.float32), axis=1, keepdims=True
        )

    query = q_scr[0, :BLOCK]
    grad = g_scr[0, :BLOCK]
    delta = row_delta(grad, a_scr[0, :BLOCK])

    def dense_back(t, dquery):
        weights = dense_scr[t]
        dprobs = nt(grad, chunk_rows(v_scr, t, steps))
        dscores = (weights.astype(jnp.float32) * (dprobs - delta)).astype(jnp.bfloat16)
        where = (t // steps, pl.ds((t % steps) * CHUNK, CHUNK))
        acc_k[where] = tn(dscores, query).reshape(CHUNK, PAIR, HD)
        acc_v[where] = tn(weights, grad).reshape(CHUNK, PAIR, HD)
        return dquery + nn(dscores, chunk_rows(k_scr, t, steps))

    dquery = lax.fori_loop(0, 2 * steps, dense_back, jnp.zeros((BLOCK, HD), jnp.float32))
    dq_ref[0, :BLOCK] = (dquery * SCALE).astype(jnp.bfloat16)
    for copy in copies[7:]:
        copy.wait()

    def sparse_block(n):
        block = 2 * n + core
        listing = key_places(table_ref, n, block, total_blocks)
        key_list = jnp.concatenate([k_scr[where] for where in listing], axis=0)
        value_list = jnp.concatenate([v_scr[where] for where in listing], axis=0)
        mine = (n // 2, pl.ds(pl.multiple_of((n % 2) * BLOCK, BLOCK), BLOCK))
        grad = g_scr[mine]
        weights = weight_scr[n]
        delta = row_delta(grad, a_scr[mine])
        dprobs = nt(grad, value_list)
        dscores = (weights.astype(jnp.float32) * (dprobs - delta)).astype(jnp.bfloat16)
        dquery = nn(dscores, key_list)
        dkey = tn(dscores, q_scr[mine])
        dvalue = tn(weights, grad)
        return listing, mine, dquery, dkey, dvalue

    def sparse_step(t, carry):
        done = [sparse_block(1 + t * unroll + u) for u in range(unroll)]
        for listing, mine, dquery, dkey, dvalue in done:
            dq_ref[mine] = (dquery * SCALE).astype(jnp.bfloat16)
            for slot, where in enumerate(listing):
                acc_k[where] += dkey[slot * BLOCK : (slot + 1) * BLOCK]
                acc_v[where] += dvalue[slot * BLOCK : (slot + 1) * BLOCK]
        return carry

    lax.fori_loop(0, (2 * places - 1) // unroll, sparse_step, 0)

    copies = [
        pltpu.make_async_copy(acc_k.at[core], own_out.at[0], out_sem.at[0]),
        pltpu.make_async_copy(acc_v.at[core], own_out.at[1], out_sem.at[1]),
    ]
    for copy in copies:
        copy.start()

    def round_other(t, carry):
        where = pl.ds(t * CHUNK, CHUNK)
        mine = acc_k[core, where] * raw_scr[core, where].astype(jnp.float32)
        far = acc_k[1 - core, where]
        theirs = far * raw_scr[1 - core, where].astype(jnp.float32)
        other_out[0, where] = far.astype(jnp.bfloat16)
        other_out[1, where] = acc_v[1 - core, where].astype(jnp.bfloat16)
        return carry + jnp.sum((mine + theirs).reshape(CHUNK * PAIR // 8, 8, HD), axis=0)

    gain_term = lax.fori_loop(0, steps, round_other, jnp.zeros((8, HD), jnp.float32))
    gain_term = jnp.sum(gain_term, axis=0, keepdims=True) * SCALE
    gain_out[...] = jnp.broadcast_to(gain_term, (8, HD))
    for copy in copies:
        copy.wait()


def backward(core, table, own, other, keys, grads, att, weights, dense, places):
    unroll = 3 if (2 * places - 1) % 3 == 0 else 1
    both = (2, places, PAIR, HD)
    half = (places, PAIR, HD)
    blocks = 2 * places
    smem = pl.BlockSpec(memory_space=pltpu.SMEM)
    vmem = pl.BlockSpec(memory_space=pltpu.VMEM)
    hbm = pl.BlockSpec(memory_space=pl.ANY)
    return pl.pallas_call(
        functools.partial(backward_kernel, places, unroll),
        in_specs=[smem, smem] + [hbm] * 7,
        out_specs=[vmem, hbm, vmem, vmem],
        out_shape=[
            jax.ShapeDtypeStruct(half, jnp.bfloat16),
            jax.ShapeDtypeStruct(both, jnp.float32),
            jax.ShapeDtypeStruct(both, jnp.bfloat16),
            jax.ShapeDtypeStruct((8, HD), jnp.float32),
        ],
        scratch_shapes=[
            pltpu.VMEM(both, jnp.bfloat16),
            pltpu.VMEM(both, jnp.bfloat16),
            pltpu.VMEM(half, jnp.bfloat16),
            pltpu.VMEM(half, jnp.bfloat16),
            pltpu.VMEM(half, jnp.bfloat16),
            pltpu.VMEM(weights.shape, jnp.bfloat16),
            pltpu.VMEM(dense.shape, jnp.bfloat16),
            pltpu.VMEM(both, jnp.float32),
            pltpu.VMEM(both, jnp.float32),
            pltpu.VMEM(both, jnp.bfloat16),
            pltpu.SemaphoreType.DMA((10,)),
            pltpu.SemaphoreType.DMA((2,)),
        ],
        compiler_params=pltpu.CompilerParams(vmem_limit_bytes=VMEM_LIMIT),
        cost_estimate=pl.CostEstimate(
            flops=8 * blocks * BLOCK * HD * 3 * NK * BLOCK,
            bytes_accessed=100 << 20,
            transcendentals=0,
        ),
        name="backward",
    )(core, table, own, other, keys, grads, att, weights, dense)


def finish_kernel(own_ref, other_ref, scaled_gain_ref, gain_grad_ref, out_ref):
    gain = scaled_gain_ref[...]
    dkey = own_ref[0] + other_ref[0].astype(jnp.float32)
    out_ref[:, :PAIR] = (dkey * gain).astype(jnp.bfloat16)
    dvalue = own_ref[1] + other_ref[1].astype(jnp.float32)
    out_ref[:, PAIR : 2 * PAIR] = dvalue.astype(jnp.bfloat16)
    total = gain_grad_ref[...]
    high = total.astype(jnp.bfloat16)
    rest = total - high.astype(jnp.float32)
    middle = rest.astype(jnp.bfloat16)
    low = (rest - middle.astype(jnp.float32)).astype(jnp.bfloat16)
    row = lax.broadcasted_iota(jnp.int32, (SPARE, HD), 0)
    spare = jnp.where(
        row == 0,
        high.astype(jnp.float32),
        jnp.where(row == 1, middle.astype(jnp.float32), low.astype(jnp.float32)),
    ).astype(jnp.bfloat16)
    out_ref[:, 2 * PAIR :] = jnp.broadcast_to(spare, (out_ref.shape[0], SPARE, HD))


def finish(own, other, scaled_gain, gain_grad, places):
    group = 4
    spec = pl.BlockSpec((2, group, PAIR, HD), lambda i: (0, i, 0, 0))
    row = pl.BlockSpec((1, HD), lambda i: (0, 0))
    rows = 2 * PAIR + SPARE
    return pl.pallas_call(
        finish_kernel,
        grid=(places // group,),
        in_specs=[spec, spec, row, row],
        out_specs=pl.BlockSpec((group, rows, HD), lambda i: (i, 0, 0)),
        out_shape=jax.ShapeDtypeStruct((places, rows, HD), jnp.bfloat16),
        name="finish",
    )(own, other, scaled_gain, gain_grad)


def shards(queries, keys, values, key_gain, random_blocks, out_grad):
    heads = queries.shape[2] // HD
    places = lax.axis_size("seq")
    dp = lax.axis_size("dp")
    core = lax.axis_index("dp") % 2
    cores = core.reshape(1)
    head = lax.axis_index("seq") % heads

    def swap(x, bit=1):
        return lax.ppermute(x, "dp", [(i, i ^ bit) for i in range(dp)])

    def over_seq(x):
        return lax.all_to_all(x, "seq", split_axis=0, concat_axis=0, tiled=True)

    def gather(arrays, spare):
        keep, send = pack(cores, arrays, spare, heads)
        both = lax.dynamic_update_slice(keep, swap(send)[None], (1 - core, 0, 0, 0))
        return both.reshape(places, keep.shape[2], HD)

    def scatter(x, count):
        x = x.reshape(2, heads, x.shape[1], HD)
        came = swap(lax.dynamic_index_in_dim(x, 1 - core, axis=0, keepdims=False))
        return unpack(cores, x, came, count)

    named = random_blocks.reshape(heads, 2, 2, NR).transpose(2, 0, 1, 3).reshape(2, heads, 1, 2 * NR)
    named = jnp.pad(named.astype(jnp.bfloat16), ((0, 0), (0, 0), (0, 0), (0, HD - 2 * NR)))
    gain = lax.dynamic_slice_in_dim(key_gain, head * HD, HD).reshape(1, HD)

    own = over_seq(gather((keys[0], values[0], queries[0]), named))
    grads_in = gather((out_grad[0],), None)
    own, grads_in = lax.optimization_barrier((own, grads_in))
    grads = over_seq(grads_in)
    other = swap(own)
    table = own[:, 3 * PAIR, : 2 * NR].astype(jnp.int32).reshape(2 * places * NR)

    att, weights, dense, keys_scaled = forward(cores, table, gain, own, other, places)
    att_back = over_seq(att)
    dq, part_own, part_other, gain_term = backward(
        cores, table, own, other, keys_scaled, grads, att, weights, dense, places
    )
    att_back, dq = lax.optimization_barrier((att_back, dq))
    dq_back = over_seq(dq)
    part_came = swap(part_other)
    bit = 1
    while bit < dp:
        gain_term = gain_term + swap(gain_term, bit)
        bit *= 2
    dkv = finish(part_own, part_came, gain * SCALE, gain_term[:1], places)
    dq_back, dkv = lax.optimization_barrier((dq_back, dkv))
    dkv_back = over_seq(dkv)
    (attended,) = scatter(att_back, 1)
    (query_grad,) = scatter(dq_back, 1)
    dkv_back, attended, query_grad = lax.optimization_barrier((dkv_back, attended, query_grad))
    key_grad, value_grad = scatter(dkv_back, 2)
    gain_rows = dkv_back[:, 2 * PAIR : 2 * PAIR + 3].astype(jnp.float32)
    gain_grad = jnp.sum(gain_rows.reshape(2, heads, 3, HD), axis=(0, 2)).reshape(heads * HD)
    return (attended[None], query_grad[None], key_grad[None], value_grad[None], gain_grad)


def solution(mesh):
    rows = P("dp", "seq", None)
    return jax.shard_map(
        shards,
        mesh=mesh,
        in_specs=(rows, rows, rows, P(), P(None, "seq", None), rows),
        out_specs=(rows, rows, rows, rows, P()),
        check_vma=False,
    )
```

time: 379 us -> 292 us (0.77)
  blocking collectives: 172 us -> 0 us
  waiting for transfers between devices: 90 us -> 129 us
  starting transfers between devices: 26.1 us -> 56.3 us
  Pallas kernels: 82.9 us -> 92.4 us
  local copies, waits for them, and re-layouts: 3.4 us -> 8.1 us
    all_to_all x8 -> x0, blocking collectives: 172 us -> none  [the longest x4 136 us: over_seq(): return lax.all_to_all(x, 'seq', split_axis=0, concat_axis=0, tiled=True)]
    all_to_all x2 -> x5, waiting for transfers between devices: 86.3 us -> 118 us  [over_seq(): return lax.all_to_all(x, 'seq', split_axis=0, concat_axis=0, tiled=True)]
    all_to_all x2 -> x5, starting transfers between devices: 11.6 us -> 39.9 us  [over_seq(): return lax.all_to_all(x, 'seq', split_axis=0, concat_axis=0, tiled=True)]
    pallas_call x5 -> x7, Pallas kernels: 75.8 us -> 85.7 us  [the longest x1 36.2 us: backward(): pl.pallas_call(functools.partial(backward_kernel, places, unroll), in_spe...]
    ppermute x2 -> x10, starting transfers between devices: 7.38 us -> 16.4 us  [swap(): return lax.ppermute(x, 'dp', [(i, i ^ bit) for i in range(dp)])]
    ppermute x2 -> x10, waiting for transfers between devices: 3.79 us -> 11.8 us  [swap(): return lax.ppermute(x, 'dp', [(i, i ^ bit) for i in range(dp)])]
    all_to_all x1 -> x0, starting transfers between devices: 7.12 us -> none  [between_cores(): lax.all_to_all(x, 'dp', split_axis=0, concat_axis=0, axis_index_groups=pa...]
  transfers between devices with their start and end apart: 5 -> 15, of which waited for: 3 -> 10; matrix products, arithmetic and copies ran while one was open for 1% -> 2% of each run, Pallas kernels for 2% -> 29%
where the time goes in v2:
time: 292 us; the launch traced here: 290 us
  waiting for transfers between devices  129 us (44%)
  Pallas kernels  92.4 us (32%)
  starting transfers between devices  56.3 us (19%)
  local copies, waits for them, and re-layouts  8.1 us (3%)
  other arithmetic  3.38 us (1%)
    all_to_all x5, waiting for transfers between devices, over_seq(): return lax.all_to_all(x, 'seq', split_axis=0, concat_axis=0, tiled=True)  118 us
    all_to_all x5, starting transfers between devices, over_seq(): return lax.all_to_all(x, 'seq', split_axis=0, concat_axis=0, tiled=True)  39.9 us
    pallas_call x1, Pallas kernels, backward(): pl.pallas_call(functools.partial(backward_kernel, places, unroll), in_spe...  36.2 us
    pallas_call x1, Pallas kernels, forward(): pl.pallas_call(functools.partial(forward_kernel, places, unroll), in_spec...  30.9 us
    ppermute x10, starting transfers between devices, swap(): return lax.ppermute(x, 'dp', [(i, i ^ bit) for i in range(dp)])  16.4 us
    ppermute x10, waiting for transfers between devices, swap(): return lax.ppermute(x, 'dp', [(i, i ^ bit) for i in range(dp)])  11.8 us
    pallas_call x3, Pallas kernels, unpack(): pl.pallas_call(functools.partial(unpack_kernel, group), grid_spec=pltpu.P...  10.8 us
    pallas_call x2, Pallas kernels, pack(): pl.pallas_call(functools.partial(pack_kernel, group, count, spare is not...  7.83 us
  transfers between devices with their start and end apart: 15, of which 10 were waited for; matrix products, arithmetic and copies ran while one was open for 2% of the time, Pallas kernels for 29%

profile of v2, /device:TPU:1, one launch (start us, length us, event | category | flops | bytes accessed | tf_op | source)
XLA Modules:
  0.0 290.3 jit_solution(7330824755789409882)
XLA Ops:
  0.6 0.7 convert_element_type.32
  1.3 0.1 copy.15
  1.5 0.6 pad.4.refs_3_
  2.1 4.4 %pack.2 = (bf16[2,16,400,128]{3,2,1,0:T(8,128)(2,1)}, bf16[16,400,128]{2,1,0:T(8,128)(2,1)}) custom-call(s32[1]{0:T(128)} %bitcast.core_ref, bf16[256,2048]{1,0:T(8,128)(2,1)} %bitcast.41, bf16[256,2048]{1,0:T(8,128)(2,1)} %bitcast.42, bf16[256,2048]{1,0:T(8,128)(2,1)} %bitcast.43, bf16[2,16,1,128]{3,2,1,0:T(2,128)(2,1)} %pad.4.refs_3_), custom_call_target="tpu_custom_call" | custom-call | tf_op jit(solution)/shard_map/pack/pallas_call | solution.py:63
  6.5 3.3 %collective-permute-start = (bf16[16,400,128]{2,1,0:T(8,128)(2,1)}, bf16[16,400,128]{2,1,0:T(8,128)(2,1)S(1)}, u32[]{:S(2)}, u32[]{:S(2)}) collective-permute-start(bf16[16,400,128]{2,1,0:T(8,128)(2,1)} %get-tuple-element.29), channel_id=1, source_target_pairs={{0,32},{32,0},{64,96},{96,64},{128,160},{160,128},{192,224},{224,1... | collective-permute-start | bytes 4915208 | tf_op jit(solution)/shard_map/ppermute | solution.py:493
  9.7 3.3 %collective-permute-done = bf16[16,400,128]{2,1,0:T(8,128)(2,1)S(1)} collective-permute-done((bf16[16,400,128]{2,1,0:T(8,128)(2,1)}, bf16[16,400,128]{2,1,0:T(8,128)(2,1)S(1)}, u32[]{:S(2)}, u32[]{:S(2)}) %collective-permute-start) | collective-permute-done | bytes 1638432 | tf_op jit(solution)/shard_map/ppermute | solution.py:493
  13.1 1.3 bitcast_dynamic-update-slice_fusion
  14.4 9.5 %all-to-all-start = ((bf16[32,400,128]{2,1,0:T(8,128)(2,1)}), bf16[32,400,128]{2,1,0:T(8,128)(2,1)S(1)}, u32[]{:S(2)}, u32[]{:S(2)}) async-start(bf16[32,400,128]{2,1,0:T(8,128)(2,1)} %bitcast.40), calls=%async_computation | async-start | bytes 6553600 | tf_op jit(solution)/shard_map/all_to_all | solution.py:496
  23.9 3.4 %pack.3 = (bf16[2,16,128,128]{3,2,1,0:T(8,128)(2,1)}, bf16[16,128,128]{2,1,0:T(8,128)(2,1)}) custom-call(s32[1]{0:T(128)} %bitcast.core_ref, bf16[256,2048]{1,0:T(8,128)(2,1)} %bitcast.44), custom_call_target="tpu_custom_call" | custom-call | tf_op jit(solution)/shard_map/pack/pallas_call | solution.py:63
  27.3 0.6 collective-permute-start.1
  27.9 1.7 collective-permute-done.1
  29.7 0.8 bitcast_dynamic-update-slice_fusion.1
  30.5 67.1 %all-to-all-done.own_ref = bf16[32,400,128]{2,1,0:T(8,128)(2,1)S(1)} async-done(((bf16[32,400,128]{2,1,0:T(8,128)(2,1)}), bf16[32,400,128]{2,1,0:T(8,128)(2,1)S(1)}, u32[]{:S(2)}, u32[]{:S(2)}) %all-to-all-start) | async-done | bytes 3276832 | tf_op jit(solution)/shard_map/all_to_all | solution.py:496
  97.6 0.0 copy-start.3
  97.6 2.2 collective-permute-start.2
  99.8 6.1 %all-to-all-start.2 = ((bf16[32,128,128]{2,1,0:T(8,128)(2,1)}), bf16[32,128,128]{2,1,0:T(8,128)(2,1)}, u32[]{:S(2)}, u32[]{:S(2)}) async-start(bf16[32,128,128]{2,1,0:T(8,128)(2,1)} %bitcast.47), calls=%async_computation.2 | async-start | bytes 2097152 | tf_op jit(solution)/shard_map/all_to_all | solution.py:496
  105.9 1.3 multiply_bitcast_fusion
  107.2 0.1 convert_reduce_fusion.1
  107.3 0.7 reshape.65.table_ref
  107.9 0.0 collective-permute-done.2.other_ref
  107.9 0.0 copy-done.3
  107.9 30.9 %forward.1 = (bf16[32,128,128]{2,1,0:T(8,128)(2,1)}, bf16[64,64,512]{2,1,0:T(8,128)(2,1)}, bf16[16,64,512]{2,1,0:T(8,128)(2,1)}, bf16[2,32,128,128]{3,2,1,0:T(8,128)(2,1)}) custom-call(s32[1]{0:T(128)} %bitcast.core_ref, s32[192]{0:T(256)} %reshape.65.table_ref, f32[1,128]{1,0:T(1,128)} %get-tuple-element.52.gain_ref, bf16[32,400,128]{2,1,0:T(8,128)(2,1)} %copy-done.3, ...), custom_call_target="tpu_custom_call" | custom-call | flops 3221225472 | bytes 62914560 | tf_op jit(solution)/shard_map/forward/pallas_call | solution.py:248
  138.9 0.0 all-to-all-done.2.grad_ref
  138.9 9.2 %all-to-all-start.1 = ((bf16[32,128,128]{2,1,0:T(8,128)(2,1)}), bf16[32,128,128]{2,1,0:T(8,128)(2,1)S(1)}, u32[]{:S(2)}, u32[]{:S(2)}) async-start(bf16[32,128,128]{2,1,0:T(8,128)(2,1)} %get-tuple-element.33.att_ref), calls=%async_computation.1 | async-start | bytes 2097152 | tf_op jit(solution)/shard_map/all_to_all | solution.py:496
  148.0 36.2 %backward.1 = (bf16[32,128,128]{2,1,0:T(8,128)(2,1)}, f32[2,32,128,128]{3,2,1,0:T(8,128)}, bf16[2,32,128,128]{3,2,1,0:T(8,128)(2,1)}, f32[8,128]{1,0:T(8,128)}) custom-call(s32[1]{0:T(128)} %bitcast.core_ref, s32[192]{0:T(256)} %reshape.65.table_ref, bf16[32,400,128]{2,1,0:T(8,128)(2,1)} %copy-done.3, ...), custom_call_target="tpu_custom_call" | custom-call | flops 6442450944 | bytes 104857600 | tf_op jit(solution)/shard_map/backward/pallas_call | solution.py:415
  184.2 0.9 collective-permute-start.3
  185.2 0.0 all-to-all-done.1
  185.2 0.0 copy-start.1
  185.2 9.5 %all-to-all-start.3 = ((bf16[32,128,128]{2,1,0:T(8,128)(2,1)}), bf16[32,128,128]{2,1,0:T(8,128)(2,1)S(1)}, u32[]{:S(2)}, u32[]{:S(2)}) async-start(bf16[32,128,128]{2,1,0:T(8,128)(2,1)} %get-tuple-element.39), calls=%async_computation.3 | async-start | bytes 2097152 | tf_op jit(solution)/shard_map/all_to_all | solution.py:496
  194.7 0.4 collective-permute-start.4
  195.1 1.1 collective-permute-done.4
  196.2 0.7 add.35
  196.8 1.2 collective-permute-start.5
  198.1 1.5 collective-permute-done.5
  199.6 2.7 collective-permute-start.6
  202.3 1.5 collective-permute-done.6
  203.9 0.5 slice.10.gain_grad_ref
  204.4 0.0 collective-permute-done.3.other_ref
  204.4 6.6 %finish.1 = bf16[32,272,128]{2,1,0:T(8,128)(2,1)} custom-call(f32[2,32,128,128]{3,2,1,0:T(8,128)} %get-tuple-element.40.own_ref, bf16[2,32,128,128]{3,2,1,0:T(8,128)(2,1)} %collective-permute-done.3.other_ref, f32[1,128]{1,0:T(1,128)} %get-tuple-element.51.scaled_gain_ref, f32[1,128]{1,0:T(1,128)} %slice.10.gain_grad_ref), custom_call_target="tpu_custom_call" | custom-call | tf_op jit(solution)/shard_map/finish/pallas_call | solution.py:474
  211.0 11.0 %all-to-all-done.3 = bf16[32,128,128]{2,1,0:T(8,128)(2,1)S(1)} async-done(((bf16[32,128,128]{2,1,0:T(8,128)(2,1)}), bf16[32,128,128]{2,1,0:T(8,128)(2,1)S(1)}, u32[]{:S(2)}, u32[]{:S(2)}) %all-to-all-start.3) | async-done | bytes 1048608 | tf_op jit(solution)/shard_map/all_to_all | solution.py:496
  222.0 0.0 copy-start.2
  222.0 1.0 copy-done.2
  223.0 5.7 %all-to-all-start.4 = ((bf16[32,272,128]{2,1,0:T(8,128)(2,1)}), bf16[32,272,128]{2,1,0:T(8,128)(2,1)S(1)}, u32[]{:S(2)}, u32[]{:S(2)}) async-start(bf16[32,272,128]{2,1,0:T(8,128)(2,1)} %finish.1), calls=%async_computation.4 | async-start | bytes 4456448 | tf_op jit(solution)/shard_map/all_to_all | solution.py:496
  228.7 0.0 copy-done.1
  228.7 1.7 collective-permute-start.7
  230.4 1.1 dynamic-slice_bitcast_fusion.1
  231.5 0.1 collective-permute-start.8
  231.6 0.5 collective-permute-done.7.came_ref
  232.1 3.5 %unpack.3 = bf16[256,2048]{1,0:T(8,128)(2,1)} custom-call(s32[1]{0:T(128)} %bitcast.core_ref, bf16[2,16,128,128]{3,2,1,0:T(8,128)(2,1)} %bitcast.37, bf16[16,128,128]{2,1,0:T(8,128)(2,1)} %collective-permute-done.7.came_ref), custom_call_target="tpu_custom_call" | custom-call | tf_op jit(solution)/shard_map/unpack/pallas_call | solution.py:96
  235.5 0.0 collective-permute-done.8.came_ref
  235.5 0.0 copy-start.4
  235.5 0.8 copy-done.4
  236.3 3.5 %unpack.4 = bf16[256,2048]{1,0:T(8,128)(2,1)} custom-call(s32[1]{0:T(128)} %bitcast.core_ref, bf16[2,16,128,128]{3,2,1,0:T(8,128)(2,1)} %bitcast.39, bf16[16,128,128]{2,1,0:T(8,128)(2,1)} %copy-done.4), custom_call_target="tpu_custom_call" | custom-call | tf_op jit(solution)/shard_map/unpack/pallas_call | solution.py:96
  239.8 39.5 %all-to-all-done.4 = bf16[32,272,128]{2,1,0:T(8,128)(2,1)S(1)} async-done(((bf16[32,272,128]{2,1,0:T(8,128)(2,1)}), bf16[32,272,128]{2,1,0:T(8,128)(2,1)S(1)}, u32[]{:S(2)}, u32[]{:S(2)}) %all-to-all-start.4) | async-done | bytes 2228256 | tf_op jit(solution)/shard_map/all_to_all | solution.py:496
  279.3 0.0 copy-start
  279.3 1.1 dynamic-slice_bitcast_fusion
  280.4 3.3 %collective-permute-start.9 = (bf16[16,272,128]{2,1,0:T(8,128)(2,1)}, bf16[16,272,128]{2,1,0:T(8,128)(2,1)}, u32[]{:S(2)}, u32[]{:S(2)}) collective-permute-start(bf16[16,272,128]{2,1,0:T(8,128)(2,1)} %dynamic-slice_bitcast_fusion), channel_id=1, source_target_pairs={{0,32},{32,0},{64,96},{96,64},{128,160},{160,128},{192,224},{224,1... | collective-permute-start | bytes 3342344 | tf_op jit(solution)/shard_map/ppermute | solution.py:493
  283.7 0.6 reduce_sum.18
  284.3 2.1 collective-permute-done.9.came_ref
  286.4 0.0 copy-done
  286.4 3.9 %unpack.5 = (bf16[256,2048]{1,0:T(8,128)(2,1)}, bf16[256,2048]{1,0:T(8,128)(2,1)}) custom-call(s32[1]{0:T(128)} %bitcast.core_ref, bf16[2,16,272,128]{3,2,1,0:T(8,128)(2,1)} %bitcast.35, bf16[16,272,128]{2,1,0:T(8,128)(2,1)} %collective-permute-done.9.came_ref), custom_call_target="tpu_custom_call" | custom-call | tf_op jit(solution)/shard_map/unpack/pallas_call | solution.py:96
  (5 shorter events, 0.1 us)
Async XLA Ops:
  6.5 6.6 %collective-permute-start = (bf16[16,400,128]{2,1,0:T(8,128)(2,1)}, bf16[16,400,128]{2,1,0:T(8,128)(2,1)S(1)}, u32[]{:S(2)}, u32[]{:S(2)}) collective-permute-start(bf16[16,400,128]{2,1,0:T(8,128)(2,1)} %get-tuple-element.29), channel_id=1, source_target_pairs={{0,32},{32,0},{64,96},{96,64},{128,160},{160,128},{192,224},{224,1... | collective-permute-start | bytes 4915208 | tf_op jit(solution)/shard_map/ppermute | solution.py:493
  14.4 83.2 %all-to-all-start = ((bf16[32,400,128]{2,1,0:T(8,128)(2,1)}), bf16[32,400,128]{2,1,0:T(8,128)(2,1)S(1)}, u32[]{:S(2)}, u32[]{:S(2)}) async-start(bf16[32,400,128]{2,1,0:T(8,128)(2,1)} %bitcast.40), calls=%async_computation | async-start | bytes 6553600 | tf_op jit(solution)/shard_map/all_to_all | solution.py:496
  27.3 2.4 collective-permute-start.1
  97.6 10.4 %copy-start.3 = (bf16[32,400,128]{2,1,0:T(8,128)(2,1)}, bf16[32,400,128]{2,1,0:T(8,128)(2,1)S(1)}, u32[]{:S(2)}) copy-start(bf16[32,400,128]{2,1,0:T(8,128)(2,1)S(1)} %all-to-all-done.own_ref) | copy-start | bytes 9830404
  97.6 10.4 %collective-permute-start.2 = (bf16[32,400,128]{2,1,0:T(8,128)(2,1)S(1)}, bf16[32,400,128]{2,1,0:T(8,128)(2,1)}, u32[]{:S(2)}, u32[]{:S(2)}) collective-permute-start(bf16[32,400,128]{2,1,0:T(8,128)(2,1)S(1)} %all-to-all-done.own_ref), channel_id=1, source_target_pairs={{0,32},{32,0},{64,96},{96,64},{128,160},{160,128},{192,224},{224,1... | collective-permute-start | bytes 9830408 | tf_op jit(solution)/shard_map/ppermute | solution.py:493
  99.8 39.1 %all-to-all-start.2 = ((bf16[32,128,128]{2,1,0:T(8,128)(2,1)}), bf16[32,128,128]{2,1,0:T(8,128)(2,1)}, u32[]{:S(2)}, u32[]{:S(2)}) async-start(bf16[32,128,128]{2,1,0:T(8,128)(2,1)} %bitcast.47), calls=%async_computation.2 | async-start | bytes 2097152 | tf_op jit(solution)/shard_map/all_to_all | solution.py:496
  138.9 46.3 %all-to-all-start.1 = ((bf16[32,128,128]{2,1,0:T(8,128)(2,1)}), bf16[32,128,128]{2,1,0:T(8,128)(2,1)S(1)}, u32[]{:S(2)}, u32[]{:S(2)}) async-start(bf16[32,128,128]{2,1,0:T(8,128)(2,1)} %get-tuple-element.33.att_ref), calls=%async_computation.1 | async-start | bytes 2097152 | tf_op jit(solution)/shard_map/all_to_all | solution.py:496
  184.2 20.1 %collective-permute-start.3 = (bf16[2,32,128,128]{3,2,1,0:T(8,128)(2,1)}, bf16[2,32,128,128]{3,2,1,0:T(8,128)(2,1)}, u32[]{:S(2)}, u32[]{:S(2)}) collective-permute-start(bf16[2,32,128,128]{3,2,1,0:T(8,128)(2,1)} %get-tuple-element.41), channel_id=1, source_target_pairs={{0,32},{32,0},{64,96},{96,64},{128,160},{160,128},{192,224},{224,1... | collective-permute-start | bytes 6291464 | tf_op jit(solution)/shard_map/ppermute | solution.py:493
  185.2 43.5 %copy-start.1 = (bf16[32,128,128]{2,1,0:T(8,128)(2,1)}, bf16[32,128,128]{2,1,0:T(8,128)(2,1)S(1)}, u32[]{:S(2)}) copy-start(bf16[32,128,128]{2,1,0:T(8,128)(2,1)S(1)} %all-to-all-done.1) | copy-start | bytes 3145732
  185.2 36.8 %all-to-all-start.3 = ((bf16[32,128,128]{2,1,0:T(8,128)(2,1)}), bf16[32,128,128]{2,1,0:T(8,128)(2,1)S(1)}, u32[]{:S(2)}, u32[]{:S(2)}) async-start(bf16[32,128,128]{2,1,0:T(8,128)(2,1)} %get-tuple-element.39), calls=%async_computation.3 | async-start | bytes 2097152 | tf_op jit(solution)/shard_map/all_to_all | solution.py:496
  194.7 1.5 collective-permute-start.4
  196.8 2.8 collective-permute-start.5
  199.6 4.3 %collective-permute-start.6 = (f32[8,128]{1,0:T(8,128)S(1)}, f32[8,128]{1,0:T(8,128)S(1)}, u32[]{:S(2)}, u32[]{:S(2)}) collective-permute-start(f32[8,128]{1,0:T(8,128)S(1)} %add.36), channel_id=1, source_target_pairs={{0,128},{32,160},{64,192},{96,224},{128,0},{160,32},{192,64},{224,... | collective-permute-start | bytes 12296 | tf_op jit(solution)/shard_map/ppermute | solution.py:493
  222.0 1.0 copy-start.2
  223.0 56.3 %all-to-all-start.4 = ((bf16[32,272,128]{2,1,0:T(8,128)(2,1)}), bf16[32,272,128]{2,1,0:T(8,128)(2,1)S(1)}, u32[]{:S(2)}, u32[]{:S(2)}) async-start(bf16[32,272,128]{2,1,0:T(8,128)(2,1)} %finish.1), calls=%async_computation.4 | async-start | bytes 4456448 | tf_op jit(solution)/shard_map/all_to_all | solution.py:496
  228.7 3.4 %collective-permute-start.7 = (bf16[16,128,128]{2,1,0:T(8,128)(2,1)S(1)}, bf16[16,128,128]{2,1,0:T(8,128)(2,1)}, u32[]{:S(2)}, u32[]{:S(2)}) collective-permute-start(bf16[16,128,128]{2,1,0:T(8,128)(2,1)S(1)} %dynamic-slice_bitcast_fusion.2), channel_id=1, source_target_pairs={{0,32},{32,0},{64,96},{96,64},{128,160},{160,128},{192,224},{224,1... | collective-permute-start | bytes 1572872 | tf_op jit(solution)/shard_map/ppermute | solution.py:493
  231.5 4.1 %collective-permute-start.8 = (bf16[16,128,128]{2,1,0:T(8,128)(2,1)S(1)}, bf16[16,128,128]{2,1,0:T(8,128)(2,1)S(1)}, u32[]{:S(2)}, u32[]{:S(2)}) collective-permute-start(bf16[16,128,128]{2,1,0:T(8,128)(2,1)S(1)} %dynamic-slice_bitcast_fusion.1), channel_id=1, source_target_pairs={{0,32},{32,0},{64,96},{96,64},{128,160},{160,128},{192,224},{224,1... | collective-permute-start | bytes 1572872 | tf_op jit(solution)/shard_map/ppermute | solution.py:493
  235.5 0.8 copy-start.4
  279.3 7.1 %copy-start = (bf16[32,272,128]{2,1,0:T(8,128)(2,1)}, bf16[32,272,128]{2,1,0:T(8,128)(2,1)S(1)}, u32[]{:S(2)}) copy-start(bf16[32,272,128]{2,1,0:T(8,128)(2,1)S(1)} %all-to-all-done.4) | copy-start | bytes 6684676
  280.4 6.0 %collective-permute-start.9 = (bf16[16,272,128]{2,1,0:T(8,128)(2,1)}, bf16[16,272,128]{2,1,0:T(8,128)(2,1)}, u32[]{:S(2)}, u32[]{:S(2)}) collective-permute-start(bf16[16,272,128]{2,1,0:T(8,128)(2,1)} %dynamic-slice_bitcast_fusion), channel_id=1, source_target_pairs={{0,32},{32,0},{64,96},{96,64},{128,160},{160,128},{192,224},{224,1... | collective-permute-start | bytes 3342344 | tf_op jit(solution)/shard_map/ppermute | solution.py:493

commit v3 on v2

--- a/solution.py
+++ b/solution.py
@@ -34,79 +34,101 @@
     return lax.dot_general(a, b, (((0,), (0,)), ((), ())), preferred_element_type=jnp.float32)
 
 
-def pack_kernel(group, count, with_spare, core_ref, *refs):
-    core = core_ref[0]
-    keep_ref, send_ref = refs[-2:]
-    for out_ref, parity in ((keep_ref, core), (send_ref, 1 - core)):
-        for h in range(group):
-            columns = slice(h * HD, (h + 1) * HD)
-            for slot in range(count):
-                for turn in range(2):
-                    row = slot * PAIR + turn * BLOCK
-                    at = pl.multiple_of((2 * turn + parity) * BLOCK, BLOCK)
-                    out_ref[h, row : row + BLOCK] = refs[slot][pl.ds(at, BLOCK), columns]
-            if with_spare:
-                out_ref[h, count * PAIR :] = jnp.broadcast_to(
-                    refs[count][parity, h], (SPARE, HD)
-                )
-
-
-def pack(core, arrays, spare, heads):
+def pack_kernel(group, count, with_spare, parity_ref, *refs):
+    out_ref = refs[-1]
+    for h in range(group):
+        for slot in range(count):
+            for turn in range(2):
+                row = slot * PAIR + turn * BLOCK
+                out_ref[h, row : row + BLOCK] = refs[2 * slot + turn][:, h * HD : (h + 1) * HD]
+        if with_spare:
+            out_ref[h, count * PAIR :] = jnp.broadcast_to(
+                refs[2 * count][parity_ref[0], h], (SPARE, HD)
+            )
+
+
+def pack(parity, arrays, spare, heads, own):
     group = min(heads, 4)
     count = len(arrays)
     rows = count * PAIR + (SPARE if spare is not None else 0)
-    specs = [pl.BlockSpec((4 * BLOCK, group * HD), lambda i, c: (0, i))] * count
-    args = list(arrays)
+    specs = []
+    args = []
+    for array in arrays:
+        for turn in range(2):
+            specs.append(
+                pl.BlockSpec((BLOCK, group * HD), lambda i, p, turn=turn: (2 * turn + p[0], i))
+            )
+            args.append(array)
     if spare is not None:
-        specs.append(pl.BlockSpec((2, group, 1, HD), lambda i, c: (0, i, 0, 0)))
+        specs.append(pl.BlockSpec((2, group, 1, HD), lambda i, p: (0, i, 0, 0)))
         args.append(spare)
+    if own:
+        shape = (2, heads, rows, HD)
+        out_spec = pl.BlockSpec((pl.Squeezed(), group, rows, HD), lambda i, p: (p[0], i, 0, 0))
+    else:
+        shape = (heads, rows, HD)
+        out_spec = pl.BlockSpec((group, rows, HD), lambda i, p: (i, 0, 0))
+    size = 2 * heads * rows * HD
     return pl.pallas_call(
         functools.partial(pack_kernel, group, count, spare is not None),
         grid_spec=pltpu.PrefetchScalarGridSpec(
             num_scalar_prefetch=1,
             grid=(heads // group,),
             in_specs=specs,
-            out_specs=[
-                pl.BlockSpec((pl.Squeezed(), group, rows, HD), lambda i, c: (c[0], i, 0, 0)),
-                pl.BlockSpec((group, rows, HD), lambda i, c: (i, 0, 0)),
-            ],
+            out_specs=out_spec,
         ),
-        out_shape=[
-            jax.ShapeDtypeStruct((2, heads, rows, HD), jnp.bfloat16),
-            jax.ShapeDtypeStruct((heads, rows, HD), jnp.bfloat16),
-        ],
-        name="pack",
-    )(core, *args)
-
-
-def unpack_kernel(group, core_ref, keep_ref, came_ref, *out_refs):
-    core = core_ref[0]
-    for in_ref, parity in ((keep_ref, core), (came_ref, 1 - core)):
-        for h in range(group):
-            for slot, ref in enumerate(out_refs):
-                for turn in range(2):
-                    row = slot * PAIR + turn * BLOCK
-                    at = pl.multiple_of((2 * turn + parity) * BLOCK, BLOCK)
-                    ref[pl.ds(at, BLOCK), h * HD : (h + 1) * HD] = in_ref[h, row : row + BLOCK]
-
-
-def unpack(core, keep, came, count):
-    heads, rows = keep.shape[1:3]
+        out_shape=jax.ShapeDtypeStruct(shape, jnp.bfloat16),
+        cost_estimate=pl.CostEstimate(flops=0, bytes_accessed=2 * size, transcendentals=0),
+        name="pack_own" if own else "pack_sent",
+    )(parity, *args)
+
+
+def unpack_kernel(group, count, place_ref, *refs):
+    out_refs = refs[-count:]
+    for h in range(group):
+        for slot in range(count):
+            out_refs[slot][:, h * HD : (h + 1) * HD] = refs[slot][h]
+
+
+def unpack(place, x, count, filled):
+    heads = x.shape[-3]
     group = min(heads, 4)
+    specs = []
+    for slot in range(count):
+        if filled is None:
+            specs.append(
+                pl.BlockSpec(
+                    (pl.Squeezed(), group, BLOCK, HD),
+                    lambda i, turn, p, slot=slot: (p[0], i, 2 * slot + turn, 0),
+                )
+            )
+        else:
+            specs.append(
+                pl.BlockSpec(
+                    (group, BLOCK, HD), lambda i, turn, p, slot=slot: (i, 2 * slot + turn, 0)
+                )
+            )
+    args = [x] * count
+    aliases = {}
+    if filled is not None:
+        aliases = {1 + count + slot: slot for slot in range(count)}
+        specs += [pl.BlockSpec(memory_space=pl.ANY)] * count
+        args += list(filled)
+    out_spec = pl.BlockSpec((BLOCK, group * HD), lambda i, turn, p: (2 * turn + p[0], i))
+    size = 2 * count * heads * PAIR * HD
     return pl.pallas_call(
-        functools.partial(unpack_kernel, group),
+        functools.partial(unpack_kernel, group, count),
         grid_spec=pltpu.PrefetchScalarGridSpec(
             num_scalar_prefetch=1,
-            grid=(heads // group,),
-            in_specs=[
-                pl.BlockSpec((pl.Squeezed(), group, rows, HD), lambda i, c: (c[0], i, 0, 0)),
-                pl.BlockSpec((group, rows, HD), lambda i, c: (i, 0, 0)),
-            ],
-            out_specs=[pl.BlockSpec((4 * BLOCK, group * HD), lambda i, c: (0, i))] * count,
+            grid=(heads // group, 2),
+            in_specs=specs,
+            out_specs=[out_spec] * count,
         ),
-        out_shape=[jax.ShapeDtypeStruct((4 * BLOCK, heads * HD), keep.dtype)] * count,
-        name="unpack",
-    )(core, keep, came)
+        out_shape=[jax.ShapeDtypeStruct((4 * BLOCK, heads * HD), x.dtype)] * count,
+        input_output_aliases=aliases,
+        cost_estimate=pl.CostEstimate(flops=0, bytes_accessed=2 * size, transcendentals=0),
+        name="unpack_own" if filled is None else "unpack_sent",
+    )(place, *args)
 
 
 def locate(block):
@@ -144,8 +166,11 @@
     v_scr,
     q_scr,
     score_scr,
+    weight_scr,
+    dense_scr,
     in_sem,
     out_sem,
+    weight_sem,
 ):
     core = core_ref[0]
     total_blocks = 4 * places
@@ -184,10 +209,10 @@
         return jnp.maximum(top, lanes(scores, jnp.maximum))
 
     top = lax.fori_loop(
-        0, 2 * steps, dense_scores, jnp.full((BLOCK, HD), NEGATIVE, jnp.float32)
+        0, 2 * steps, dense_scores, jnp.full((BLOCK, HD), NEGATIVE, jnp.float32), unroll=4
     )
     top = jnp.max(top, axis=1, keepdims=True)
-    key_copy = pltpu.make_async_copy(k_scr, key_out, out_sem)
+    key_copy = pltpu.make_async_copy(k_scr, key_out, out_sem.at[0])
     key_copy.start()
     for copy in copies[3:]:
         copy.wait()
@@ -200,16 +225,18 @@
         return total + lanes(expo, jnp.add), numer
 
     zero = jnp.zeros((BLOCK, HD), jnp.float32)
-    total, numer = lax.fori_loop(0, 2 * steps, dense_expo, (zero, zero))
+    total, numer = lax.fori_loop(0, 2 * steps, dense_expo, (zero, zero), unroll=4)
     inverse = 1.0 / jnp.sum(total, axis=1, keepdims=True)
     att_ref[0, :BLOCK] = (numer * inverse).astype(jnp.bfloat16)
 
     def dense_weights(t, carry):
-        dense_ref[t] = (score_scr[t] * inverse).astype(jnp.bfloat16)
+        dense_scr[t] = (score_scr[t] * inverse).astype(jnp.bfloat16)
         return carry
 
-    lax.fori_loop(0, 2 * steps, dense_weights, 0)
-
+    lax.fori_loop(0, 2 * steps, dense_weights, 0, unroll=4)
+
+    dense_copy = pltpu.make_async_copy(dense_scr, dense_ref, out_sem.at[1])
+    dense_copy.start()
     column = lax.broadcasted_iota(jnp.int32, (1, NK * BLOCK), 1) // BLOCK
 
     def sparse_block(n):
@@ -231,15 +258,24 @@
         done = [sparse_block(first + u) for u in range(unroll)]
         for u, (mine, attended, weights) in enumerate(done):
             att_ref[mine] = attended
-            weight_ref[first + u] = weights
+            weight_scr[first + u] = weights
+        weight_copy(t).start()
         return carry
 
-    lax.fori_loop(0, (2 * places - 1) // unroll, sparse_step, 0)
+    def weight_copy(t):
+        part = pl.ds(1 + t * unroll, unroll)
+        return pltpu.make_async_copy(weight_scr.at[part], weight_ref.at[part], weight_sem.at[t])
+
+    rounds = (2 * places - 1) // unroll
+    lax.fori_loop(0, rounds, sparse_step, 0)
     key_copy.wait()
+    dense_copy.wait()
+    for t in range(rounds):
+        weight_copy(t).wait()
 
 
 def forward(core, table, gain, own, other, places):
-    unroll = 3 if (2 * places - 1) % 3 == 0 else 1
+    unroll = 9 if (2 * places - 1) % 9 == 0 else 1
     both = (2, places, PAIR, HD)
     smem = pl.BlockSpec(memory_space=pltpu.SMEM)
     vmem = pl.BlockSpec(memory_space=pltpu.VMEM)
@@ -248,7 +284,7 @@
     return pl.pallas_call(
         functools.partial(forward_kernel, places, unroll),
         in_specs=[smem, smem, vmem, hbm, hbm],
-        out_specs=[vmem, vmem, vmem, hbm],
+        out_specs=[vmem, hbm, hbm, hbm],
         out_shape=[
             jax.ShapeDtypeStruct((places, PAIR, HD), jnp.bfloat16),
             jax.ShapeDtypeStruct((blocks, BLOCK, NK * BLOCK), jnp.bfloat16),
@@ -260,8 +296,11 @@
             pltpu.VMEM(both, jnp.bfloat16),
             pltpu.VMEM((places, PAIR, HD), jnp.bfloat16),
             pltpu.VMEM((places // 2, BLOCK, WIDTH), jnp.float32),
+            pltpu.VMEM((blocks, BLOCK, NK * BLOCK), jnp.bfloat16),
+            pltpu.VMEM((places // 2, BLOCK, WIDTH), jnp.bfloat16),
             pltpu.SemaphoreType.DMA((5,)),
-            pltpu.SemaphoreType.DMA,
+            pltpu.SemaphoreType.DMA((2,)),
+            pltpu.SemaphoreType.DMA(((blocks - 1) // unroll,)),
         ],
         compiler_params=pltpu.CompilerParams(vmem_limit_bytes=VMEM_LIMIT),
         cost_estimate=pl.CostEstimate(
@@ -271,6 +310,17 @@
         ),
         name="forward",
     )(core, table, gain, own, other)
+
+
+def diagonal(query, grad):
+    zero = jnp.zeros_like(query)
+    return jnp.concatenate(
+        [jnp.concatenate([query, zero], axis=1), jnp.concatenate([zero, grad], axis=1)], axis=0
+    )
+
+
+def joint_terms(dscores, weights, operand):
+    return tn(jnp.concatenate([dscores, weights], axis=0), operand)
 
 
 def backward_kernel(
@@ -339,20 +389,22 @@
     query = q_scr[0, :BLOCK]
     grad = g_scr[0, :BLOCK]
     delta = row_delta(grad, a_scr[0, :BLOCK])
+    operand = diagonal(query, grad)
 
     def dense_back(t, dquery):
         weights = dense_scr[t]
         dprobs = nt(grad, chunk_rows(v_scr, t, steps))
         dscores = (weights.astype(jnp.float32) * (dprobs - delta)).astype(jnp.bfloat16)
         where = (t // steps, pl.ds((t % steps) * CHUNK, CHUNK))
-        acc_k[where] = tn(dscores, query).reshape(CHUNK, PAIR, HD)
-        acc_v[where] = tn(weights, grad).reshape(CHUNK, PAIR, HD)
+        both = joint_terms(dscores, weights, operand)
+        acc_k[where] = both[:, :HD].reshape(CHUNK, PAIR, HD)
+        acc_v[where] = both[:, HD:].reshape(CHUNK, PAIR, HD)
         return dquery + nn(dscores, chunk_rows(k_scr, t, steps))
 
-    dquery = lax.fori_loop(0, 2 * steps, dense_back, jnp.zeros((BLOCK, HD), jnp.float32))
+    zero = jnp.zeros((BLOCK, HD), jnp.float32)
+    dquery = lax.fori_loop(0, 2 * steps, dense_back, zero, unroll=4)
     dq_ref[0, :BLOCK] = (dquery * SCALE).astype(jnp.bfloat16)
-    for copy in copies[7:]:
-        copy.wait()
+    copies[7].wait()
 
     def sparse_block(n):
         block = 2 * n + core
@@ -366,20 +418,20 @@
         dprobs = nt(grad, value_list)
         dscores = (weights.astype(jnp.float32) * (dprobs - delta)).astype(jnp.bfloat16)
         dquery = nn(dscores, key_list)
-        dkey = tn(dscores, q_scr[mine])
-        dvalue = tn(weights, grad)
-        return listing, mine, dquery, dkey, dvalue
+        return listing, mine, dquery, joint_terms(dscores, weights, diagonal(q_scr[mine], grad))
 
     def sparse_step(t, carry):
         done = [sparse_block(1 + t * unroll + u) for u in range(unroll)]
-        for listing, mine, dquery, dkey, dvalue in done:
+        for listing, mine, dquery, terms in done:
             dq_ref[mine] = (dquery * SCALE).astype(jnp.bfloat16)
             for slot, where in enumerate(listing):
-                acc_k[where] += dkey[slot * BLOCK : (slot + 1) * BLOCK]
-                acc_v[where] += dvalue[slot * BLOCK : (slot + 1) * BLOCK]
+                acc_k[where] += terms[slot * BLOCK : (slot + 1) * BLOCK, :HD]
+                acc_v[where] += terms[slot * BLOCK : (slot + 1) * BLOCK, HD:]
         return carry
 
     lax.fori_loop(0, (2 * places - 1) // unroll, sparse_step, 0)
+    for copy in copies[8:]:
+        copy.wait()
 
     copies = [
         pltpu.make_async_copy(acc_k.at[core], own_out.at[0], out_sem.at[0]),
@@ -397,7 +449,7 @@
         other_out[1, where] = acc_v[1 - core, where].astype(jnp.bfloat16)
         return carry + jnp.sum((mine + theirs).reshape(CHUNK * PAIR // 8, 8, HD), axis=0)
 
-    gain_term = lax.fori_loop(0, steps, round_other, jnp.zeros((8, HD), jnp.float32))
+    gain_term = lax.fori_loop(0, steps, round_other, jnp.zeros((8, HD), jnp.float32), unroll=2)
     gain_term = jnp.sum(gain_term, axis=0, keepdims=True) * SCALE
     gain_out[...] = jnp.broadcast_to(gain_term, (8, HD))
     for copy in copies:
@@ -405,7 +457,7 @@
 
 
 def backward(core, table, own, other, keys, grads, att, weights, dense, places):
-    unroll = 3 if (2 * places - 1) % 3 == 0 else 1
+    unroll = 9 if (2 * places - 1) % 9 == 0 else 1
     both = (2, places, PAIR, HD)
     half = (places, PAIR, HD)
     blocks = 2 * places
@@ -496,14 +548,15 @@
         return lax.all_to_all(x, "seq", split_axis=0, concat_axis=0, tiled=True)
 
     def gather(arrays, spare):
-        keep, send = pack(cores, arrays, spare, heads)
-        both = lax.dynamic_update_slice(keep, swap(send)[None], (1 - core, 0, 0, 0))
-        return both.reshape(places, keep.shape[2], HD)
+        came = swap(pack(1 - cores, arrays, spare, heads, False))
+        both = pack(cores, arrays, spare, heads, True)
+        both = lax.dynamic_update_slice(both, came[None], (1 - core, 0, 0, 0))
+        return both.reshape(places, both.shape[2], HD)
 
     def scatter(x, count):
         x = x.reshape(2, heads, x.shape[1], HD)
         came = swap(lax.dynamic_index_in_dim(x, 1 - core, axis=0, keepdims=False))
-        return unpack(cores, x, came, count)
+        return unpack(1 - cores, came, count, unpack(cores, x, count, None))
 
     named = random_blocks.reshape(heads, 2, 2, NR).transpose(2, 0, 1, 3).reshape(2, heads, 1, 2 * NR)
     named = jnp.pad(named.astype(jnp.bfloat16), ((0, 0), (0, 0), (0, 0), (0, HD - 2 * NR)))

time: 292 us -> 282 us (0.966)
  waiting for transfers between devices: 129 us -> 109 us
  Pallas kernels: 92.4 us -> 101 us
    pallas_call x3 -> x6, Pallas kernels: 10.8 us -> 29.3 us  [unpack(): pl.pallas_call(functools.partial(unpack_kernel, group, count), grid_spec=...]
    all_to_all x5, waiting for transfers between devices: 118 us -> 105 us  [over_seq(): return lax.all_to_all(x, 'seq', split_axis=0, concat_axis=0, tiled=True)]
    pallas_call x1, Pallas kernels: 36.2 us -> 27 us  [backward(): pl.pallas_call(functools.partial(backward_kernel, places, unroll), in_spe...]
    ppermute x10, waiting for transfers between devices: 11.8 us -> 4.12 us  [swap(): return lax.ppermute(x, 'dp', [(i, i ^ bit) for i in range(dp)])]
    pallas_call x1, Pallas kernels: 30.9 us -> 24 us  [forward(): pl.pallas_call(functools.partial(forward_kernel, places, unroll), in_spec...]
    pallas_call x2 -> x4, Pallas kernels: 7.83 us -> 13.6 us  [pack(): pl.pallas_call(functools.partial(pack_kernel, group, count, spare is not...]
  transfers between devices with their start and end apart: 15 -> 15, of which waited for: 10 -> 7; matrix products, arithmetic and copies ran while one was open for 2% -> 3% of each run, Pallas kernels for 29% -> 33%
where the time goes in v3:
time: 282 us; the launch traced here: 279 us
  waiting for transfers between devices  109 us (39%)
  Pallas kernels  101 us (36%)
  starting transfers between devices  54.7 us (19%)
  local copies, waits for them, and re-layouts  9.93 us (4%)
  other arithmetic  4.22 us (1%)
    all_to_all x5, waiting for transfers between devices, over_seq(): return lax.all_to_all(x, 'seq', split_axis=0, concat_axis=0, tiled=True)  105 us
    all_to_all x5, starting transfers between devices, over_seq(): return lax.all_to_all(x, 'seq', split_axis=0, concat_axis=0, tiled=True)  39.2 us
    pallas_call x6, Pallas kernels, unpack(): pl.pallas_call(functools.partial(unpack_kernel, group, count), grid_spec=...  29.3 us
    pallas_call x1, Pallas kernels, backward(): pl.pallas_call(functools.partial(backward_kernel, places, unroll), in_spe...  27 us
    pallas_call x1, Pallas kernels, forward(): pl.pallas_call(functools.partial(forward_kernel, places, unroll), in_spec...  24 us
    ppermute x10, starting transfers between devices, swap(): return lax.ppermute(x, 'dp', [(i, i ^ bit) for i in range(dp)])  15.5 us
    pallas_call x4, Pallas kernels, pack(): pl.pallas_call(functools.partial(pack_kernel, group, count, spare is not...  13.6 us
    pallas_call x1, Pallas kernels, finish(): pl.pallas_call(finish_kernel, grid=(places // group,), in_specs=[spec, sp...  6.62 us
  transfers between devices with their start and end apart: 15, of which 7 were waited for; matrix products, arithmetic and copies ran while one was open for 3% of the time, Pallas kernels for 33%

profile of v3, /device:TPU:1, one launch (start us, length us, event | category | flops | bytes accessed | tf_op | source)
XLA Modules:
  0.0 278.9 jit_solution(8434895584952899517)
XLA Ops:
  0.6 0.7 convert_element_type.32
  1.3 0.1 copy.19
  1.5 0.6 pad.4.refs_6_
  2.1 3.7 %pack_sent.2 = bf16[16,400,128]{2,1,0:T(8,128)(2,1)} custom-call(s32[1]{0:T(128)S(6)} %sub.4.parity_ref.place_ref, bf16[256,2048]{1,0:T(8,128)(2,1)} %bitcast.37, bf16[256,2048]{1,0:T(8,128)(2,1)} %bitcast.38, bf16[256,2048]{1,0:T(8,128)(2,1)} %bitcast.41, bf16[256,2048]{1,0:T(8,128)(2,1)} %bitcast.42, bf16[256,2048]{1,0:T(8,128)(2,1)} %bitcast.45, ...), custom_call_target="tpu_custom_call" | custom-call | bytes 3276800 | tf_op jit(solution)/shard_map/pack_sent/pallas_call | solution.py:72
  5.8 3.2 %collective-permute-start = (bf16[16,400,128]{2,1,0:T(8,128)(2,1)}, bf16[16,400,128]{2,1,0:T(8,128)(2,1)S(1)}, u32[]{:S(2)}, u32[]{:S(2)}) collective-permute-start(bf16[16,400,128]{2,1,0:T(8,128)(2,1)} %pack_sent.2), channel_id=1, source_target_pairs={{0,32},{32,0},{64,96},{96,64},{128,160},{160,128},{192,224},{224,1... | collective-permute-start | bytes 4915208 | tf_op jit(solution)/shard_map/ppermute | solution.py:545
  9.0 3.7 %pack_own.2 = bf16[2,16,400,128]{3,2,1,0:T(8,128)(2,1)} custom-call(s32[1]{0:T(128)} %bitcast.parity_ref.core_ref.place_ref, bf16[256,2048]{1,0:T(8,128)(2,1)} %bitcast.39, bf16[256,2048]{1,0:T(8,128)(2,1)} %bitcast.40, bf16[256,2048]{1,0:T(8,128)(2,1)} %bitcast.43, bf16[256,2048]{1,0:T(8,128)(2,1)} %bitcast.44, bf16[256,2048]{1,0:T(8,128)(2,1)} %bitcast.47, ...), custom_call_target="tpu_custom_call" | custom-call | bytes 3276800 | tf_op jit(solution)/shard_map/pack_own/pallas_call | solution.py:72
  12.7 0.0 collective-permute-done
  12.7 1.3 bitcast_dynamic-update-slice_fusion
  14.0 9.5 %all-to-all-start = ((bf16[32,400,128]{2,1,0:T(8,128)(2,1)}), bf16[32,400,128]{2,1,0:T(8,128)(2,1)S(1)}, u32[]{:S(2)}, u32[]{:S(2)}) async-start(bf16[32,400,128]{2,1,0:T(8,128)(2,1)} %bitcast.53), calls=%async_computation | async-start | bytes 6553600 | tf_op jit(solution)/shard_map/all_to_all | solution.py:548
  23.5 3.1 %pack_sent.3 = bf16[16,128,128]{2,1,0:T(8,128)(2,1)} custom-call(s32[1]{0:T(128)S(6)} %sub.4.parity_ref.place_ref, bf16[256,2048]{1,0:T(8,128)(2,1)} %bitcast.49, bf16[256,2048]{1,0:T(8,128)(2,1)} %bitcast.50), custom_call_target="tpu_custom_call" | custom-call | bytes 1048576 | tf_op jit(solution)/shard_map/pack_sent/pallas_call | solution.py:72
  26.6 0.3 collective-permute-start.1
  26.9 3.1 %pack_own.3 = bf16[2,16,128,128]{3,2,1,0:T(8,128)(2,1)} custom-call(s32[1]{0:T(128)} %bitcast.parity_ref.core_ref.place_ref, bf16[256,2048]{1,0:T(8,128)(2,1)} %bitcast.51, bf16[256,2048]{1,0:T(8,128)(2,1)} %bitcast.52), custom_call_target="tpu_custom_call" | custom-call | bytes 1048576 | tf_op jit(solution)/shard_map/pack_own/pallas_call | solution.py:72
  30.0 0.0 collective-permute-done.1
  30.0 1.9 bitcast_dynamic-update-slice_fusion.1
  31.9 65.4 %all-to-all-done.own_ref = bf16[32,400,128]{2,1,0:T(8,128)(2,1)S(1)} async-done(((bf16[32,400,128]{2,1,0:T(8,128)(2,1)}), bf16[32,400,128]{2,1,0:T(8,128)(2,1)S(1)}, u32[]{:S(2)}, u32[]{:S(2)}) %all-to-all-start) | async-done | bytes 3276832 | tf_op jit(solution)/shard_map/all_to_all | solution.py:548
  97.3 0.0 copy-start.3
  97.3 1.7 collective-permute-start.2
  99.0 6.4 %all-to-all-start.2 = ((bf16[32,128,128]{2,1,0:T(8,128)(2,1)}), bf16[32,128,128]{2,1,0:T(8,128)(2,1)}, u32[]{:S(2)}, u32[]{:S(2)}) async-start(bf16[32,128,128]{2,1,0:T(8,128)(2,1)} %bitcast.60), calls=%async_computation.2 | async-start | bytes 2097152 | tf_op jit(solution)/shard_map/all_to_all | solution.py:548
  105.5 1.3 multiply_bitcast_fusion
  106.8 0.1 convert_reduce_fusion.1
  106.8 0.7 reshape.65.table_ref
  107.5 0.0 collective-permute-done.2.other_ref
  107.5 0.0 copy-done.3
  107.5 24.0 %forward.1 = (bf16[32,128,128]{2,1,0:T(8,128)(2,1)}, bf16[64,64,512]{2,1,0:T(8,128)(2,1)}, bf16[16,64,512]{2,1,0:T(8,128)(2,1)}, bf16[2,32,128,128]{3,2,1,0:T(8,128)(2,1)}) custom-call(s32[1]{0:T(128)} %bitcast.parity_ref.core_ref.place_ref, s32[192]{0:T(256)} %reshape.65.table_ref, f32[1,128]{1,0:T(1,128)} %get-tuple-element.48.gain_ref, ...), custom_call_target="tpu_custom_call" | custom-call | flops 3221225472 | bytes 62914560 | tf_op jit(solution)/shard_map/forward/pallas_call | solution.py:284
  131.5 1.2 all-to-all-done.2.grad_ref
  132.7 8.0 %all-to-all-start.1 = ((bf16[32,128,128]{2,1,0:T(8,128)(2,1)}), bf16[32,128,128]{2,1,0:T(8,128)(2,1)S(1)}, u32[]{:S(2)}, u32[]{:S(2)}) async-start(bf16[32,128,128]{2,1,0:T(8,128)(2,1)} %get-tuple-element.27.att_ref), calls=%async_computation.1 | async-start | bytes 2097152 | tf_op jit(solution)/shard_map/all_to_all | solution.py:548
  140.7 27.0 %backward.1 = (bf16[32,128,128]{2,1,0:T(8,128)(2,1)}, f32[2,32,128,128]{3,2,1,0:T(8,128)}, bf16[2,32,128,128]{3,2,1,0:T(8,128)(2,1)}, f32[8,128]{1,0:T(8,128)}) custom-call(s32[1]{0:T(128)} %bitcast.parity_ref.core_ref.place_ref, s32[192]{0:T(256)} %reshape.65.table_ref, bf16[32,400,128]{2,1,0:T(8,128)(2,1)} %copy-done.3, ...), custom_call_target="tpu_custom_call" | custom-call | flops 6442450944 | bytes 104857600 | tf_op jit(solution)/shard_map/backward/pallas_call | solution.py:467
  167.7 0.9 collective-permute-start.3
  168.6 0.0 all-to-all-done.1
  168.6 9.5 %all-to-all-start.3 = ((bf16[32,128,128]{2,1,0:T(8,128)(2,1)}), bf16[32,128,128]{2,1,0:T(8,128)(2,1)S(1)}, u32[]{:S(2)}, u32[]{:S(2)}) async-start(bf16[32,128,128]{2,1,0:T(8,128)(2,1)} %get-tuple-element.33), calls=%async_computation.3 | async-start | bytes 2097152 | tf_op jit(solution)/shard_map/all_to_all | solution.py:548
  178.1 0.4 collective-permute-start.4
  178.6 1.1 collective-permute-done.4
  179.6 0.7 add.35
  180.3 1.2 collective-permute-start.5
  181.5 1.5 collective-permute-done.5
  183.1 2.7 collective-permute-start.6
  185.8 1.5 collective-permute-done.6
  187.3 0.5 slice.10.gain_grad_ref
  187.8 0.0 collective-permute-done.3.other_ref
  187.8 6.6 %finish.1 = bf16[32,272,128]{2,1,0:T(8,128)(2,1)} custom-call(f32[2,32,128,128]{3,2,1,0:T(8,128)} %get-tuple-element.34.own_ref, bf16[2,32,128,128]{3,2,1,0:T(8,128)(2,1)} %collective-permute-done.3.other_ref, f32[1,128]{1,0:T(1,128)} %get-tuple-element.47.scaled_gain_ref, f32[1,128]{1,0:T(1,128)} %slice.10.gain_grad_ref), custom_call_target="tpu_custom_call" | custom-call | tf_op jit(solution)/shard_map/finish/pallas_call | solution.py:526
  194.5 11.0 %all-to-all-done.3 = bf16[32,128,128]{2,1,0:T(8,128)(2,1)S(1)} async-done(((bf16[32,128,128]{2,1,0:T(8,128)(2,1)}), bf16[32,128,128]{2,1,0:T(8,128)(2,1)S(1)}, u32[]{:S(2)}, u32[]{:S(2)}) %all-to-all-start.3) | async-done | bytes 1048608 | tf_op jit(solution)/shard_map/all_to_all | solution.py:548
  205.4 1.0 copy-done.2
  206.4 5.9 %all-to-all-start.4 = ((bf16[32,272,128]{2,1,0:T(8,128)(2,1)}), bf16[32,272,128]{2,1,0:T(8,128)(2,1)S(1)}, u32[]{:S(2)}, u32[]{:S(2)}) async-start(bf16[32,272,128]{2,1,0:T(8,128)(2,1)} %finish.1), calls=%async_computation.4 | async-start | bytes 4456448 | tf_op jit(solution)/shard_map/all_to_all | solution.py:548
  212.3 0.0 copy-done.1
  212.3 0.8 dynamic-slice_bitcast_fusion.2
  213.1 1.6 collective-permute-start.7
  214.7 1.1 dynamic-slice_bitcast_fusion.1
  215.8 0.1 collective-permute-start.8
  215.9 4.8 %unpack_own.3.refs_1_ = bf16[256,2048]{1,0:T(8,128)(2,1)} custom-call(s32[1]{0:T(128)} %bitcast.parity_ref.core_ref.place_ref, bf16[2,16,128,128]{3,2,1,0:T(8,128)(2,1)} %bitcast.55), custom_call_target="tpu_custom_call" | custom-call | bytes 1048576 | tf_op jit(solution)/shard_map/unpack_own/pallas_call | solution.py:119
  220.7 0.0 collective-permute-done.7.refs_0_
  220.7 4.8 %unpack_sent.3 = bf16[256,2048]{1,0:T(8,128)(2,1)} custom-call(s32[1]{0:T(128)S(6)} %sub.4.parity_ref.place_ref, bf16[16,128,128]{2,1,0:T(8,128)(2,1)} %collective-permute-done.7.refs_0_, bf16[256,2048]{1,0:T(8,128)(2,1)} %unpack_own.3.refs_1_), custom_call_target="tpu_custom_call", output_to_operand_aliasing={{}: (2, {})} | custom-call | bytes 1048576 | tf_op jit(solution)/shard_map/unpack_sent/pallas_call | solution.py:119
  225.5 4.8 %unpack_own.4.refs_1_ = bf16[256,2048]{1,0:T(8,128)(2,1)} custom-call(s32[1]{0:T(128)} %bitcast.parity_ref.core_ref.place_ref, bf16[2,16,128,128]{3,2,1,0:T(8,128)(2,1)} %bitcast.57), custom_call_target="tpu_custom_call" | custom-call | bytes 1048576 | tf_op jit(solution)/shard_map/unpack_own/pallas_call | solution.py:119
  230.3 0.0 collective-permute-done.8.refs_0_
  230.3 0.8 copy-done.4
  231.1 4.8 %unpack_sent.4 = bf16[256,2048]{1,0:T(8,128)(2,1)} custom-call(s32[1]{0:T(128)S(6)} %sub.4.parity_ref.place_ref, bf16[16,128,128]{2,1,0:T(8,128)(2,1)} %copy-done.4, bf16[256,2048]{1,0:T(8,128)(2,1)} %unpack_own.4.refs_1_), custom_call_target="tpu_custom_call", output_to_operand_aliasing={{}: (2, {})} | custom-call | bytes 1048576 | tf_op jit(solution)/shard_map/unpack_sent/pallas_call | solution.py:119
  235.9 27.0 %all-to-all-done.4 = bf16[32,272,128]{2,1,0:T(8,128)(2,1)S(1)} async-done(((bf16[32,272,128]{2,1,0:T(8,128)(2,1)}), bf16[32,272,128]{2,1,0:T(8,128)(2,1)S(1)}, u32[]{:S(2)}, u32[]{:S(2)}) %all-to-all-start.4) | async-done | bytes 2228256 | tf_op jit(solution)/shard_map/all_to_all | solution.py:548
  262.9 1.1 dynamic-slice_bitcast_fusion
  264.1 3.3 %collective-permute-start.9 = (bf16[16,272,128]{2,1,0:T(8,128)(2,1)}, bf16[16,272,128]{2,1,0:T(8,128)(2,1)}, u32[]{:S(2)}, u32[]{:S(2)}) collective-permute-start(bf16[16,272,128]{2,1,0:T(8,128)(2,1)} %dynamic-slice_bitcast_fusion), channel_id=1, source_target_pairs={{0,32},{32,0},{64,96},{96,64},{128,160},{160,128},{192,224},{224,1... | collective-permute-start | bytes 3342344 | tf_op jit(solution)/shard_map/ppermute | solution.py:545
  267.3 0.0 copy-done
  267.3 5.1 %unpack_own.5 = (bf16[256,2048]{1,0:T(8,128)(2,1)}, bf16[256,2048]{1,0:T(8,128)(2,1)}) custom-call(s32[1]{0:T(128)} %bitcast.parity_ref.core_ref.place_ref, bf16[2,16,272,128]{3,2,1,0:T(8,128)(2,1)} %bitcast.35, bf16[2,16,272,128]{3,2,1,0:T(8,128)(2,1)} %bitcast.36), custom_call_target="tpu_custom_call" | custom-call | bytes 2097152 | tf_op jit(solution)/shard_map/unpack_own/pallas_call | solution.py:119
  272.4 0.9 convert_reduce_fusion
  273.3 0.6 reduce_sum.18
  273.9 0.0 collective-permute-done.9.refs_0_.refs_1_
  273.9 5.1 %unpack_sent.5 = (bf16[256,2048]{1,0:T(8,128)(2,1)}, bf16[256,2048]{1,0:T(8,128)(2,1)}) custom-call(s32[1]{0:T(128)S(6)} %sub.4.parity_ref.place_ref, bf16[16,272,128]{2,1,0:T(8,128)(2,1)} %collective-permute-done.9.refs_0_.refs_1_, bf16[16,272,128]{2,1,0:T(8,128)(2,1)} %collective-permute-done.9.refs_0_.refs_1_, ...), custom_call_target="tpu_custom_call", output_to_operand_aliasing={{0}: (3, {}), {1}: (4, {})} | custom-call | bytes 2097152 | tf_op jit(solution)/shard_map/unpack_sent/pallas_call | solution.py:119
  (7 shorter events, 0.0 us)
Async XLA Ops:
  5.8 6.9 %collective-permute-start = (bf16[16,400,128]{2,1,0:T(8,128)(2,1)}, bf16[16,400,128]{2,1,0:T(8,128)(2,1)S(1)}, u32[]{:S(2)}, u32[]{:S(2)}) collective-permute-start(bf16[16,400,128]{2,1,0:T(8,128)(2,1)} %pack_sent.2), channel_id=1, source_target_pairs={{0,32},{32,0},{64,96},{96,64},{128,160},{160,128},{192,224},{224,1... | collective-permute-start | bytes 4915208 | tf_op jit(solution)/shard_map/ppermute | solution.py:545
  14.0 83.3 %all-to-all-start = ((bf16[32,400,128]{2,1,0:T(8,128)(2,1)}), bf16[32,400,128]{2,1,0:T(8,128)(2,1)S(1)}, u32[]{:S(2)}, u32[]{:S(2)}) async-start(bf16[32,400,128]{2,1,0:T(8,128)(2,1)} %bitcast.53), calls=%async_computation | async-start | bytes 6553600 | tf_op jit(solution)/shard_map/all_to_all | solution.py:548
  26.6 3.4 %collective-permute-start.1 = (bf16[16,128,128]{2,1,0:T(8,128)(2,1)}, bf16[16,128,128]{2,1,0:T(8,128)(2,1)}, u32[]{:S(2)}, u32[]{:S(2)}) collective-permute-start(bf16[16,128,128]{2,1,0:T(8,128)(2,1)} %pack_sent.3), channel_id=1, source_target_pairs={{0,32},{32,0},{64,96},{96,64},{128,160},{160,128},{192,224},{224,1... | collective-permute-start | bytes 1572872 | tf_op jit(solution)/shard_map/ppermute | solution.py:545
  97.3 10.2 %copy-start.3 = (bf16[32,400,128]{2,1,0:T(8,128)(2,1)}, bf16[32,400,128]{2,1,0:T(8,128)(2,1)S(1)}, u32[]{:S(2)}) copy-start(bf16[32,400,128]{2,1,0:T(8,128)(2,1)S(1)} %all-to-all-done.own_ref) | copy-start | bytes 9830404
  97.3 10.2 %collective-permute-start.2 = (bf16[32,400,128]{2,1,0:T(8,128)(2,1)S(1)}, bf16[32,400,128]{2,1,0:T(8,128)(2,1)}, u32[]{:S(2)}, u32[]{:S(2)}) collective-permute-start(bf16[32,400,128]{2,1,0:T(8,128)(2,1)S(1)} %all-to-all-done.own_ref), channel_id=1, source_target_pairs={{0,32},{32,0},{64,96},{96,64},{128,160},{160,128},{192,224},{224,1... | collective-permute-start | bytes 9830408 | tf_op jit(solution)/shard_map/ppermute | solution.py:545
  99.0 33.7 %all-to-all-start.2 = ((bf16[32,128,128]{2,1,0:T(8,128)(2,1)}), bf16[32,128,128]{2,1,0:T(8,128)(2,1)}, u32[]{:S(2)}, u32[]{:S(2)}) async-start(bf16[32,128,128]{2,1,0:T(8,128)(2,1)} %bitcast.60), calls=%async_computation.2 | async-start | bytes 2097152 | tf_op jit(solution)/shard_map/all_to_all | solution.py:548
  132.7 35.9 %all-to-all-start.1 = ((bf16[32,128,128]{2,1,0:T(8,128)(2,1)}), bf16[32,128,128]{2,1,0:T(8,128)(2,1)S(1)}, u32[]{:S(2)}, u32[]{:S(2)}) async-start(bf16[32,128,128]{2,1,0:T(8,128)(2,1)} %get-tuple-element.27.att_ref), calls=%async_computation.1 | async-start | bytes 2097152 | tf_op jit(solution)/shard_map/all_to_all | solution.py:548
  167.7 20.1 %collective-permute-start.3 = (bf16[2,32,128,128]{3,2,1,0:T(8,128)(2,1)}, bf16[2,32,128,128]{3,2,1,0:T(8,128)(2,1)}, u32[]{:S(2)}, u32[]{:S(2)}) collective-permute-start(bf16[2,32,128,128]{3,2,1,0:T(8,128)(2,1)} %get-tuple-element.35), channel_id=1, source_target_pairs={{0,32},{32,0},{64,96},{96,64},{128,160},{160,128},{192,224},{224,1... | collective-permute-start | bytes 6291464 | tf_op jit(solution)/shard_map/ppermute | solution.py:545
  168.6 43.6 %copy-start.1 = (bf16[32,128,128]{2,1,0:T(8,128)(2,1)}, bf16[32,128,128]{2,1,0:T(8,128)(2,1)S(1)}, u32[]{:S(2)}) copy-start(bf16[32,128,128]{2,1,0:T(8,128)(2,1)S(1)} %all-to-all-done.1) | copy-start | bytes 3145732
  168.6 36.8 %all-to-all-start.3 = ((bf16[32,128,128]{2,1,0:T(8,128)(2,1)}), bf16[32,128,128]{2,1,0:T(8,128)(2,1)S(1)}, u32[]{:S(2)}, u32[]{:S(2)}) async-start(bf16[32,128,128]{2,1,0:T(8,128)(2,1)} %get-tuple-element.33), calls=%async_computation.3 | async-start | bytes 2097152 | tf_op jit(solution)/shard_map/all_to_all | solution.py:548
  178.1 1.5 collective-permute-start.4
  180.3 2.8 collective-permute-start.5
  183.1 4.3 %collective-permute-start.6 = (f32[8,128]{1,0:T(8,128)S(1)}, f32[8,128]{1,0:T(8,128)S(1)}, u32[]{:S(2)}, u32[]{:S(2)}) collective-permute-start(f32[8,128]{1,0:T(8,128)S(1)} %add.36), channel_id=1, source_target_pairs={{0,128},{32,160},{64,192},{96,224},{128,0},{160,32},{192,64},{224,... | collective-permute-start | bytes 12296 | tf_op jit(solution)/shard_map/ppermute | solution.py:545
  205.4 1.0 copy-start.2
  206.4 56.5 %all-to-all-start.4 = ((bf16[32,272,128]{2,1,0:T(8,128)(2,1)}), bf16[32,272,128]{2,1,0:T(8,128)(2,1)S(1)}, u32[]{:S(2)}, u32[]{:S(2)}) async-start(bf16[32,272,128]{2,1,0:T(8,128)(2,1)} %finish.1), calls=%async_computation.4 | async-start | bytes 4456448 | tf_op jit(solution)/shard_map/all_to_all | solution.py:548
  213.1 7.6 %collective-permute-start.7 = (bf16[16,128,128]{2,1,0:T(8,128)(2,1)}, bf16[16,128,128]{2,1,0:T(8,128)(2,1)}, u32[]{:S(2)}, u32[]{:S(2)}) collective-permute-start(bf16[16,128,128]{2,1,0:T(8,128)(2,1)} %dynamic-slice_bitcast_fusion.2), channel_id=1, source_target_pairs={{0,32},{32,0},{64,96},{96,64},{128,160},{160,128},{192,224},{224,1... | collective-permute-start | bytes 1572872 | tf_op jit(solution)/shard_map/ppermute | solution.py:545
  215.8 14.5 %collective-permute-start.8 = (bf16[16,128,128]{2,1,0:T(8,128)(2,1)S(1)}, bf16[16,128,128]{2,1,0:T(8,128)(2,1)S(1)}, u32[]{:S(2)}, u32[]{:S(2)}) collective-permute-start(bf16[16,128,128]{2,1,0:T(8,128)(2,1)S(1)} %dynamic-slice_bitcast_fusion.1), channel_id=1, source_target_pairs={{0,32},{32,0},{64,96},{96,64},{128,160},{160,128},{192,224},{224,1... | collective-permute-start | bytes 1572872 | tf_op jit(solution)/shard_map/ppermute | solution.py:545
  230.3 0.8 copy-start.4
  262.9 4.4 %copy-start = (bf16[32,272,128]{2,1,0:T(8,128)(2,1)}, bf16[32,272,128]{2,1,0:T(8,128)(2,1)S(1)}, u32[]{:S(2)}) copy-start(bf16[32,272,128]{2,1,0:T(8,128)(2,1)S(1)} %all-to-all-done.4) | copy-start | bytes 6684676
  264.1 9.8 %collective-permute-start.9 = (bf16[16,272,128]{2,1,0:T(8,128)(2,1)}, bf16[16,272,128]{2,1,0:T(8,128)(2,1)}, u32[]{:S(2)}, u32[]{:S(2)}) collective-permute-start(bf16[16,272,128]{2,1,0:T(8,128)(2,1)} %dynamic-slice_bitcast_fusion), channel_id=1, source_target_pairs={{0,32},{32,0},{64,96},{96,64},{128,160},{160,128},{192,224},{224,1... | collective-permute-start | bytes 3342344 | tf_op jit(solution)/shard_map/ppermute | solution.py:545

commit v4 on v3

--- a/solution.py
+++ b/solution.py
@@ -15,7 +15,7 @@
 PAIR = 2 * BLOCK
 CHUNK = 4
 WIDTH = CHUNK * PAIR
-SPARE = 16
+SPARE = 8
 NEGATIVE = -1e30
 SCALE = HD**-0.5
 EXP_SCALE = SCALE * math.log2(math.e)
@@ -48,7 +48,7 @@
 
 
 def pack(parity, arrays, spare, heads, own):
-    group = min(heads, 4)
+    group = min(heads, 8)
     count = len(arrays)
     rows = count * PAIR + (SPARE if spare is not None else 0)
     specs = []
@@ -83,52 +83,37 @@
     )(parity, *args)
 
 
-def unpack_kernel(group, count, place_ref, *refs):
-    out_refs = refs[-count:]
-    for h in range(group):
-        for slot in range(count):
-            out_refs[slot][:, h * HD : (h + 1) * HD] = refs[slot][h]
-
-
-def unpack(place, x, count, filled):
-    heads = x.shape[-3]
-    group = min(heads, 4)
-    specs = []
-    for slot in range(count):
-        if filled is None:
-            specs.append(
-                pl.BlockSpec(
-                    (pl.Squeezed(), group, BLOCK, HD),
-                    lambda i, turn, p, slot=slot: (p[0], i, 2 * slot + turn, 0),
-                )
-            )
-        else:
-            specs.append(
-                pl.BlockSpec(
-                    (group, BLOCK, HD), lambda i, turn, p, slot=slot: (i, 2 * slot + turn, 0)
-                )
-            )
-    args = [x] * count
-    aliases = {}
-    if filled is not None:
-        aliases = {1 + count + slot: slot for slot in range(count)}
-        specs += [pl.BlockSpec(memory_space=pl.ANY)] * count
-        args += list(filled)
-    out_spec = pl.BlockSpec((BLOCK, group * HD), lambda i, turn, p: (2 * turn + p[0], i))
-    size = 2 * count * heads * PAIR * HD
+def unpack_kernel(group, core_ref, keep_ref, came_ref, *out_refs):
+    core = core_ref[0]
+    for in_ref, parity in ((keep_ref, core), (came_ref, 1 - core)):
+        for h in range(group):
+            for slot, ref in enumerate(out_refs):
+                for turn in range(2):
+                    row = slot * PAIR + turn * BLOCK
+                    at = pl.multiple_of((2 * turn + parity) * BLOCK, BLOCK)
+                    ref[pl.ds(at, BLOCK), h * HD : (h + 1) * HD] = in_ref[h, row : row + BLOCK]
+
+
+def unpack(core, keep, came, count):
+    heads, rows = keep.shape[1:3]
+    group = min(heads, 8)
     return pl.pallas_call(
-        functools.partial(unpack_kernel, group, count),
+        functools.partial(unpack_kernel, group),
         grid_spec=pltpu.PrefetchScalarGridSpec(
             num_scalar_prefetch=1,
-            grid=(heads // group, 2),
-            in_specs=specs,
-            out_specs=[out_spec] * count,
+            grid=(heads // group,),
+            in_specs=[
+                pl.BlockSpec((pl.Squeezed(), group, rows, HD), lambda i, c: (c[0], i, 0, 0)),
+                pl.BlockSpec((group, rows, HD), lambda i, c: (i, 0, 0)),
+            ],
+            out_specs=[pl.BlockSpec((4 * BLOCK, group * HD), lambda i, c: (0, i))] * count,
         ),
-        out_shape=[jax.ShapeDtypeStruct((4 * BLOCK, heads * HD), x.dtype)] * count,
-        input_output_aliases=aliases,
-        cost_estimate=pl.CostEstimate(flops=0, bytes_accessed=2 * size, transcendentals=0),
-        name="unpack_own" if filled is None else "unpack_sent",
-    )(place, *args)
+        out_shape=[jax.ShapeDtypeStruct((4 * BLOCK, heads * HD), keep.dtype)] * count,
+        cost_estimate=pl.CostEstimate(
+            flops=0, bytes_accessed=16 * count * BLOCK * heads * HD, transcendentals=0
+        ),
+        name="unpack",
+    )(core, keep, came)
 
 
 def locate(block):
@@ -519,7 +504,7 @@
 
 
 def finish(own, other, scaled_gain, gain_grad, places):
-    group = 4
+    group = 8 if places % 8 == 0 else 4
     spec = pl.BlockSpec((2, group, PAIR, HD), lambda i: (0, i, 0, 0))
     row = pl.BlockSpec((1, HD), lambda i: (0, 0))
     rows = 2 * PAIR + SPARE
@@ -556,7 +541,7 @@
     def scatter(x, count):
         x = x.reshape(2, heads, x.shape[1], HD)
         came = swap(lax.dynamic_index_in_dim(x, 1 - core, axis=0, keepdims=False))
-        return unpack(1 - cores, came, count, unpack(cores, x, count, None))
+        return unpack(cores, x, came, count)
 
     named = random_blocks.reshape(heads, 2, 2, NR).transpose(2, 0, 1, 3).reshape(2, heads, 1, 2 * NR)
     named = jnp.pad(named.astype(jnp.bfloat16), ((0, 0), (0, 0), (0, 0), (0, HD - 2 * NR)))

time: 282 us -> 269 us (0.954)
  Pallas kernels: 101 us -> 71.6 us
  waiting for transfers between devices: 109 us -> 128 us
    pallas_call x6 -> x3, Pallas kernels: 29.3 us -> 7.07 us  [unpack(): pl.pallas_call(functools.partial(unpack_kernel, group), grid_spec=pltpu.P...]
    all_to_all x5, waiting for transfers between devices: 105 us -> 121 us  [over_seq(): return lax.all_to_all(x, 'seq', split_axis=0, concat_axis=0, tiled=True)]
    pallas_call x4, Pallas kernels: 13.6 us -> 8.8 us  [pack(): pl.pallas_call(functools.partial(pack_kernel, group, count, spare is not...]
    ppermute x10, waiting for transfers between devices: 4.12 us -> 7.42 us  [swap(): return lax.ppermute(x, 'dp', [(i, i ^ bit) for i in range(dp)])]
  transfers between devices with their start and end apart: 15 -> 15, of which waited for: 7 -> 10; matrix products, arithmetic and copies ran while one was open for 3% -> 3% of each run, Pallas kernels for 33% -> 25%
where the time goes in v4:
time: 269 us; the launch traced here: 268 us
  waiting for transfers between devices  128 us (48%)
  Pallas kernels  71.6 us (27%)
  starting transfers between devices  55.3 us (21%)
  local copies, waits for them, and re-layouts  9.11 us (3%)
  other arithmetic  3.44 us (1%)
    all_to_all x5, waiting for transfers between devices, over_seq(): return lax.all_to_all(x, 'seq', split_axis=0, concat_axis=0, tiled=True)  121 us
    all_to_all x5, starting transfers between devices, over_seq(): return lax.all_to_all(x, 'seq', split_axis=0, concat_axis=0, tiled=True)  38.8 us
    pallas_call x1, Pallas kernels, backward(): pl.pallas_call(functools.partial(backward_kernel, places, unroll), in_spe...  27 us
    pallas_call x1, Pallas kernels, forward(): pl.pallas_call(functools.partial(forward_kernel, places, unroll), in_spec...  24 us
    ppermute x10, starting transfers between devices, swap(): return lax.ppermute(x, 'dp', [(i, i ^ bit) for i in range(dp)])  16.5 us
    pallas_call x4, Pallas kernels, pack(): pl.pallas_call(functools.partial(pack_kernel, group, count, spare is not...  8.8 us
    ppermute x10, waiting for transfers between devices, swap(): return lax.ppermute(x, 'dp', [(i, i ^ bit) for i in range(dp)])  7.42 us
    pallas_call x3, Pallas kernels, unpack(): pl.pallas_call(functools.partial(unpack_kernel, group), grid_spec=pltpu.P...  7.07 us
  transfers between devices with their start and end apart: 15, of which 10 were waited for; matrix products, arithmetic and copies ran while one was open for 3% of the time, Pallas kernels for 25%

profile of v4, /device:TPU:1, one launch (start us, length us, event | category | flops | bytes accessed | tf_op | source)
XLA Modules:
  0.0 268.4 jit_solution(14856848474148419472)
XLA Ops:
  0.6 0.7 convert_element_type.32
  1.3 0.1 copy.15
  1.5 0.6 pad.4.refs_6_
  2.1 2.5 pack_sent.2
  4.6 3.2 %collective-permute-start = (bf16[16,392,128]{2,1,0:T(8,128)(2,1)}, bf16[16,392,128]{2,1,0:T(8,128)(2,1)S(1)}, u32[]{:S(2)}, u32[]{:S(2)}) collective-permute-start(bf16[16,392,128]{2,1,0:T(8,128)(2,1)} %pack_sent.2), channel_id=1, source_target_pairs={{0,32},{32,0},{64,96},{96,64},{128,160},{160,128},{192,224},{224,1... | collective-permute-start | bytes 4816904 | tf_op jit(solution)/shard_map/ppermute | solution.py:530
  7.9 2.5 pack_own.2
  10.4 0.8 collective-permute-done
  11.2 1.3 bitcast_dynamic-update-slice_fusion
  12.4 9.5 %all-to-all-start = ((bf16[32,392,128]{2,1,0:T(8,128)(2,1)}), bf16[32,392,128]{2,1,0:T(8,128)(2,1)S(1)}, u32[]{:S(2)}, u32[]{:S(2)}) async-start(bf16[32,392,128]{2,1,0:T(8,128)(2,1)} %bitcast.52), calls=%async_computation | async-start | bytes 6422528 | tf_op jit(solution)/shard_map/all_to_all | solution.py:533
  21.9 1.9 pack_sent.3
  23.8 0.6 collective-permute-start.1
  24.4 1.8 pack_own.3
  26.3 0.0 collective-permute-done.1
  26.3 1.9 bitcast_dynamic-update-slice_fusion.1
  28.2 66.0 %all-to-all-done.own_ref = bf16[32,392,128]{2,1,0:T(8,128)(2,1)S(1)} async-done(((bf16[32,392,128]{2,1,0:T(8,128)(2,1)}), bf16[32,392,128]{2,1,0:T(8,128)(2,1)S(1)}, u32[]{:S(2)}, u32[]{:S(2)}) %all-to-all-start) | async-done | bytes 3211296 | tf_op jit(solution)/shard_map/all_to_all | solution.py:533
  94.2 0.0 copy-start.3
  94.2 2.3 collective-permute-start.2
  96.5 6.1 %all-to-all-start.2 = ((bf16[32,128,128]{2,1,0:T(8,128)(2,1)}), bf16[32,128,128]{2,1,0:T(8,128)(2,1)}, u32[]{:S(2)}, u32[]{:S(2)}) async-start(bf16[32,128,128]{2,1,0:T(8,128)(2,1)} %bitcast.57), calls=%async_computation.2 | async-start | bytes 2097152 | tf_op jit(solution)/shard_map/all_to_all | solution.py:533
  102.6 1.4 multiply_bitcast_fusion
  103.9 0.1 convert_reduce_fusion.1
  104.0 0.7 reshape.65.table_ref
  104.7 0.0 collective-permute-done.2.other_ref
  104.7 0.0 copy-done.3
  104.7 24.0 %forward.1 = (bf16[32,128,128]{2,1,0:T(8,128)(2,1)}, bf16[64,64,512]{2,1,0:T(8,128)(2,1)}, bf16[16,64,512]{2,1,0:T(8,128)(2,1)}, bf16[2,32,128,128]{3,2,1,0:T(8,128)(2,1)}) custom-call(s32[1]{0:T(128)} %bitcast.parity_ref.core_ref, s32[192]{0:T(256)} %reshape.65.table_ref, f32[1,128]{1,0:T(1,128)} %get-tuple-element.44.gain_ref, ...), custom_call_target="tpu_custom_call" | custom-call | flops 3221225472 | bytes 62914560 | tf_op jit(solution)/shard_map/forward/pallas_call | solution.py:269
  128.7 1.1 all-to-all-done.2.grad_ref
  129.8 8.1 %all-to-all-start.1 = ((bf16[32,128,128]{2,1,0:T(8,128)(2,1)}), bf16[32,128,128]{2,1,0:T(8,128)(2,1)S(1)}, u32[]{:S(2)}, u32[]{:S(2)}) async-start(bf16[32,128,128]{2,1,0:T(8,128)(2,1)} %get-tuple-element.25.att_ref), calls=%async_computation.1 | async-start | bytes 2097152 | tf_op jit(solution)/shard_map/all_to_all | solution.py:533
  137.9 27.0 %backward.1 = (bf16[32,128,128]{2,1,0:T(8,128)(2,1)}, f32[2,32,128,128]{3,2,1,0:T(8,128)}, bf16[2,32,128,128]{3,2,1,0:T(8,128)(2,1)}, f32[8,128]{1,0:T(8,128)}) custom-call(s32[1]{0:T(128)} %bitcast.parity_ref.core_ref, s32[192]{0:T(256)} %reshape.65.table_ref, bf16[32,392,128]{2,1,0:T(8,128)(2,1)} %copy-done.3, ...), custom_call_target="tpu_custom_call" | custom-call | flops 6442450944 | bytes 104857600 | tf_op jit(solution)/shard_map/backward/pallas_call | solution.py:452
  164.9 0.9 collective-permute-start.3
  165.8 0.0 all-to-all-done.1
  165.8 0.0 copy-start.1
  165.8 9.5 %all-to-all-start.3 = ((bf16[32,128,128]{2,1,0:T(8,128)(2,1)}), bf16[32,128,128]{2,1,0:T(8,128)(2,1)S(1)}, u32[]{:S(2)}, u32[]{:S(2)}) async-start(bf16[32,128,128]{2,1,0:T(8,128)(2,1)} %get-tuple-element.31), calls=%async_computation.3 | async-start | bytes 2097152 | tf_op jit(solution)/shard_map/all_to_all | solution.py:533
  175.3 0.4 collective-permute-start.4
  175.7 1.1 collective-permute-done.4
  176.8 0.7 add.35
  177.5 1.2 collective-permute-start.5
  178.7 1.5 collective-permute-done.5
  180.2 2.7 %collective-permute-start.6 = (f32[8,128]{1,0:T(8,128)S(1)}, f32[8,128]{1,0:T(8,128)S(1)}, u32[]{:S(2)}, u32[]{:S(2)}) collective-permute-start(f32[8,128]{1,0:T(8,128)S(1)} %add.36), channel_id=1, source_target_pairs={{0,128},{32,160},{64,192},{96,224},{128,0},{160,32},{192,64},{224,... | collective-permute-start | bytes 12296 | tf_op jit(solution)/shard_map/ppermute | solution.py:530
  183.0 1.5 collective-permute-done.6
  184.5 0.5 slice.10.gain_grad_ref
  185.0 0.0 collective-permute-done.3.other_ref
  185.0 4.7 %finish.1 = bf16[32,264,128]{2,1,0:T(8,128)(2,1)} custom-call(f32[2,32,128,128]{3,2,1,0:T(8,128)} %get-tuple-element.32.own_ref, bf16[2,32,128,128]{3,2,1,0:T(8,128)(2,1)} %collective-permute-done.3.other_ref, f32[1,128]{1,0:T(1,128)} %get-tuple-element.43.scaled_gain_ref, f32[1,128]{1,0:T(1,128)} %slice.10.gain_grad_ref), custom_call_target="tpu_custom_call" | custom-call | tf_op jit(solution)/shard_map/finish/pallas_call | solution.py:511
  189.7 12.9 %all-to-all-done.3 = bf16[32,128,128]{2,1,0:T(8,128)(2,1)S(1)} async-done(((bf16[32,128,128]{2,1,0:T(8,128)(2,1)}), bf16[32,128,128]{2,1,0:T(8,128)(2,1)S(1)}, u32[]{:S(2)}, u32[]{:S(2)}) %all-to-all-start.3) | async-done | bytes 1048608 | tf_op jit(solution)/shard_map/all_to_all | solution.py:533
  202.6 0.0 copy-start.2
  202.6 1.0 copy-done.2
  203.6 5.7 %all-to-all-start.4 = ((bf16[32,264,128]{2,1,0:T(8,128)(2,1)}), bf16[32,264,128]{2,1,0:T(8,128)(2,1)S(1)}, u32[]{:S(2)}, u32[]{:S(2)}) async-start(bf16[32,264,128]{2,1,0:T(8,128)(2,1)} %finish.1), calls=%async_computation.4 | async-start | bytes 4325376 | tf_op jit(solution)/shard_map/all_to_all | solution.py:533
  209.3 0.0 copy-done.1
  209.3 1.7 collective-permute-start.7
  211.0 1.1 dynamic-slice_bitcast_fusion.1
  212.1 0.1 collective-permute-start.8
  212.2 0.5 collective-permute-done.7.came_ref
  212.7 2.1 unpack.3
  214.8 0.0 collective-permute-done.8.came_ref
  214.8 0.0 copy-start.4
  214.8 0.8 copy-done.4
  215.6 2.1 unpack.4
  217.8 40.8 %all-to-all-done.4 = bf16[32,264,128]{2,1,0:T(8,128)(2,1)S(1)} async-done(((bf16[32,264,128]{2,1,0:T(8,128)(2,1)}), bf16[32,264,128]{2,1,0:T(8,128)(2,1)S(1)}, u32[]{:S(2)}, u32[]{:S(2)}) %all-to-all-start.4) | async-done | bytes 2162720 | tf_op jit(solution)/shard_map/all_to_all | solution.py:533
  258.5 0.0 copy-start
  258.5 1.1 dynamic-slice_bitcast_fusion
  259.6 3.3 %collective-permute-start.9 = (bf16[16,264,128]{2,1,0:T(8,128)(2,1)}, bf16[16,264,128]{2,1,0:T(8,128)(2,1)}, u32[]{:S(2)}, u32[]{:S(2)}) collective-permute-start(bf16[16,264,128]{2,1,0:T(8,128)(2,1)} %dynamic-slice_bitcast_fusion), channel_id=1, source_target_pairs={{0,32},{32,0},{64,96},{96,64},{128,160},{160,128},{192,224},{224,1... | collective-permute-start | bytes 3244040 | tf_op jit(solution)/shard_map/ppermute | solution.py:530
  263.0 0.6 reduce_sum.18
  263.6 2.0 collective-permute-done.9.came_ref
  265.6 0.0 copy-done
  265.6 2.8 %unpack.5 = (bf16[256,2048]{1,0:T(8,128)(2,1)}, bf16[256,2048]{1,0:T(8,128)(2,1)}) custom-call(s32[1]{0:T(128)} %bitcast.parity_ref.core_ref, bf16[2,16,264,128]{3,2,1,0:T(8,128)(2,1)} %bitcast.51, bf16[16,264,128]{2,1,0:T(8,128)(2,1)} %collective-permute-done.9.came_ref), custom_call_target="tpu_custom_call" | custom-call | bytes 4194304 | tf_op jit(solution)/shard_map/unpack/pallas_call | solution.py:100
  (5 shorter events, 0.1 us)
Async XLA Ops:
  4.6 6.5 %collective-permute-start = (bf16[16,392,128]{2,1,0:T(8,128)(2,1)}, bf16[16,392,128]{2,1,0:T(8,128)(2,1)S(1)}, u32[]{:S(2)}, u32[]{:S(2)}) collective-permute-start(bf16[16,392,128]{2,1,0:T(8,128)(2,1)} %pack_sent.2), channel_id=1, source_target_pairs={{0,32},{32,0},{64,96},{96,64},{128,160},{160,128},{192,224},{224,1... | collective-permute-start | bytes 4816904 | tf_op jit(solution)/shard_map/ppermute | solution.py:530
  12.4 81.8 %all-to-all-start = ((bf16[32,392,128]{2,1,0:T(8,128)(2,1)}), bf16[32,392,128]{2,1,0:T(8,128)(2,1)S(1)}, u32[]{:S(2)}, u32[]{:S(2)}) async-start(bf16[32,392,128]{2,1,0:T(8,128)(2,1)} %bitcast.52), calls=%async_computation | async-start | bytes 6422528 | tf_op jit(solution)/shard_map/all_to_all | solution.py:533
  23.8 2.5 collective-permute-start.1
  94.2 10.4 %copy-start.3 = (bf16[32,392,128]{2,1,0:T(8,128)(2,1)}, bf16[32,392,128]{2,1,0:T(8,128)(2,1)S(1)}, u32[]{:S(2)}) copy-start(bf16[32,392,128]{2,1,0:T(8,128)(2,1)S(1)} %all-to-all-done.own_ref) | copy-start | bytes 9633796
  94.2 10.4 %collective-permute-start.2 = (bf16[32,392,128]{2,1,0:T(8,128)(2,1)S(1)}, bf16[32,392,128]{2,1,0:T(8,128)(2,1)}, u32[]{:S(2)}, u32[]{:S(2)}) collective-permute-start(bf16[32,392,128]{2,1,0:T(8,128)(2,1)S(1)} %all-to-all-done.own_ref), channel_id=1, source_target_pairs={{0,32},{32,0},{64,96},{96,64},{128,160},{160,128},{192,224},{224,1... | collective-permute-start | bytes 9633800 | tf_op jit(solution)/shard_map/ppermute | solution.py:530
  96.5 33.3 %all-to-all-start.2 = ((bf16[32,128,128]{2,1,0:T(8,128)(2,1)}), bf16[32,128,128]{2,1,0:T(8,128)(2,1)}, u32[]{:S(2)}, u32[]{:S(2)}) async-start(bf16[32,128,128]{2,1,0:T(8,128)(2,1)} %bitcast.57), calls=%async_computation.2 | async-start | bytes 2097152 | tf_op jit(solution)/shard_map/all_to_all | solution.py:533
  129.8 36.0 %all-to-all-start.1 = ((bf16[32,128,128]{2,1,0:T(8,128)(2,1)}), bf16[32,128,128]{2,1,0:T(8,128)(2,1)S(1)}, u32[]{:S(2)}, u32[]{:S(2)}) async-start(bf16[32,128,128]{2,1,0:T(8,128)(2,1)} %get-tuple-element.25.att_ref), calls=%async_computation.1 | async-start | bytes 2097152 | tf_op jit(solution)/shard_map/all_to_all | solution.py:533
  164.9 20.1 %collective-permute-start.3 = (bf16[2,32,128,128]{3,2,1,0:T(8,128)(2,1)}, bf16[2,32,128,128]{3,2,1,0:T(8,128)(2,1)}, u32[]{:S(2)}, u32[]{:S(2)}) collective-permute-start(bf16[2,32,128,128]{3,2,1,0:T(8,128)(2,1)} %get-tuple-element.33), channel_id=1, source_target_pairs={{0,32},{32,0},{64,96},{96,64},{128,160},{160,128},{192,224},{224,1... | collective-permute-start | bytes 6291464 | tf_op jit(solution)/shard_map/ppermute | solution.py:530
  165.8 43.5 %copy-start.1 = (bf16[32,128,128]{2,1,0:T(8,128)(2,1)}, bf16[32,128,128]{2,1,0:T(8,128)(2,1)S(1)}, u32[]{:S(2)}) copy-start(bf16[32,128,128]{2,1,0:T(8,128)(2,1)S(1)} %all-to-all-done.1) | copy-start | bytes 3145732
  165.8 36.8 %all-to-all-start.3 = ((bf16[32,128,128]{2,1,0:T(8,128)(2,1)}), bf16[32,128,128]{2,1,0:T(8,128)(2,1)S(1)}, u32[]{:S(2)}, u32[]{:S(2)}) async-start(bf16[32,128,128]{2,1,0:T(8,128)(2,1)} %get-tuple-element.31), calls=%async_computation.3 | async-start | bytes 2097152 | tf_op jit(solution)/shard_map/all_to_all | solution.py:533
  175.3 1.5 collective-permute-start.4
  177.5 2.8 %collective-permute-start.5 = (f32[8,128]{1,0:T(8,128)S(1)}, f32[8,128]{1,0:T(8,128)S(1)}, u32[]{:S(2)}, u32[]{:S(2)}) collective-permute-start(f32[8,128]{1,0:T(8,128)S(1)} %add.35), channel_id=1, source_target_pairs={{0,64},{32,96},{64,0},{96,32},{128,192},{160,224},{192,128},{224,1... | collective-permute-start | bytes 12296 | tf_op jit(solution)/shard_map/ppermute | solution.py:530
  180.2 4.3 %collective-permute-start.6 = (f32[8,128]{1,0:T(8,128)S(1)}, f32[8,128]{1,0:T(8,128)S(1)}, u32[]{:S(2)}, u32[]{:S(2)}) collective-permute-start(f32[8,128]{1,0:T(8,128)S(1)} %add.36), channel_id=1, source_target_pairs={{0,128},{32,160},{64,192},{96,224},{128,0},{160,32},{192,64},{224,... | collective-permute-start | bytes 12296 | tf_op jit(solution)/shard_map/ppermute | solution.py:530
  202.6 1.0 copy-start.2
  203.6 54.9 %all-to-all-start.4 = ((bf16[32,264,128]{2,1,0:T(8,128)(2,1)}), bf16[32,264,128]{2,1,0:T(8,128)(2,1)S(1)}, u32[]{:S(2)}, u32[]{:S(2)}) async-start(bf16[32,264,128]{2,1,0:T(8,128)(2,1)} %finish.1), calls=%async_computation.4 | async-start | bytes 4325376 | tf_op jit(solution)/shard_map/all_to_all | solution.py:533
  209.3 3.4 %collective-permute-start.7 = (bf16[16,128,128]{2,1,0:T(8,128)(2,1)S(1)}, bf16[16,128,128]{2,1,0:T(8,128)(2,1)}, u32[]{:S(2)}, u32[]{:S(2)}) collective-permute-start(bf16[16,128,128]{2,1,0:T(8,128)(2,1)S(1)} %dynamic-slice_bitcast_fusion.2), channel_id=1, source_target_pairs={{0,32},{32,0},{64,96},{96,64},{128,160},{160,128},{192,224},{224,1... | collective-permute-start | bytes 1572872 | tf_op jit(solution)/shard_map/ppermute | solution.py:530
  212.1 2.7 %collective-permute-start.8 = (bf16[16,128,128]{2,1,0:T(8,128)(2,1)S(1)}, bf16[16,128,128]{2,1,0:T(8,128)(2,1)S(1)}, u32[]{:S(2)}, u32[]{:S(2)}) collective-permute-start(bf16[16,128,128]{2,1,0:T(8,128)(2,1)S(1)} %dynamic-slice_bitcast_fusion.1), channel_id=1, source_target_pairs={{0,32},{32,0},{64,96},{96,64},{128,160},{160,128},{192,224},{224,1... | collective-permute-start | bytes 1572872 | tf_op jit(solution)/shard_map/ppermute | solution.py:530
  214.8 0.8 copy-start.4
  258.5 7.1 %copy-start = (bf16[32,264,128]{2,1,0:T(8,128)(2,1)}, bf16[32,264,128]{2,1,0:T(8,128)(2,1)S(1)}, u32[]{:S(2)}) copy-start(bf16[32,264,128]{2,1,0:T(8,128)(2,1)S(1)} %all-to-all-done.4) | copy-start | bytes 6488068
  259.6 5.9 %collective-permute-start.9 = (bf16[16,264,128]{2,1,0:T(8,128)(2,1)}, bf16[16,264,128]{2,1,0:T(8,128)(2,1)}, u32[]{:S(2)}, u32[]{:S(2)}) collective-permute-start(bf16[16,264,128]{2,1,0:T(8,128)(2,1)} %dynamic-slice_bitcast_fusion), channel_id=1, source_target_pairs={{0,32},{32,0},{64,96},{96,64},{128,160},{160,128},{192,224},{224,1... | collective-permute-start | bytes 3244040 | tf_op jit(solution)/shard_map/ppermute | solution.py:530

commit v5 on v4

--- a/solution.py
+++ b/solution.py
@@ -483,39 +483,35 @@
     )(core, table, own, other, keys, grads, att, weights, dense)
 
 
-def finish_kernel(own_ref, other_ref, scaled_gain_ref, gain_grad_ref, out_ref):
+def finish_kernel(own_ref, other_ref, dq_ref, scaled_gain_ref, out_ref):
     gain = scaled_gain_ref[...]
     dkey = own_ref[0] + other_ref[0].astype(jnp.float32)
     out_ref[:, :PAIR] = (dkey * gain).astype(jnp.bfloat16)
     dvalue = own_ref[1] + other_ref[1].astype(jnp.float32)
     out_ref[:, PAIR : 2 * PAIR] = dvalue.astype(jnp.bfloat16)
-    total = gain_grad_ref[...]
-    high = total.astype(jnp.bfloat16)
-    rest = total - high.astype(jnp.float32)
-    middle = rest.astype(jnp.bfloat16)
-    low = (rest - middle.astype(jnp.float32)).astype(jnp.bfloat16)
-    row = lax.broadcasted_iota(jnp.int32, (SPARE, HD), 0)
-    spare = jnp.where(
-        row == 0,
-        high.astype(jnp.float32),
-        jnp.where(row == 1, middle.astype(jnp.float32), low.astype(jnp.float32)),
-    ).astype(jnp.bfloat16)
-    out_ref[:, 2 * PAIR :] = jnp.broadcast_to(spare, (out_ref.shape[0], SPARE, HD))
-
-
-def finish(own, other, scaled_gain, gain_grad, places):
+    out_ref[:, 2 * PAIR : 3 * PAIR] = dq_ref[...]
+
+
+def finish(own, other, dq, scaled_gain, places):
     group = 8 if places % 8 == 0 else 4
     spec = pl.BlockSpec((2, group, PAIR, HD), lambda i: (0, i, 0, 0))
-    row = pl.BlockSpec((1, HD), lambda i: (0, 0))
-    rows = 2 * PAIR + SPARE
+    rows = 3 * PAIR
     return pl.pallas_call(
         finish_kernel,
         grid=(places // group,),
-        in_specs=[spec, spec, row, row],
+        in_specs=[
+            spec,
+            spec,
+            pl.BlockSpec((group, PAIR, HD), lambda i: (i, 0, 0)),
+            pl.BlockSpec((1, HD), lambda i: (0, 0)),
+        ],
         out_specs=pl.BlockSpec((group, rows, HD), lambda i: (i, 0, 0)),
         out_shape=jax.ShapeDtypeStruct((places, rows, HD), jnp.bfloat16),
+        cost_estimate=pl.CostEstimate(
+            flops=0, bytes_accessed=20 * places * PAIR * HD, transcendentals=0
+        ),
         name="finish",
-    )(own, other, scaled_gain, gain_grad)
+    )(own, other, dq, scaled_gain)
 
 
 def shards(queries, keys, values, key_gain, random_blocks, out_grad):
@@ -529,6 +525,9 @@
     def swap(x, bit=1):
         return lax.ppermute(x, "dp", [(i, i ^ bit) for i in range(dp)])
 
+    def swap_seq(x, bit):
+        return lax.ppermute(x, "seq", [(i, i ^ bit) for i in range(places)])
+
     def over_seq(x):
         return lax.all_to_all(x, "seq", split_axis=0, concat_axis=0, tiled=True)
 
@@ -559,22 +558,32 @@
     dq, part_own, part_other, gain_term = backward(
         cores, table, own, other, keys_scaled, grads, att, weights, dense, places
     )
-    att_back, dq = lax.optimization_barrier((att_back, dq))
-    dq_back = over_seq(dq)
-    part_came = swap(part_other)
+    att_back, part_other = lax.optimization_barrier((att_back, part_other))
+    grads_out = finish(part_own, swap(part_other), dq, gain * SCALE, places)
+    grads_out, gain_term = lax.optimization_barrier((grads_out, gain_term))
+    grads_back = over_seq(grads_out)
+    (attended,) = scatter(att_back, 1)
     bit = 1
     while bit < dp:
         gain_term = gain_term + swap(gain_term, bit)
         bit *= 2
-    dkv = finish(part_own, part_came, gain * SCALE, gain_term[:1], places)
-    dq_back, dkv = lax.optimization_barrier((dq_back, dkv))
-    dkv_back = over_seq(dkv)
-    (attended,) = scatter(att_back, 1)
-    (query_grad,) = scatter(dq_back, 1)
-    dkv_back, attended, query_grad = lax.optimization_barrier((dkv_back, attended, query_grad))
-    key_grad, value_grad = scatter(dkv_back, 2)
-    gain_rows = dkv_back[:, 2 * PAIR : 2 * PAIR + 3].astype(jnp.float32)
-    gain_grad = jnp.sum(gain_rows.reshape(2, heads, 3, HD), axis=(0, 2)).reshape(heads * HD)
+    gain_term = gain_term[:1]
+    gain_term = gain_term + swap_seq(gain_term, heads)
+    bit = 1
+    while bit < heads:
+        other_heads = swap_seq(gain_term, bit)
+        lower = (head // bit) % 2 == 0
+        gain_term = jnp.concatenate(
+            [
+                jnp.where(lower, gain_term, other_heads),
+                jnp.where(lower, other_heads, gain_term),
+            ],
+            axis=0,
+        )
+        bit *= 2
+    gain_grad = gain_term.reshape(heads * HD)
+    grads_back, attended, gain_grad = lax.optimization_barrier((grads_back, attended, gain_grad))
+    key_grad, value_grad, query_grad = scatter(grads_back, 3)
     return (attended[None], query_grad[None], key_grad[None], value_grad[None], gain_grad)
 
 

time: 269 us -> 286 us (1.063)
  starting transfers between devices: 55.3 us -> 65.4 us
  waiting for transfers between devices: 128 us -> 137 us
    ppermute x0 -> x5, waiting for transfers between devices: none -> 58.7 us  [swap_seq(): return lax.ppermute(x, 'seq', [(i, i ^ bit) for i in range(places)])]
    all_to_all x5 -> x4, waiting for transfers between devices: 121 us -> 67.4 us  [over_seq(): return lax.all_to_all(x, 'seq', split_axis=0, concat_axis=0, tiled=True)]
    ppermute x0 -> x5, starting transfers between devices: none -> 15.1 us  [swap_seq(): return lax.ppermute(x, 'seq', [(i, i ^ bit) for i in range(places)])]
    all_to_all x5 -> x4, starting transfers between devices: 38.8 us -> 33.1 us  [over_seq(): return lax.all_to_all(x, 'seq', split_axis=0, concat_axis=0, tiled=True)]
    ppermute x10 -> x9, waiting for transfers between devices: 7.42 us -> 11.2 us  [swap(): return lax.ppermute(x, 'dp', [(i, i ^ bit) for i in range(dp)])]
    pallas_call x3 -> x2, Pallas kernels: 7.07 us -> 5.6 us  [unpack(): pl.pallas_call(functools.partial(unpack_kernel, group), grid_spec=pltpu.P...]
    ppermute x10 -> x9, starting transfers between devices: 16.5 us -> 17.2 us  [swap(): return lax.ppermute(x, 'dp', [(i, i ^ bit) for i in range(dp)])]
  transfers between devices with their start and end apart: 15 -> 18, of which waited for: 10 -> 11; matrix products, arithmetic and copies ran while one was open for 3% -> 2% of each run, Pallas kernels for 25% -> 21%
where the time goes in v5:
time: 286 us; the launch traced here: 285 us
  waiting for transfers between devices  137 us (48%)
  Pallas kernels  70.6 us (25%)
  starting transfers between devices  65.4 us (23%)
  local copies, waits for them, and re-layouts  6.96 us (2%)
  other arithmetic  3.62 us (1%)
    all_to_all x4, waiting for transfers between devices, over_seq(): return lax.all_to_all(x, 'seq', split_axis=0, concat_axis=0, tiled=True)  67.4 us
    ppermute x5, waiting for transfers between devices, swap_seq(): return lax.ppermute(x, 'seq', [(i, i ^ bit) for i in range(places)])  58.7 us
    all_to_all x4, starting transfers between devices, over_seq(): return lax.all_to_all(x, 'seq', split_axis=0, concat_axis=0, tiled=True)  33.1 us
    pallas_call x1, Pallas kernels, backward(): pl.pallas_call(functools.partial(backward_kernel, places, unroll), in_spe...  27 us
    pallas_call x1, Pallas kernels, forward(): pl.pallas_call(functools.partial(forward_kernel, places, unroll), in_spec...  24 us
    ppermute x9, starting transfers between devices, swap(): return lax.ppermute(x, 'dp', [(i, i ^ bit) for i in range(dp)])  17.2 us
    ppermute x5, starting transfers between devices, swap_seq(): return lax.ppermute(x, 'seq', [(i, i ^ bit) for i in range(places)])  15.1 us
    ppermute x9, waiting for transfers between devices, swap(): return lax.ppermute(x, 'dp', [(i, i ^ bit) for i in range(dp)])  11.2 us
  transfers between devices with their start and end apart: 18, of which 11 were waited for; matrix products, arithmetic and copies ran while one was open for 2% of the time, Pallas kernels for 21%

profile of v5, /device:TPU:1, one launch (start us, length us, event | category | flops | bytes accessed | tf_op | source)
XLA Modules:
  0.0 284.7 jit_solution(9891099430795126435)
XLA Ops:
  0.6 0.7 convert_element_type.29
  1.3 0.1 copy.13
  1.5 0.6 pad.4.refs_6_
  2.1 2.5 pack_sent.2
  4.6 3.2 %collective-permute-start = (bf16[16,392,128]{2,1,0:T(8,128)(2,1)}, bf16[16,392,128]{2,1,0:T(8,128)(2,1)S(1)}, u32[]{:S(2)}, u32[]{:S(2)}) collective-permute-start(bf16[16,392,128]{2,1,0:T(8,128)(2,1)} %pack_sent.2), channel_id=1, source_target_pairs={{0,32},{32,0},{64,96},{96,64},{128,160},{160,128},{192,224},{224,1... | collective-permute-start | bytes 4816904 | tf_op jit(solution)/shard_map/ppermute | solution.py:526
  7.8 2.5 pack_own.2
  10.3 0.8 collective-permute-done
  11.1 1.3 bitcast_dynamic-update-slice_fusion
  12.4 9.6 %all-to-all-start = ((bf16[32,392,128]{2,1,0:T(8,128)(2,1)}), bf16[32,392,128]{2,1,0:T(8,128)(2,1)}, u32[]{:S(2)}, u32[]{:S(2)}) async-start(bf16[32,392,128]{2,1,0:T(8,128)(2,1)} %bitcast.49), calls=%async_computation | async-start | bytes 6422528 | tf_op jit(solution)/shard_map/all_to_all | solution.py:532
  22.0 1.9 pack_sent.3
  23.9 0.6 collective-permute-start.1
  24.5 1.8 pack_own.3
  26.4 0.0 collective-permute-done.1
  26.4 0.8 bitcast_dynamic-update-slice_fusion.1
  27.2 67.1 %all-to-all-done.own_ref = bf16[32,392,128]{2,1,0:T(8,128)(2,1)} async-done(((bf16[32,392,128]{2,1,0:T(8,128)(2,1)}), bf16[32,392,128]{2,1,0:T(8,128)(2,1)}, u32[]{:S(2)}, u32[]{:S(2)}) %all-to-all-start) | async-done | bytes 3211296 | tf_op jit(solution)/shard_map/all_to_all | solution.py:532
  94.3 2.2 collective-permute-start.2
  96.5 6.0 %all-to-all-start.1 = ((bf16[32,128,128]{2,1,0:T(8,128)(2,1)}), bf16[32,128,128]{2,1,0:T(8,128)(2,1)S(1)}, u32[]{:S(2)}, u32[]{:S(2)}) async-start(bf16[32,128,128]{2,1,0:T(8,128)(2,1)} %bitcast.52), calls=%async_computation.1 | async-start | bytes 2097152 | tf_op jit(solution)/shard_map/all_to_all | solution.py:532
  102.5 1.4 multiply_bitcast_fusion
  103.9 0.9 convert_reduce_fusion
  104.8 0.7 reshape.59.table_ref
  105.5 0.0 collective-permute-done.2.other_ref
  105.5 24.0 %forward.1 = (bf16[32,128,128]{2,1,0:T(8,128)(2,1)}, bf16[64,64,512]{2,1,0:T(8,128)(2,1)}, bf16[16,64,512]{2,1,0:T(8,128)(2,1)}, bf16[2,32,128,128]{3,2,1,0:T(8,128)(2,1)}) custom-call(s32[1]{0:T(128)} %bitcast.parity_ref.core_ref, s32[192]{0:T(256)} %reshape.59.table_ref, f32[1,128]{1,0:T(1,128)} %get-tuple-element.48.gain_ref, ...), custom_call_target="tpu_custom_call" | custom-call | flops 3221225472 | bytes 62914560 | tf_op jit(solution)/shard_map/forward/pallas_call | solution.py:269
  129.5 0.3 all-to-all-done.1.grad_ref
  129.8 0.0 copy-start.3
  129.8 9.0 %all-to-all-start.2 = ((bf16[32,128,128]{2,1,0:T(8,128)(2,1)}), bf16[32,128,128]{2,1,0:T(8,128)(2,1)S(1)}, u32[]{:S(2)}, u32[]{:S(2)}) async-start(bf16[32,128,128]{2,1,0:T(8,128)(2,1)} %get-tuple-element.28.att_ref), calls=%async_computation.2 | async-start | bytes 2097152 | tf_op jit(solution)/shard_map/all_to_all | solution.py:532
  138.8 0.0 copy-done.3
  138.8 27.0 %backward.1 = (bf16[32,128,128]{2,1,0:T(8,128)(2,1)}, f32[2,32,128,128]{3,2,1,0:T(8,128)}, bf16[2,32,128,128]{3,2,1,0:T(8,128)(2,1)}, f32[8,128]{1,0:T(8,128)}) custom-call(s32[1]{0:T(128)} %bitcast.parity_ref.core_ref, s32[192]{0:T(256)} %reshape.59.table_ref, bf16[32,392,128]{2,1,0:T(8,128)(2,1)} %all-to-all-done.own_ref, ...), custom_call_target="tpu_custom_call" | custom-call | flops 6442450944 | bytes 104857600 | tf_op jit(solution)/shard_map/backward/pallas_call | solution.py:452
  165.8 0.0 all-to-all-done.2
  165.8 0.0 copy-start.1
  165.8 1.9 collective-permute-start.3
  167.8 4.0 %collective-permute-done.3.other_ref = bf16[2,32,128,128]{3,2,1,0:T(8,128)(2,1)S(1)} collective-permute-done((bf16[2,32,128,128]{3,2,1,0:T(8,128)(2,1)}, bf16[2,32,128,128]{3,2,1,0:T(8,128)(2,1)S(1)}, u32[]{:S(2)}, u32[]{:S(2)}) %collective-permute-start.3) | collective-permute-done | bytes 2097184 | tf_op jit(solution)/shard_map/ppermute | solution.py:526
  171.7 0.0 copy-start.2
  171.8 1.4 copy-done.2
  173.1 5.2 %finish.1 = bf16[32,384,128]{2,1,0:T(8,128)(2,1)} custom-call(f32[2,32,128,128]{3,2,1,0:T(8,128)} %get-tuple-element.31.own_ref, bf16[2,32,128,128]{3,2,1,0:T(8,128)(2,1)} %copy-done.2, bf16[32,128,128]{2,1,0:T(8,128)(2,1)} %get-tuple-element.34.dq_ref, f32[1,128]{1,0:T(1,128)} %get-tuple-element.47.scaled_gain_ref), custom_call_target="tpu_custom_call" | custom-call | bytes 10485760 | tf_op jit(solution)/shard_map/finish/pallas_call | solution.py:499
  178.3 0.0 copy-done.1
  178.3 8.6 %all-to-all-start.3 = ((bf16[32,384,128]{2,1,0:T(8,128)(2,1)}), bf16[32,384,128]{2,1,0:T(8,128)(2,1)S(1)}, u32[]{:S(2)}, u32[]{:S(2)}) async-start(bf16[32,384,128]{2,1,0:T(8,128)(2,1)} %finish.1), calls=%async_computation.3 | async-start | bytes 6291456 | tf_op jit(solution)/shard_map/all_to_all | solution.py:532
  186.9 0.0 copy-done.4
  187.0 0.7 collective-permute-start.5
  187.7 0.8 collective-permute-done.5
  188.5 1.2 collective-permute-start.6
  189.7 1.2 collective-permute-done.6
  191.0 2.7 collective-permute-start.7
  193.7 1.2 collective-permute-done.7
  195.0 6.0 %collective-permute-start.8 = (f32[1,128]{1,0:T(1,128)S(1)}, f32[1,128]{1,0:T(1,128)S(1)}, u32[]{:S(2)}, u32[]{:S(2)}) collective-permute-start(f32[1,128]{1,0:T(1,128)S(1)} %slice.7), channel_id=1, source_target_pairs={{0,16},{1,17},{2,18},{3,19},{4,20},{5,21},{6,22},{7,23},{8,24},{9,... | collective-permute-start | bytes 1544 | tf_op jit(solution)/shard_map/ppermute | solution.py:529
  201.0 56.8 %collective-permute-done.8 = f32[1,128]{1,0:T(1,128)S(1)} collective-permute-done((f32[1,128]{1,0:T(1,128)S(1)}, f32[1,128]{1,0:T(1,128)S(1)}, u32[]{:S(2)}, u32[]{:S(2)}) %collective-permute-start.8) | collective-permute-done | bytes 544 | tf_op jit(solution)/shard_map/ppermute | solution.py:529
  257.8 2.5 collective-permute-start.9
  260.3 0.9 collective-permute-done.9
  261.2 2.6 collective-permute-start.10
  263.8 1.9 dynamic-slice_bitcast_fusion.1
  265.7 2.1 collective-permute-start.4
  267.8 0.0 collective-permute-done.10
  267.8 2.5 collective-permute-start.11
  270.3 1.0 collective-permute-done.11
  271.3 1.6 collective-permute-start.12
  272.9 0.0 collective-permute-done.4.came_ref
  272.9 2.1 unpack.2
  275.0 0.0 collective-permute-done.12
  275.0 0.6 maximum_bitcast_fusion
  275.6 0.0 all-to-all-done.3
  275.6 0.1 dynamic-slice_bitcast_fusion
  275.7 2.4 collective-permute-start.13
  278.1 3.2 %collective-permute-done.13.came_ref = bf16[16,384,128]{2,1,0:T(8,128)(2,1)} collective-permute-done((bf16[16,384,128]{2,1,0:T(8,128)(2,1)S(1)}, bf16[16,384,128]{2,1,0:T(8,128)(2,1)}, u32[]{:S(2)}, u32[]{:S(2)}) %collective-permute-start.13) | collective-permute-done | bytes 1572896 | tf_op jit(solution)/shard_map/ppermute | solution.py:526
  281.3 0.0 copy-done
  281.3 3.5 %unpack.3 = (bf16[256,2048]{1,0:T(8,128)(2,1)}, bf16[256,2048]{1,0:T(8,128)(2,1)}, bf16[256,2048]{1,0:T(8,128)(2,1)}) custom-call(s32[1]{0:T(128)} %bitcast.parity_ref.core_ref, bf16[2,16,384,128]{3,2,1,0:T(8,128)(2,1)} %bitcast.32, bf16[16,384,128]{2,1,0:T(8,128)(2,1)} %collective-permute-done.13.came_ref), custom_call_target="tpu_custom_call" | custom-call | bytes 6291456 | tf_op jit(solution)/shard_map/unpack/pallas_call | solution.py:100
  (15 shorter events, 0.1 us)
Async XLA Ops:
  4.6 6.5 %collective-permute-start = (bf16[16,392,128]{2,1,0:T(8,128)(2,1)}, bf16[16,392,128]{2,1,0:T(8,128)(2,1)S(1)}, u32[]{:S(2)}, u32[]{:S(2)}) collective-permute-start(bf16[16,392,128]{2,1,0:T(8,128)(2,1)} %pack_sent.2), channel_id=1, source_target_pairs={{0,32},{32,0},{64,96},{96,64},{128,160},{160,128},{192,224},{224,1... | collective-permute-start | bytes 4816904 | tf_op jit(solution)/shard_map/ppermute | solution.py:526
  12.4 81.9 %all-to-all-start = ((bf16[32,392,128]{2,1,0:T(8,128)(2,1)}), bf16[32,392,128]{2,1,0:T(8,128)(2,1)}, u32[]{:S(2)}, u32[]{:S(2)}) async-start(bf16[32,392,128]{2,1,0:T(8,128)(2,1)} %bitcast.49), calls=%async_computation | async-start | bytes 6422528 | tf_op jit(solution)/shard_map/all_to_all | solution.py:532
  23.9 2.5 collective-permute-start.1
  94.3 11.1 %collective-permute-start.2 = (bf16[32,392,128]{2,1,0:T(8,128)(2,1)}, bf16[32,392,128]{2,1,0:T(8,128)(2,1)}, u32[]{:S(2)}, u32[]{:S(2)}) collective-permute-start(bf16[32,392,128]{2,1,0:T(8,128)(2,1)} %all-to-all-done.own_ref), channel_id=1, source_target_pairs={{0,32},{32,0},{64,96},{96,64},{128,160},{160,128},{192,224},{224,1... | collective-permute-start | bytes 9633800 | tf_op jit(solution)/shard_map/ppermute | solution.py:526
  96.5 33.2 %all-to-all-start.1 = ((bf16[32,128,128]{2,1,0:T(8,128)(2,1)}), bf16[32,128,128]{2,1,0:T(8,128)(2,1)S(1)}, u32[]{:S(2)}, u32[]{:S(2)}) async-start(bf16[32,128,128]{2,1,0:T(8,128)(2,1)} %bitcast.52), calls=%async_computation.1 | async-start | bytes 2097152 | tf_op jit(solution)/shard_map/all_to_all | solution.py:532
  129.8 9.0 %copy-start.3 = (bf16[32,128,128]{2,1,0:T(8,128)(2,1)}, bf16[32,128,128]{2,1,0:T(8,128)(2,1)S(1)}, u32[]{:S(2)}) copy-start(bf16[32,128,128]{2,1,0:T(8,128)(2,1)S(1)} %all-to-all-done.1.grad_ref) | copy-start | bytes 3145732
  129.8 36.0 %all-to-all-start.2 = ((bf16[32,128,128]{2,1,0:T(8,128)(2,1)}), bf16[32,128,128]{2,1,0:T(8,128)(2,1)S(1)}, u32[]{:S(2)}, u32[]{:S(2)}) async-start(bf16[32,128,128]{2,1,0:T(8,128)(2,1)} %get-tuple-element.28.att_ref), calls=%async_computation.2 | async-start | bytes 2097152 | tf_op jit(solution)/shard_map/all_to_all | solution.py:532
  165.8 12.5 %copy-start.1 = (bf16[32,128,128]{2,1,0:T(8,128)(2,1)}, bf16[32,128,128]{2,1,0:T(8,128)(2,1)S(1)}, u32[]{:S(2)}) copy-start(bf16[32,128,128]{2,1,0:T(8,128)(2,1)S(1)} %all-to-all-done.2) | copy-start | bytes 3145732
  165.8 5.9 %collective-permute-start.3 = (bf16[2,32,128,128]{3,2,1,0:T(8,128)(2,1)}, bf16[2,32,128,128]{3,2,1,0:T(8,128)(2,1)S(1)}, u32[]{:S(2)}, u32[]{:S(2)}) collective-permute-start(bf16[2,32,128,128]{3,2,1,0:T(8,128)(2,1)} %get-tuple-element.33), channel_id=1, source_target_pairs={{0,32},{32,0},{64,96},{96,64},{128,160},{160,128},{192,224},{224,1... | collective-permute-start | bytes 6291464 | tf_op jit(solution)/shard_map/ppermute | solution.py:526
  171.7 1.4 copy-start.2
  178.3 8.6 %copy-start.4 = (f32[8,128]{1,0:T(8,128)S(1)}, f32[8,128]{1,0:T(8,128)}, u32[]{:S(2)}) copy-start(f32[8,128]{1,0:T(8,128)} %get-tuple-element.38) | copy-start | bytes 12292
  178.3 97.3 %all-to-all-start.3 = ((bf16[32,384,128]{2,1,0:T(8,128)(2,1)}), bf16[32,384,128]{2,1,0:T(8,128)(2,1)S(1)}, u32[]{:S(2)}, u32[]{:S(2)}) async-start(bf16[32,384,128]{2,1,0:T(8,128)(2,1)} %finish.1), calls=%async_computation.3 | async-start | bytes 6291456 | tf_op jit(solution)/shard_map/all_to_all | solution.py:532
  187.0 1.6 collective-permute-start.5
  188.5 2.5 collective-permute-start.6
  191.0 4.0 %collective-permute-start.7 = (f32[8,128]{1,0:T(8,128)S(1)}, f32[8,128]{1,0:T(8,128)S(1)}, u32[]{:S(2)}, u32[]{:S(2)}) collective-permute-start(f32[8,128]{1,0:T(8,128)S(1)} %add.58), channel_id=1, source_target_pairs={{0,128},{32,160},{64,192},{96,224},{128,0},{160,32},{192,64},{224,... | collective-permute-start | bytes 12296 | tf_op jit(solution)/shard_map/ppermute | solution.py:526
  195.0 62.8 %collective-permute-start.8 = (f32[1,128]{1,0:T(1,128)S(1)}, f32[1,128]{1,0:T(1,128)S(1)}, u32[]{:S(2)}, u32[]{:S(2)}) collective-permute-start(f32[1,128]{1,0:T(1,128)S(1)} %slice.7), channel_id=1, source_target_pairs={{0,16},{1,17},{2,18},{3,19},{4,20},{5,21},{6,22},{7,23},{8,24},{9,... | collective-permute-start | bytes 1544 | tf_op jit(solution)/shard_map/ppermute | solution.py:529
  257.8 3.4 %collective-permute-start.9 = (f32[1,128]{1,0:T(1,128)S(1)}, f32[1,128]{1,0:T(1,128)S(1)}, u32[]{:S(2)}, u32[]{:S(2)}) collective-permute-start(f32[1,128]{1,0:T(1,128)S(1)} %slice_add_fusion), channel_id=1, source_target_pairs={{0,1},{1,0},{2,3},{3,2},{4,5},{5,4},{6,7},{7,6},{8,9},{9,8},{10,11... | collective-permute-start | bytes 1544 | tf_op jit(solution)/shard_map/ppermute | solution.py:529
  261.2 6.6 %collective-permute-start.10 = (f32[2,128]{1,0:T(2,128)S(1)}, f32[2,128]{1,0:T(2,128)S(1)}, u32[]{:S(2)}, u32[]{:S(2)}) collective-permute-start(f32[2,128]{1,0:T(2,128)S(1)} %pad_maximum_fusion.2), channel_id=1, source_target_pairs={{0,2},{1,3},{2,0},{3,1},{4,6},{5,7},{6,4},{7,5},{8,10},{9,11},{10,... | collective-permute-start | bytes 3080 | tf_op jit(solution)/shard_map/ppermute | solution.py:529
  265.7 7.2 %collective-permute-start.4 = (bf16[16,128,128]{2,1,0:T(8,128)(2,1)}, bf16[16,128,128]{2,1,0:T(8,128)(2,1)}, u32[]{:S(2)}, u32[]{:S(2)}) collective-permute-start(bf16[16,128,128]{2,1,0:T(8,128)(2,1)} %dynamic-slice_bitcast_fusion.1), channel_id=1, source_target_pairs={{0,32},{32,0},{64,96},{96,64},{128,160},{160,128},{192,224},{224,1... | collective-permute-start | bytes 1572872 | tf_op jit(solution)/shard_map/ppermute | solution.py:526
  267.8 3.4 %collective-permute-start.11 = (f32[4,128]{1,0:T(4,128)S(1)}, f32[4,128]{1,0:T(4,128)S(1)}, u32[]{:S(2)}, u32[]{:S(2)}) collective-permute-start(f32[4,128]{1,0:T(4,128)S(1)} %pad_maximum_fusion.1), channel_id=1, source_target_pairs={{0,4},{1,5},{2,6},{3,7},{4,0},{5,1},{6,2},{7,3},{8,12},{9,13},{10,... | collective-permute-start | bytes 6152 | tf_op jit(solution)/shard_map/ppermute | solution.py:529
  271.3 3.7 %collective-permute-start.12 = (f32[8,128]{1,0:T(8,128)S(1)}, f32[8,128]{1,0:T(8,128)S(1)}, u32[]{:S(2)}, u32[]{:S(2)}) collective-permute-start(f32[8,128]{1,0:T(8,128)S(1)} %pad_maximum_fusion), channel_id=1, source_target_pairs={{0,8},{1,9},{2,10},{3,11},{4,12},{5,13},{6,14},{7,15},{8,0},{9,1},... | collective-permute-start | bytes 12296 | tf_op jit(solution)/shard_map/ppermute | solution.py:529
  275.6 5.6 %copy-start = (bf16[32,384,128]{2,1,0:T(8,128)(2,1)}, bf16[32,384,128]{2,1,0:T(8,128)(2,1)S(1)}, u32[]{:S(2)}) copy-start(bf16[32,384,128]{2,1,0:T(8,128)(2,1)S(1)} %all-to-all-done.3) | copy-start | bytes 9437188
  275.7 5.5 %collective-permute-start.13 = (bf16[16,384,128]{2,1,0:T(8,128)(2,1)S(1)}, bf16[16,384,128]{2,1,0:T(8,128)(2,1)}, u32[]{:S(2)}, u32[]{:S(2)}) collective-permute-start(bf16[16,384,128]{2,1,0:T(8,128)(2,1)S(1)} %dynamic-slice_bitcast_fusion), channel_id=1, source_target_pairs={{0,32},{32,0},{64,96},{96,64},{128,160},{160,128},{192,224},{224,1... | collective-permute-start | bytes 4718600 | tf_op jit(solution)/shard_map/ppermute | solution.py:526

commit v6 on v4

--- a/solution.py
+++ b/solution.py
@@ -334,6 +334,7 @@
     acc_k,
     acc_v,
     raw_scr,
+    first_scr,
     in_sem,
     out_sem,
 ):
@@ -348,12 +349,15 @@
         pltpu.make_async_copy(src, dst, in_sem.at[at])
         for at, (src, dst) in enumerate(
             [
-                (grad_ref, g_scr),
-                (att_ref, a_scr),
+                (own_ref.at[0, 2 * PAIR : 2 * PAIR + BLOCK], first_scr.at[0]),
+                (grad_ref.at[0, :BLOCK], first_scr.at[1]),
+                (att_ref.at[0, :BLOCK], first_scr.at[2]),
                 (dense_ref, dense_scr),
                 (rows(own_ref, 1), v_scr.at[core]),
                 (rows(other_ref, 1), v_scr.at[1 - core]),
                 (key_ref, k_scr),
+                (grad_ref, g_scr),
+                (att_ref, a_scr),
                 (rows(own_ref, 2), q_scr),
                 (weight_ref, weight_scr),
                 (rows(own_ref, 0), raw_scr.at[core]),
@@ -371,9 +375,9 @@
             grad.astype(jnp.float32) * attended.astype(jnp.float32), axis=1, keepdims=True
         )
 
-    query = q_scr[0, :BLOCK]
-    grad = g_scr[0, :BLOCK]
-    delta = row_delta(grad, a_scr[0, :BLOCK])
+    query = first_scr[0]
+    grad = first_scr[1]
+    delta = row_delta(grad, first_scr[2])
     operand = diagonal(query, grad)
 
     def dense_back(t, dquery):
@@ -389,7 +393,8 @@
     zero = jnp.zeros((BLOCK, HD), jnp.float32)
     dquery = lax.fori_loop(0, 2 * steps, dense_back, zero, unroll=4)
     dq_ref[0, :BLOCK] = (dquery * SCALE).astype(jnp.bfloat16)
-    copies[7].wait()
+    for copy in copies[7:11]:
+        copy.wait()
 
     def sparse_block(n):
         block = 2 * n + core
@@ -415,7 +420,7 @@
         return carry
 
     lax.fori_loop(0, (2 * places - 1) // unroll, sparse_step, 0)
-    for copy in copies[8:]:
+    for copy in copies[11:]:
         copy.wait()
 
     copies = [
@@ -470,7 +475,8 @@
             pltpu.VMEM(both, jnp.float32),
             pltpu.VMEM(both, jnp.float32),
             pltpu.VMEM(both, jnp.bfloat16),
-            pltpu.SemaphoreType.DMA((10,)),
+            pltpu.VMEM((3, BLOCK, HD), jnp.bfloat16),
+            pltpu.SemaphoreType.DMA((13,)),
             pltpu.SemaphoreType.DMA((2,)),
         ],
         compiler_params=pltpu.CompilerParams(vmem_limit_bytes=VMEM_LIMIT),

time: 269 us -> 269 us (level)
  transfers between devices with their start and end apart: 15 -> 15, of which waited for: 10 -> 10; matrix products, arithmetic and copies ran while one was open for 3% -> 3% of each run, Pallas kernels for 25% -> 24%
where the time goes in v6:
time: 269 us; the launch traced here: 268 us
  waiting for transfers between devices  128 us (48%)
  Pallas kernels  70.8 us (26%)
  starting transfers between devices  55.3 us (21%)
  local copies, waits for them, and re-layouts  9.11 us (3%)
  other arithmetic  3.44 us (1%)
    all_to_all x5, waiting for transfers between devices, over_seq(): return lax.all_to_all(x, 'seq', split_axis=0, concat_axis=0, tiled=True)  121 us
    all_to_all x5, starting transfers between devices, over_seq(): return lax.all_to_all(x, 'seq', split_axis=0, concat_axis=0, tiled=True)  38.8 us
    pallas_call x1, Pallas kernels, backward(): pl.pallas_call(functools.partial(backward_kernel, places, unroll), in_spe...  26.2 us
    pallas_call x1, Pallas kernels, forward(): pl.pallas_call(functools.partial(forward_kernel, places, unroll), in_spec...  24 us
    ppermute x10, starting transfers between devices, swap(): return lax.ppermute(x, 'dp', [(i, i ^ bit) for i in range(dp)])  16.5 us
    pallas_call x4, Pallas kernels, pack(): pl.pallas_call(functools.partial(pack_kernel, group, count, spare is not...  8.8 us
    ppermute x10, waiting for transfers between devices, swap(): return lax.ppermute(x, 'dp', [(i, i ^ bit) for i in range(dp)])  7.42 us
    pallas_call x3, Pallas kernels, unpack(): pl.pallas_call(functools.partial(unpack_kernel, group), grid_spec=pltpu.P...  7.07 us
  transfers between devices with their start and end apart: 15, of which 10 were waited for; matrix products, arithmetic and copies ran while one was open for 3% of the time, Pallas kernels for 24%

profile of v6, /device:TPU:1, one launch (start us, length us, event | category | flops | bytes accessed | tf_op | source)
XLA Modules:
  0.0 267.6 jit_solution(15134526268241961941)
XLA Ops:
  0.6 0.7 convert_element_type.32
  1.3 0.1 copy.15
  1.5 0.6 pad.4.refs_6_
  2.1 2.5 pack_sent.2
  4.6 3.2 %collective-permute-start = (bf16[16,392,128]{2,1,0:T(8,128)(2,1)}, bf16[16,392,128]{2,1,0:T(8,128)(2,1)S(1)}, u32[]{:S(2)}, u32[]{:S(2)}) collective-permute-start(bf16[16,392,128]{2,1,0:T(8,128)(2,1)} %pack_sent.2), channel_id=1, source_target_pairs={{0,32},{32,0},{64,96},{96,64},{128,160},{160,128},{192,224},{224,1... | collective-permute-start | bytes 4816904 | tf_op jit(solution)/shard_map/ppermute | solution.py:536
  7.9 2.5 pack_own.2
  10.4 0.8 collective-permute-done
  11.2 1.3 bitcast_dynamic-update-slice_fusion
  12.4 9.5 %all-to-all-start = ((bf16[32,392,128]{2,1,0:T(8,128)(2,1)}), bf16[32,392,128]{2,1,0:T(8,128)(2,1)S(1)}, u32[]{:S(2)}, u32[]{:S(2)}) async-start(bf16[32,392,128]{2,1,0:T(8,128)(2,1)} %bitcast.52), calls=%async_computation | async-start | bytes 6422528 | tf_op jit(solution)/shard_map/all_to_all | solution.py:539
  21.9 1.9 pack_sent.3
  23.8 0.6 collective-permute-start.1
  24.4 1.8 pack_own.3
  26.3 0.0 collective-permute-done.1
  26.3 1.9 bitcast_dynamic-update-slice_fusion.1
  28.2 66.0 %all-to-all-done.own_ref = bf16[32,392,128]{2,1,0:T(8,128)(2,1)S(1)} async-done(((bf16[32,392,128]{2,1,0:T(8,128)(2,1)}), bf16[32,392,128]{2,1,0:T(8,128)(2,1)S(1)}, u32[]{:S(2)}, u32[]{:S(2)}) %all-to-all-start) | async-done | bytes 3211296 | tf_op jit(solution)/shard_map/all_to_all | solution.py:539
  94.2 0.0 copy-start.3
  94.2 2.3 collective-permute-start.2
  96.5 6.1 %all-to-all-start.2 = ((bf16[32,128,128]{2,1,0:T(8,128)(2,1)}), bf16[32,128,128]{2,1,0:T(8,128)(2,1)}, u32[]{:S(2)}, u32[]{:S(2)}) async-start(bf16[32,128,128]{2,1,0:T(8,128)(2,1)} %bitcast.57), calls=%async_computation.2 | async-start | bytes 2097152 | tf_op jit(solution)/shard_map/all_to_all | solution.py:539
  102.6 1.4 multiply_bitcast_fusion
  103.9 0.1 convert_reduce_fusion.1
  104.0 0.7 reshape.65.table_ref
  104.7 0.0 collective-permute-done.2.other_ref
  104.7 0.0 copy-done.3
  104.7 24.0 %forward.1 = (bf16[32,128,128]{2,1,0:T(8,128)(2,1)}, bf16[64,64,512]{2,1,0:T(8,128)(2,1)}, bf16[16,64,512]{2,1,0:T(8,128)(2,1)}, bf16[2,32,128,128]{3,2,1,0:T(8,128)(2,1)}) custom-call(s32[1]{0:T(128)} %bitcast.parity_ref.core_ref, s32[192]{0:T(256)} %reshape.65.table_ref, f32[1,128]{1,0:T(1,128)} %get-tuple-element.44.gain_ref, ...), custom_call_target="tpu_custom_call" | custom-call | flops 3221225472 | bytes 62914560 | tf_op jit(solution)/shard_map/forward/pallas_call | solution.py:269
  128.7 1.1 all-to-all-done.2.grad_ref
  129.8 8.1 %all-to-all-start.1 = ((bf16[32,128,128]{2,1,0:T(8,128)(2,1)}), bf16[32,128,128]{2,1,0:T(8,128)(2,1)S(1)}, u32[]{:S(2)}, u32[]{:S(2)}) async-start(bf16[32,128,128]{2,1,0:T(8,128)(2,1)} %get-tuple-element.25.att_ref), calls=%async_computation.1 | async-start | bytes 2097152 | tf_op jit(solution)/shard_map/all_to_all | solution.py:539
  137.9 26.2 %backward.1 = (bf16[32,128,128]{2,1,0:T(8,128)(2,1)}, f32[2,32,128,128]{3,2,1,0:T(8,128)}, bf16[2,32,128,128]{3,2,1,0:T(8,128)(2,1)}, f32[8,128]{1,0:T(8,128)}) custom-call(s32[1]{0:T(128)} %bitcast.parity_ref.core_ref, s32[192]{0:T(256)} %reshape.65.table_ref, bf16[32,392,128]{2,1,0:T(8,128)(2,1)} %copy-done.3, ...), custom_call_target="tpu_custom_call" | custom-call | flops 6442450944 | bytes 104857600 | tf_op jit(solution)/shard_map/backward/pallas_call | solution.py:457
  164.0 0.9 collective-permute-start.3
  165.0 0.0 all-to-all-done.1
  165.0 0.0 copy-start.1
  165.0 9.5 %all-to-all-start.3 = ((bf16[32,128,128]{2,1,0:T(8,128)(2,1)}), bf16[32,128,128]{2,1,0:T(8,128)(2,1)S(1)}, u32[]{:S(2)}, u32[]{:S(2)}) async-start(bf16[32,128,128]{2,1,0:T(8,128)(2,1)} %get-tuple-element.31), calls=%async_computation.3 | async-start | bytes 2097152 | tf_op jit(solution)/shard_map/all_to_all | solution.py:539
  174.6 0.4 collective-permute-start.4
  175.0 1.1 collective-permute-done.4
  176.0 0.7 add.35
  176.7 1.2 collective-permute-start.5
  177.9 1.5 collective-permute-done.5
  179.5 2.7 %collective-permute-start.6 = (f32[8,128]{1,0:T(8,128)S(1)}, f32[8,128]{1,0:T(8,128)S(1)}, u32[]{:S(2)}, u32[]{:S(2)}) collective-permute-start(f32[8,128]{1,0:T(8,128)S(1)} %add.36), channel_id=1, source_target_pairs={{0,128},{32,160},{64,192},{96,224},{128,0},{160,32},{192,64},{224,... | collective-permute-start | bytes 12296 | tf_op jit(solution)/shard_map/ppermute | solution.py:536
  182.2 1.5 collective-permute-done.6
  183.7 0.5 slice.10.gain_grad_ref
  184.2 0.0 collective-permute-done.3.other_ref
  184.2 4.7 %finish.1 = bf16[32,264,128]{2,1,0:T(8,128)(2,1)} custom-call(f32[2,32,128,128]{3,2,1,0:T(8,128)} %get-tuple-element.32.own_ref, bf16[2,32,128,128]{3,2,1,0:T(8,128)(2,1)} %collective-permute-done.3.other_ref, f32[1,128]{1,0:T(1,128)} %get-tuple-element.43.scaled_gain_ref, f32[1,128]{1,0:T(1,128)} %slice.10.gain_grad_ref), custom_call_target="tpu_custom_call" | custom-call | tf_op jit(solution)/shard_map/finish/pallas_call | solution.py:517
  189.0 12.9 %all-to-all-done.3 = bf16[32,128,128]{2,1,0:T(8,128)(2,1)S(1)} async-done(((bf16[32,128,128]{2,1,0:T(8,128)(2,1)}), bf16[32,128,128]{2,1,0:T(8,128)(2,1)S(1)}, u32[]{:S(2)}, u32[]{:S(2)}) %all-to-all-start.3) | async-done | bytes 1048608 | tf_op jit(solution)/shard_map/all_to_all | solution.py:539
  201.9 0.0 copy-start.2
  201.9 1.0 copy-done.2
  202.8 5.7 %all-to-all-start.4 = ((bf16[32,264,128]{2,1,0:T(8,128)(2,1)}), bf16[32,264,128]{2,1,0:T(8,128)(2,1)S(1)}, u32[]{:S(2)}, u32[]{:S(2)}) async-start(bf16[32,264,128]{2,1,0:T(8,128)(2,1)} %finish.1), calls=%async_computation.4 | async-start | bytes 4325376 | tf_op jit(solution)/shard_map/all_to_all | solution.py:539
  208.5 0.0 copy-done.1
  208.6 1.7 collective-permute-start.7
  210.3 1.1 dynamic-slice_bitcast_fusion.1
  211.4 0.1 collective-permute-start.8
  211.5 0.5 collective-permute-done.7.came_ref
  211.9 2.1 unpack.3
  214.1 0.0 collective-permute-done.8.came_ref
  214.1 0.0 copy-start.4
  214.1 0.8 copy-done.4
  214.9 2.1 unpack.4
  217.0 40.8 %all-to-all-done.4 = bf16[32,264,128]{2,1,0:T(8,128)(2,1)S(1)} async-done(((bf16[32,264,128]{2,1,0:T(8,128)(2,1)}), bf16[32,264,128]{2,1,0:T(8,128)(2,1)S(1)}, u32[]{:S(2)}, u32[]{:S(2)}) %all-to-all-start.4) | async-done | bytes 2162720 | tf_op jit(solution)/shard_map/all_to_all | solution.py:539
  257.8 0.0 copy-start
  257.8 1.1 dynamic-slice_bitcast_fusion
  258.9 3.3 %collective-permute-start.9 = (bf16[16,264,128]{2,1,0:T(8,128)(2,1)}, bf16[16,264,128]{2,1,0:T(8,128)(2,1)}, u32[]{:S(2)}, u32[]{:S(2)}) collective-permute-start(bf16[16,264,128]{2,1,0:T(8,128)(2,1)} %dynamic-slice_bitcast_fusion), channel_id=1, source_target_pairs={{0,32},{32,0},{64,96},{96,64},{128,160},{160,128},{192,224},{224,1... | collective-permute-start | bytes 3244040 | tf_op jit(solution)/shard_map/ppermute | solution.py:536
  262.2 0.6 reduce_sum.18
  262.8 2.0 collective-permute-done.9.came_ref
  264.8 0.0 copy-done
  264.8 2.8 %unpack.5 = (bf16[256,2048]{1,0:T(8,128)(2,1)}, bf16[256,2048]{1,0:T(8,128)(2,1)}) custom-call(s32[1]{0:T(128)} %bitcast.parity_ref.core_ref, bf16[2,16,264,128]{3,2,1,0:T(8,128)(2,1)} %bitcast.51, bf16[16,264,128]{2,1,0:T(8,128)(2,1)} %collective-permute-done.9.came_ref), custom_call_target="tpu_custom_call" | custom-call | bytes 4194304 | tf_op jit(solution)/shard_map/unpack/pallas_call | solution.py:100
  (5 shorter events, 0.1 us)
Async XLA Ops:
  4.6 6.5 %collective-permute-start = (bf16[16,392,128]{2,1,0:T(8,128)(2,1)}, bf16[16,392,128]{2,1,0:T(8,128)(2,1)S(1)}, u32[]{:S(2)}, u32[]{:S(2)}) collective-permute-start(bf16[16,392,128]{2,1,0:T(8,128)(2,1)} %pack_sent.2), channel_id=1, source_target_pairs={{0,32},{32,0},{64,96},{96,64},{128,160},{160,128},{192,224},{224,1... | collective-permute-start | bytes 4816904 | tf_op jit(solution)/shard_map/ppermute | solution.py:536
  12.4 81.8 %all-to-all-start = ((bf16[32,392,128]{2,1,0:T(8,128)(2,1)}), bf16[32,392,128]{2,1,0:T(8,128)(2,1)S(1)}, u32[]{:S(2)}, u32[]{:S(2)}) async-start(bf16[32,392,128]{2,1,0:T(8,128)(2,1)} %bitcast.52), calls=%async_computation | async-start | bytes 6422528 | tf_op jit(solution)/shard_map/all_to_all | solution.py:539
  23.8 2.5 collective-permute-start.1
  94.2 10.4 %copy-start.3 = (bf16[32,392,128]{2,1,0:T(8,128)(2,1)}, bf16[32,392,128]{2,1,0:T(8,128)(2,1)S(1)}, u32[]{:S(2)}) copy-start(bf16[32,392,128]{2,1,0:T(8,128)(2,1)S(1)} %all-to-all-done.own_ref) | copy-start | bytes 9633796
  94.2 10.4 %collective-permute-start.2 = (bf16[32,392,128]{2,1,0:T(8,128)(2,1)S(1)}, bf16[32,392,128]{2,1,0:T(8,128)(2,1)}, u32[]{:S(2)}, u32[]{:S(2)}) collective-permute-start(bf16[32,392,128]{2,1,0:T(8,128)(2,1)S(1)} %all-to-all-done.own_ref), channel_id=1, source_target_pairs={{0,32},{32,0},{64,96},{96,64},{128,160},{160,128},{192,224},{224,1... | collective-permute-start | bytes 9633800 | tf_op jit(solution)/shard_map/ppermute | solution.py:536
  96.5 33.3 %all-to-all-start.2 = ((bf16[32,128,128]{2,1,0:T(8,128)(2,1)}), bf16[32,128,128]{2,1,0:T(8,128)(2,1)}, u32[]{:S(2)}, u32[]{:S(2)}) async-start(bf16[32,128,128]{2,1,0:T(8,128)(2,1)} %bitcast.57), calls=%async_computation.2 | async-start | bytes 2097152 | tf_op jit(solution)/shard_map/all_to_all | solution.py:539
  129.8 35.2 %all-to-all-start.1 = ((bf16[32,128,128]{2,1,0:T(8,128)(2,1)}), bf16[32,128,128]{2,1,0:T(8,128)(2,1)S(1)}, u32[]{:S(2)}, u32[]{:S(2)}) async-start(bf16[32,128,128]{2,1,0:T(8,128)(2,1)} %get-tuple-element.25.att_ref), calls=%async_computation.1 | async-start | bytes 2097152 | tf_op jit(solution)/shard_map/all_to_all | solution.py:539
  164.0 20.2 %collective-permute-start.3 = (bf16[2,32,128,128]{3,2,1,0:T(8,128)(2,1)}, bf16[2,32,128,128]{3,2,1,0:T(8,128)(2,1)}, u32[]{:S(2)}, u32[]{:S(2)}) collective-permute-start(bf16[2,32,128,128]{3,2,1,0:T(8,128)(2,1)} %get-tuple-element.33), channel_id=1, source_target_pairs={{0,32},{32,0},{64,96},{96,64},{128,160},{160,128},{192,224},{224,1... | collective-permute-start | bytes 6291464 | tf_op jit(solution)/shard_map/ppermute | solution.py:536
  165.0 43.5 %copy-start.1 = (bf16[32,128,128]{2,1,0:T(8,128)(2,1)}, bf16[32,128,128]{2,1,0:T(8,128)(2,1)S(1)}, u32[]{:S(2)}) copy-start(bf16[32,128,128]{2,1,0:T(8,128)(2,1)S(1)} %all-to-all-done.1) | copy-start | bytes 3145732
  165.0 36.9 %all-to-all-start.3 = ((bf16[32,128,128]{2,1,0:T(8,128)(2,1)}), bf16[32,128,128]{2,1,0:T(8,128)(2,1)S(1)}, u32[]{:S(2)}, u32[]{:S(2)}) async-start(bf16[32,128,128]{2,1,0:T(8,128)(2,1)} %get-tuple-element.31), calls=%async_computation.3 | async-start | bytes 2097152 | tf_op jit(solution)/shard_map/all_to_all | solution.py:539
  174.6 1.5 collective-permute-start.4
  176.7 2.8 %collective-permute-start.5 = (f32[8,128]{1,0:T(8,128)S(1)}, f32[8,128]{1,0:T(8,128)S(1)}, u32[]{:S(2)}, u32[]{:S(2)}) collective-permute-start(f32[8,128]{1,0:T(8,128)S(1)} %add.35), channel_id=1, source_target_pairs={{0,64},{32,96},{64,0},{96,32},{128,192},{160,224},{192,128},{224,1... | collective-permute-start | bytes 12296 | tf_op jit(solution)/shard_map/ppermute | solution.py:536
  179.5 4.3 %collective-permute-start.6 = (f32[8,128]{1,0:T(8,128)S(1)}, f32[8,128]{1,0:T(8,128)S(1)}, u32[]{:S(2)}, u32[]{:S(2)}) collective-permute-start(f32[8,128]{1,0:T(8,128)S(1)} %add.36), channel_id=1, source_target_pairs={{0,128},{32,160},{64,192},{96,224},{128,0},{160,32},{192,64},{224,... | collective-permute-start | bytes 12296 | tf_op jit(solution)/shard_map/ppermute | solution.py:536
  201.9 1.0 copy-start.2
  202.8 54.9 %all-to-all-start.4 = ((bf16[32,264,128]{2,1,0:T(8,128)(2,1)}), bf16[32,264,128]{2,1,0:T(8,128)(2,1)S(1)}, u32[]{:S(2)}, u32[]{:S(2)}) async-start(bf16[32,264,128]{2,1,0:T(8,128)(2,1)} %finish.1), calls=%async_computation.4 | async-start | bytes 4325376 | tf_op jit(solution)/shard_map/all_to_all | solution.py:539
  208.6 3.4 %collective-permute-start.7 = (bf16[16,128,128]{2,1,0:T(8,128)(2,1)S(1)}, bf16[16,128,128]{2,1,0:T(8,128)(2,1)}, u32[]{:S(2)}, u32[]{:S(2)}) collective-permute-start(bf16[16,128,128]{2,1,0:T(8,128)(2,1)S(1)} %dynamic-slice_bitcast_fusion.2), channel_id=1, source_target_pairs={{0,32},{32,0},{64,96},{96,64},{128,160},{160,128},{192,224},{224,1... | collective-permute-start | bytes 1572872 | tf_op jit(solution)/shard_map/ppermute | solution.py:536
  211.4 2.7 %collective-permute-start.8 = (bf16[16,128,128]{2,1,0:T(8,128)(2,1)S(1)}, bf16[16,128,128]{2,1,0:T(8,128)(2,1)S(1)}, u32[]{:S(2)}, u32[]{:S(2)}) collective-permute-start(bf16[16,128,128]{2,1,0:T(8,128)(2,1)S(1)} %dynamic-slice_bitcast_fusion.1), channel_id=1, source_target_pairs={{0,32},{32,0},{64,96},{96,64},{128,160},{160,128},{192,224},{224,1... | collective-permute-start | bytes 1572872 | tf_op jit(solution)/shard_map/ppermute | solution.py:536
  214.1 0.8 copy-start.4
  257.8 7.1 %copy-start = (bf16[32,264,128]{2,1,0:T(8,128)(2,1)}, bf16[32,264,128]{2,1,0:T(8,128)(2,1)S(1)}, u32[]{:S(2)}) copy-start(bf16[32,264,128]{2,1,0:T(8,128)(2,1)S(1)} %all-to-all-done.4) | copy-start | bytes 6488068
  258.9 5.9 %collective-permute-start.9 = (bf16[16,264,128]{2,1,0:T(8,128)(2,1)}, bf16[16,264,128]{2,1,0:T(8,128)(2,1)}, u32[]{:S(2)}, u32[]{:S(2)}) collective-permute-start(bf16[16,264,128]{2,1,0:T(8,128)(2,1)} %dynamic-slice_bitcast_fusion), channel_id=1, source_target_pairs={{0,32},{32,0},{64,96},{96,64},{128,160},{160,128},{192,224},{224,1... | collective-permute-start | bytes 3244040 | tf_op jit(solution)/shard_map/ppermute | solution.py:536
